TPU v7x, 32 devices: a whole 2x2x4 slice. The times are simulated.
32 devices in a mesh: mem: 4 (over x, core), lon: 8 (over z, y).
Axes of the slice: x: 2, y: 2, z: 4, core: 2. Of those that a mesh axis runs over, the one named last changes fastest.
Arguments:
- prior_fields: bfloat16 [80, 1536, 256], P('mem', 'lon'), may hold values from -6 to 6
- scaled_sensor_spread: bfloat16 [80, 1536, 256], P('mem', 'lon'), may hold values from -3 to 3
- measured_misfit: float32 [1536, 256], P('lon'), may hold values from -12 to 12
- inverse_error_variance: float32 [1536, 256], P('lon'), may hold values from 0.5 to 4
- active_sensor_number: int32 [1536], P('lon'), may hold values from 64 to 256, as said below
- adjacent_tiles: int32 [1536, 16], P('lon'), may hold values from 0 to 1535, as said below
Outputs:
- analysis: bfloat16 [80, 1536, 256], P('mem', 'lon')
Inputs may be any that keep to these rules, and one draw needn't show every extreme that they name: `adjacent_tiles`: row b holds 16 different block indices, all within 48 blocks of b around the closed sequence of 1536 blocks; among them b itself and the blocks exactly 48 before and after b. Slots at and beyond active_sensor_number[c] of block c are padding; some block is full in every draw.
All inputs are finite; a program needn't handle non-finite values.
Results may differ from a plain program's by a relative error of at most 0.0069.
Values may be sent and summed in bfloat16 or wider, within the bound.
No kernel may reach another device: no remote copies, remote signals or barrier semaphores. Data moves between devices by JAX's collectives and lax.ppermute only.
A program may use at most 128 MiB of HBM per device.

v0:
```python
import functools

import jax
import jax.numpy as jnp
from jax import lax
from jax.experimental import pallas as pl
from jax.experimental.pallas import tpu as pltpu
from jax.sharding import PartitionSpec as P

RADIUS = 48
SWEEPS = 5
LANES = 128
F32 = jnp.float32
BF16 = jnp.bfloat16
VMEM_BYTES = 56 * 1024 * 1024


def vmem():
    return pl.BlockSpec(memory_space=pltpu.VMEM)


def smem():
    return pl.BlockSpec(memory_space=pltpu.SMEM)


def params():
    return pltpu.CompilerParams(vmem_limit_bytes=VMEM_BYTES)


def gram_kernel(mem_ref, *refs, groups, share, blocks, width, unroll):
    parts = refs[:groups]
    scale_ref, weight_ref, own_ref, send_ref, rows_ref = refs[groups:]
    members = groups * share
    half = members // 2
    tiles = width // LANES
    mem = mem_ref[0]
    scale = scale_ref[...]
    for d in range(groups):
        base = (mem ^ d) * (share * blocks)

        def scale_member(k, carry, part=parts[d], base=base):
            value = (part[k].astype(F32) * scale).astype(BF16).astype(F32)
            start = pl.multiple_of(base + k * blocks, 8)
            for t in range(tiles):
                rows_ref[t, pl.ds(start, blocks), :] = value[:, t * LANES : (t + 1) * LANES]
            return carry

        lax.fori_loop(0, share, scale_member, 0, unroll=4)

    lane = lax.broadcasted_iota(jnp.int32, (half, LANES), 1)
    pull_lane = members + half
    from_top = (lane < members) | (lane == pull_lane) | (lane == pull_lane + 2)
    spare = LANES - pull_lane

    def block_group(i, carry):
        for u in range(unroll):
            b = i * unroll + u
            spread = jnp.concatenate(
                [rows_ref[t, pl.ds(b, members, stride=blocks), :] for t in range(tiles)], axis=1
            )
            weights = jnp.broadcast_to(weight_ref[pl.ds(b, 1), :], (spare, width))
            right = jnp.concatenate([spread, spread[half:], weights], axis=0).astype(BF16)
            product = lax.dot_general(
                spread.astype(BF16), right, (((1,), (1,)), ((), ())), preferred_element_type=F32
            )
            packed = jnp.where(from_top, product[:half], product[half:])
            own_ref[pl.ds(pl.multiple_of(b * half, 8), half), :] = packed
        return carry

    lax.fori_loop(0, blocks // unroll, block_group, 0)

    step = 2 * half
    lane2 = lax.broadcasted_iota(jnp.int32, (step, LANES), 1)

    def finish(i, carry):
        at = pl.ds(pl.multiple_of(i * step, 16), step)
        value = own_ref[at, :]
        low = value - value.astype(BF16).astype(F32)
        is_low = lane2 >= pull_lane + 2
        send_ref[at, :] = jnp.where(is_low, low, value).astype(BF16)
        own_ref[at, :] = jnp.where(is_low, 0.0, value)
        return carry

    lax.fori_loop(0, blocks // 2, finish, 0, unroll=2)


def packed_grams(mem, parts, scale, weighted):
    groups = len(parts)
    share, blocks, width = parts[0].shape
    members = groups * share
    half = members // 2
    assert members + half + 4 <= LANES and half % 8 == 0
    flat = (blocks * half, LANES)
    return pl.pallas_call(
        functools.partial(
            gram_kernel, groups=groups, share=share, blocks=blocks, width=width, unroll=4
        ),
        out_shape=(jax.ShapeDtypeStruct(flat, F32), jax.ShapeDtypeStruct(flat, BF16)),
        in_specs=[smem()] + [vmem()] * (groups + 2),
        out_specs=(vmem(), vmem()),
        scratch_shapes=[pltpu.VMEM((width // LANES, members * blocks, LANES), F32)],
        compiler_params=params(),
        cost_estimate=pl.CostEstimate(
            flops=2 * blocks * members * width * LANES,
            bytes_accessed=members * blocks * width * 2,
            transcendentals=0,
        ),
        name="packed_grams",
    )(mem, *parts, scale, weighted)


def blend_kernel(
    row_ref, taper_ref, left_ref, own_ref, right_ref, blend_ref, window_ref, *, members, neighbours, blocks, unroll
):
    half = members // 2
    pull_lane = members + half
    halo = left_ref.shape[0]
    count = own_ref.shape[0]
    window_ref[pl.ds(0, halo), :] = left_ref[...].astype(F32)
    window_ref[pl.ds(halo, count), :] = own_ref[...]
    window_ref[pl.ds(halo + count, halo), :] = right_ref[...].astype(F32)
    full = (members, LANES)
    lane = lax.broadcasted_iota(jnp.int32, full, 1)
    row = lax.broadcasted_iota(jnp.int32, full, 0)
    valid = lane < members
    eye = (lane == row).astype(F32)
    left_half = lax.broadcasted_iota(jnp.int32, (half, LANES), 1) < half
    pad_rows = jnp.zeros((LANES - half, LANES), F32)
    pad_depth = jnp.zeros((LANES - members, LANES), BF16)

    def total(x):
        return jnp.sum(jnp.sum(x, axis=0, keepdims=True), axis=1, keepdims=True)

    def times(lhs, rhs):
        return jnp.dot(
            lhs, jnp.concatenate([rhs, pad_depth], axis=0), preferred_element_type=F32
        )

    def one_block(b):
        packed = None
        for n in range(neighbours):
            start = pl.multiple_of(row_ref[b * neighbours + n], 8)
            term = taper_ref[b * neighbours + n] * window_ref[pl.ds(start, half), :]
            packed = term if packed is None else packed + term
        turned = jnp.concatenate([packed, pad_rows], axis=0).T
        low_rows = jnp.where(
            left_half, turned[half:members], pltpu.roll(packed, LANES - half, axis=1)
        )
        summed = jnp.concatenate([packed, low_rows], axis=0)
        matrix = eye + jnp.where(valid, summed, 0.0) * (1.0 / (members - 1))
        pull = turned[pull_lane : pull_lane + 8]
        pull_row = (pull[0:1] + pull[2:3]) + pltpu.roll(pull[1:2] + pull[3:4], half, axis=1)

        frob = jnp.sqrt(total(matrix * matrix))
        scaled = matrix * (1.0 / frob)
        y = total(scaled * eye) * (1.0 / members)
        y_rest = scaled - y * eye
        p, p_rest = y, y_rest
        z, z_rest = None, None
        for sweep in range(SWEEPS):
            last = sweep == SWEEPS - 1
            y_low = y_rest.astype(BF16)
            if sweep > 0:
                z_low = z_rest.astype(BF16)
                p = z * y
                p_rest = z * y_rest + y * z_rest + times(z_low, y_low)
            p_low = p_rest.astype(BF16)
            s = 1.5 - 0.5 * p
            if sweep == 0:
                y_rest = s * y_rest - 0.5 * (y * p_rest + times(y_low, p_low))
                z, z_rest = s, -0.5 * p_rest
                y = s * y
            elif not last:
                both = times(jnp.concatenate([y_low, z_low], axis=0), p_low)
                y_rest = s * y_rest - 0.5 * (y * p_rest + both[:members])
                z_rest = s * z_rest - 0.5 * (z * p_rest + both[members:])
                y, z = s * y, s * z
            else:
                z_rest = s * z_rest - 0.5 * (z * p_rest + times(z_low, p_low))
                z = s * z
        root = (z * eye + z_rest) * lax.rsqrt(frob)
        inner = jnp.sum(root * pull_row, axis=1, keepdims=True)
        shift = jnp.sum(root * inner, axis=0, keepdims=True) * (1.0 / (members - 1))
        blend_ref[pl.ds(pl.multiple_of(b * members, 16), members), :] = (root + shift).astype(BF16)

    def block_group(i, carry):
        for u in range(unroll):
            one_block(i * unroll + u)
        return carry

    lax.fori_loop(0, blocks // unroll, block_group, 0)


def blends(rows, tapers, left, own, right, members):
    blocks, neighbours = rows.shape
    return pl.pallas_call(
        functools.partial(
            blend_kernel, members=members, neighbours=neighbours, blocks=blocks, unroll=4
        ),
        out_shape=jax.ShapeDtypeStruct((blocks * members, LANES), BF16),
        in_specs=[smem(), smem(), vmem(), vmem(), vmem()],
        out_specs=vmem(),
        scratch_shapes=[
            pltpu.VMEM((left.shape[0] + own.shape[0] + right.shape[0], LANES), F32)
        ],
        compiler_params=params(),
        cost_estimate=pl.CostEstimate(
            flops=blocks * 24 * members * members * LANES,
            bytes_accessed=4 * own.shape[0] * LANES * 4,
            transcendentals=0,
        ),
        name="blends",
    )(rows.reshape(-1), tapers.reshape(-1), left, own, right)


def apply_kernel(mem_ref, *refs, groups, share, blocks, width, unroll):
    parts = refs[:groups]
    blend_ref = refs[groups]
    outs = refs[groups + 1 : 2 * groups + 1]
    center_ref, rows_ref = refs[2 * groups + 1 :]
    members = groups * share
    tiles = width // LANES
    mem = mem_ref[0]
    zero = jnp.zeros((blocks, width), F32)
    center = zero
    for d in range(groups):
        center = lax.fori_loop(
            0, share, lambda k, acc, part=parts[d]: acc + part[k].astype(F32), center, unroll=4
        )
    center = center * (1.0 / members)
    center_ref[...] = center
    for d in range(groups):
        base = (mem ^ d) * (share * blocks)

        def perturb(k, carry, part=parts[d], base=base):
            value = (part[k].astype(F32) - center_ref[...]).astype(BF16).astype(F32)
            start = pl.multiple_of(base + k * blocks, 8)
            for t in range(tiles):
                rows_ref[t, pl.ds(start, blocks), :] = value[:, t * LANES : (t + 1) * LANES]
            return carry

        lax.fori_loop(0, share, perturb, 0, unroll=4)

    pad_depth = jnp.zeros((LANES - members, width), BF16)

    def block_group(i, carry):
        for u in range(unroll):
            b = i * unroll + u
            at = pl.ds(b, members, stride=blocks)
            anomalies = jnp.concatenate([rows_ref[t, at, :] for t in range(tiles)], axis=1)
            mixed = jnp.dot(
                blend_ref[pl.ds(pl.multiple_of(b * members, 16), members), :],
                jnp.concatenate([anomalies.astype(BF16), pad_depth], axis=0),
                preferred_element_type=F32,
            )
            for t in range(tiles):
                rows_ref[t, at, :] = mixed[:, t * LANES : (t + 1) * LANES]
        return carry

    lax.fori_loop(0, blocks // unroll, block_group, 0)

    for d in range(groups):
        base = (mem ^ d) * (share * blocks)

        def finish(k, carry, out=outs[d], base=base):
            start = pl.multiple_of(base + k * blocks, 8)
            mixed = jnp.concatenate(
                [rows_ref[t, pl.ds(start, blocks), :] for t in range(tiles)], axis=1
            )
            out[k] = (center_ref[...] + mixed).astype(BF16)
            return carry

        lax.fori_loop(0, share, finish, 0, unroll=4)


def apply_blend(mem, parts, blend):
    groups = len(parts)
    share, blocks, width = parts[0].shape
    members = groups * share
    part = jax.ShapeDtypeStruct((share, blocks, width), BF16)
    return pl.pallas_call(
        functools.partial(
            apply_kernel, groups=groups, share=share, blocks=blocks, width=width, unroll=4
        ),
        out_shape=(part,) * groups,
        in_specs=[smem()] + [vmem()] * (groups + 1),
        out_specs=(vmem(),) * groups,
        scratch_shapes=[
            pltpu.VMEM((blocks, width), F32),
            pltpu.VMEM((width // LANES, members * blocks, LANES), F32),
        ],
        compiler_params=params(),
        cost_estimate=pl.CostEstimate(
            flops=2 * blocks * members * LANES * width,
            bytes_accessed=2 * members * blocks * width * 2,
            transcendentals=0,
        ),
        name="apply_blend",
    )(mem, *parts, blend)


def taper_of(offset):
    ratio = offset.astype(F32) / RADIUS
    return 1.0 / (1.0 + ratio * ratio)


def on_device(
    prior_fields,
    scaled_sensor_spread,
    measured_misfit,
    inverse_error_variance,
    active_sensor_number,
    adjacent_tiles,
):
    groups = lax.axis_size("mem")
    belts = lax.axis_size("lon")
    share, lon_rows, width = scaled_sensor_spread.shape
    members = groups * share
    half = members // 2
    total_blocks = lon_rows * belts
    blocks = lon_rows // groups
    assert groups & (groups - 1) == 0 and blocks == RADIUS
    mem = lax.axis_index("mem")
    lon = lax.axis_index("lon")
    flip = (lon % 2) * (groups - 1)
    mine = mem ^ flip
    peers = [[(i, i ^ d) for i in range(groups)] for d in range(groups)]
    far_first = sorted(range(1, groups), key=lambda d: (d < groups // 2, d))

    def holder(g):
        belt, q = divmod(g % (belts * groups), groups)
        return (q ^ ((belt % 2) * (groups - 1))) * belts + belt

    ring = range(belts * groups)
    forward = [(holder(g), holder(g + 1)) for g in ring]
    backward = [(holder(g), holder(g - 1)) for g in ring]

    def piece(x, d):
        return lax.dynamic_slice_in_dim(x, ((mem ^ d) ^ flip) * blocks, blocks, 1)

    def gathered(x):
        parts = {d: lax.ppermute(piece(x, d), "mem", peers[d]) for d in far_first}
        parts[0] = piece(x, 0)
        return [parts[d] for d in range(groups)]

    def own_rows(x):
        return lax.dynamic_slice_in_dim(x, mine * blocks, blocks, 0)

    mem_scalar = mem.astype(jnp.int32).reshape(1)
    slot_ids = jnp.arange(width, dtype=jnp.int32)
    live = (slot_ids[None, :] < own_rows(active_sensor_number)[:, None]).astype(F32)
    obs_scale = jnp.sqrt(own_rows(inverse_error_variance) * live)
    weighted = own_rows(measured_misfit) * obs_scale
    local_ids = jnp.arange(blocks, dtype=jnp.int32)
    block_ids = lon * lon_rows + mine * blocks + local_ids
    offset_raw = jnp.mod(own_rows(adjacent_tiles) - block_ids[:, None], total_blocks)
    offset = jnp.where(offset_raw > total_blocks // 2, offset_raw - total_blocks, offset_raw)
    window_rows = (local_ids[:, None] + RADIUS + offset) * half
    tapers = taper_of(offset)

    spread_parts = gathered(scaled_sensor_spread)
    field_parts = gathered(prior_fields)
    own, send = packed_grams(mem_scalar, spread_parts, obs_scale, weighted)
    left = lax.ppermute(send, ("mem", "lon"), forward)
    right = lax.ppermute(send, ("mem", "lon"), backward)
    blend = blends(window_rows, tapers, left, own, right, members)
    out_parts = apply_blend(mem_scalar, field_parts, blend)
    result = jnp.zeros(prior_fields.shape, BF16)
    result = lax.dynamic_update_slice_in_dim(result, out_parts[0], mine * blocks, 1)
    for d in reversed(far_first):
        came = lax.ppermute(out_parts[d], "mem", peers[d])
        result = lax.dynamic_update_slice_in_dim(result, came, ((mem ^ d) ^ flip) * blocks, 1)
    return result


def solution(mesh):
    return jax.shard_map(
        on_device,
        mesh=mesh,
        in_specs=(
            P("mem", "lon", None),
            P("mem", "lon", None),
            P("lon", None),
            P("lon", None),
            P("lon"),
            P("lon", None),
        ),
        out_specs=P("mem", "lon", None),
        check_vma=False,
    )
```

profile of v0, /device:TPU:0, one launch (start us, length us, event | category | flops | bytes accessed | tf_op | source)
XLA Modules:
  0.0 146.2 jit_solution(1160374672039983324)
XLA Ops:
  0.0 0.0 copy-start
  0.0 2.8 %constant_dynamic-slice_fusion = (bf16[20,48,256]{2,1,0:T(8,128)(2,1)}, bf16[20,48,256]{2,1,0:T(8,128)(2,1)S(1)}, bf16[20,48,256]{2,1,0:T(8,128)(2,1)}, bf16[20,48,256]{2,1,0:T(8,128)(2,1)}) fusion(bf16[20,192,256]{2,1,0:T(8,128)(2,1)} %param.7, s32[]{:T(128)S(6)} %select_n.45, s32[]{:T(128)S(6)} %select_n.43, s32[]{:T(128)S(6)} %select_n.42, s32[]{:T(128)S(6)} %select_n.44), kind=kLoop, calls=%fused_computation.11 | loop fusion | bytes 3932176 | tf_op jit(solution)/shard_map/dynamic_slice | solution.py:339
  2.8 0.5 collective-permute-start.3
  3.3 2.5 %collective-permute-start.4 = (bf16[20,48,256]{2,1,0:T(8,128)(2,1)}, bf16[20,48,256]{2,1,0:T(8,128)(2,1)}, u32[]{:S(2)}, u32[]{:S(2)}) collective-permute-start(bf16[20,48,256]{2,1,0:T(8,128)(2,1)} %get-tuple-element.22), channel_id=1, source_target_pairs={{0,16},{8,24},{16,0},{24,8},{1,17},{9,25},{17,1},{25,9},{2,18},{10... | collective-permute-start | bytes 1474568 | tf_op jit(solution)/shard_map/ppermute | solution.py:342
  5.7 0.0 copy-start.9
  5.7 0.1 collective-permute-start.5
  5.9 0.0 copy-done
  5.9 0.9 constant_dynamic-slice_fusion.4
  6.8 0.0 copy-start.7
  6.8 0.1 collective-permute-start
  6.9 1.9 %collective-permute-start.1 = (bf16[20,48,256]{2,1,0:T(8,128)(2,1)S(1)}, bf16[20,48,256]{2,1,0:T(8,128)(2,1)S(1)}, u32[]{:S(2)}, u32[]{:S(2)}) collective-permute-start(bf16[20,48,256]{2,1,0:T(8,128)(2,1)S(1)} %get-tuple-element.26), channel_id=1, source_target_pairs={{0,16},{8,24},{16,0},{24,8},{1,17},{9,25},{17,1},{25,9},{2,18},{10... | collective-permute-start | bytes 1474568 | tf_op jit(solution)/shard_map/ppermute | solution.py:342
  8.8 0.0 copy-done.9
  8.8 0.1 dynamic_slice.45
  8.9 1.5 %dynamic-slice_multiply_fusion = (f32[48,256]{1,0:T(8,128)}, f32[48,256]{1,0:T(8,128)}) fusion(f32[192,256]{1,0:T(8,128)} %param.8, s32[]{:T(128)S(6)} %select_n.42, f32[192,256]{1,0:T(8,128)} %param.9, s32[48]{0:T(128)S(1)} %dynamic_slice.45), kind=kLoop, calls=%fused_computation | loop fusion | flops 36864 | bytes 196804 | tf_op jit(solution)/shard_map/mul | solution.py:353
  10.4 0.0 collective-permute-done.3.refs_1_
  10.5 0.0 copy-start.6
  10.5 0.1 collective-permute-start.2
  10.5 7.6 %collective-permute-done.4.refs_2_ = bf16[20,48,256]{2,1,0:T(8,128)(2,1)} collective-permute-done((bf16[20,48,256]{2,1,0:T(8,128)(2,1)}, bf16[20,48,256]{2,1,0:T(8,128)(2,1)}, u32[]{:S(2)}, u32[]{:S(2)}) %collective-permute-start.4) | collective-permute-done | bytes 491552 | tf_op jit(solution)/shard_map/ppermute | solution.py:342
  18.1 10.2 %collective-permute-done.5.refs_3_ = bf16[20,48,256]{2,1,0:T(8,128)(2,1)} collective-permute-done((bf16[20,48,256]{2,1,0:T(8,128)(2,1)}, bf16[20,48,256]{2,1,0:T(8,128)(2,1)}, u32[]{:S(2)}, u32[]{:S(2)}) %collective-permute-start.5) | collective-permute-done | bytes 491552 | tf_op jit(solution)/shard_map/ppermute | solution.py:342
  28.3 0.0 copy-done.6
  28.3 6.5 %packed_grams.1 = (f32[1920,128]{1,0:T(8,128)}, bf16[1920,128]{1,0:T(8,128)(2,1)}) custom-call(s32[1]{0:T(128)} %bitcast.mem_ref, bf16[20,48,256]{2,1,0:T(8,128)(2,1)} %get-tuple-element.21.refs_0_, bf16[20,48,256]{2,1,0:T(8,128)(2,1)} %copy-done.6, bf16[20,48,256]{2,1,0:T(8,128)(2,1)} %collective-permute-done.4.refs_2_, ...), custom_call_target="tpu_custom_call" | custom-call | flops 251658240 | bytes 1966080 | tf_op jit(solution)/shard_map/packed_grams/pallas_call | solution.py:94
  34.8 0.2 collective-permute-start.6
  35.0 4.5 %collective-permute-start.7 = (bf16[1920,128]{1,0:T(8,128)(2,1)}, bf16[1920,128]{1,0:T(8,128)(2,1)}, u32[]{:S(2)}, u32[]{:S(2)}) collective-permute-start(bf16[1920,128]{1,0:T(8,128)(2,1)} %get-tuple-element.11), channel_id=1, source_target_pairs={{0,7},{8,0},{16,8},{24,16},{25,24},{17,25},{9,17},{1,9},{2,1},{10,... | collective-permute-start | bytes 1474568 | tf_op jit(solution)/shard_map/ppermute | solution.py:365
  39.5 0.0 copy-done.7
  39.5 0.1 add_multiply_fusion
  39.6 0.1 copy.7
  39.7 0.7 reshape.20.row_ref
  40.4 0.1 add_divide_fusion
  40.5 0.1 copy.8
  40.5 0.7 reshape.21.taper_ref
  41.2 5.3 %collective-permute-done.6.left_ref = bf16[1920,128]{1,0:T(8,128)(2,1)S(1)} collective-permute-done((bf16[1920,128]{1,0:T(8,128)(2,1)}, bf16[1920,128]{1,0:T(8,128)(2,1)S(1)}, u32[]{:S(2)}, u32[]{:S(2)}) %collective-permute-start.6) | collective-permute-done | bytes 491552 | tf_op jit(solution)/shard_map/ppermute | solution.py:364
  46.5 0.0 copy-start.8
  46.5 0.0 collective-permute-done.7.right_ref
  46.5 0.8 copy-done.8
  47.3 56.7 %blends.1.refs_4_ = bf16[3840,128]{1,0:T(8,128)(2,1)} custom-call(s32[768]{0:T(1024)} %reshape.20.row_ref, f32[768]{0:T(1024)} %reshape.21.taper_ref, bf16[1920,128]{1,0:T(8,128)(2,1)} %copy-done.8, f32[1920,128]{1,0:T(8,128)} %get-tuple-element.12.own_ref, bf16[1920,128]{1,0:T(8,128)(2,1)} %collective-permute-done.7.right_ref), custom_call_target="tpu_custom_call" | custom-call | flops 943718400 | bytes 3932160 | tf_op jit(solution)/shard_map/blends/pallas_call | solution.py:196
  104.1 0.0 collective-permute-done.refs_1_
  104.1 0.0 copy-start.2
  104.1 0.0 collective-permute-done.1.refs_2_
  104.1 0.0 copy-start.3
  104.1 0.0 collective-permute-done.2.refs_3_
  104.1 0.0 copy-start.4
  104.1 0.7 copy-done.2
  104.8 0.2 copy-done.3
  105.0 0.1 copy-done.4
  105.2 7.7 %apply_blend.1 = (bf16[20,48,256]{2,1,0:T(8,128)(2,1)}, bf16[20,48,256]{2,1,0:T(8,128)(2,1)}, bf16[20,48,256]{2,1,0:T(8,128)(2,1)}, bf16[20,48,256]{2,1,0:T(8,128)(2,1)}) custom-call(s32[1]{0:T(128)} %bitcast.mem_ref, bf16[20,48,256]{2,1,0:T(8,128)(2,1)} %get-tuple-element.25.refs_0_, bf16[20,48,256]{2,1,0:T(8,128)(2,1)} %copy-done.2, ...), custom_call_target="tpu_custom_call" | custom-call | flops 251658240 | bytes 3932160 | tf_op jit(solution)/shard_map/apply_blend/pallas_call | solution.py:281
  112.9 0.0 copy-start.5
  112.9 7.7 %collective-permute-start.8 = (bf16[20,48,256]{2,1,0:T(8,128)(2,1)}, bf16[20,48,256]{2,1,0:T(8,128)(2,1)S(1)}, u32[]{:S(2)}, u32[]{:S(2)}) collective-permute-start(bf16[20,48,256]{2,1,0:T(8,128)(2,1)} %get-tuple-element.14), channel_id=1, source_target_pairs={{0,8},{8,0},{16,24},{24,16},{1,9},{9,1},{17,25},{25,17},{2,10},{10... | collective-permute-start | bytes 1474568 | tf_op jit(solution)/shard_map/ppermute | solution.py:371
  120.5 2.4 %collective-permute-start.9 = (bf16[20,48,256]{2,1,0:T(8,128)(2,1)}, bf16[20,48,256]{2,1,0:T(8,128)(2,1)S(1)}, u32[]{:S(2)}, u32[]{:S(2)}) collective-permute-start(bf16[20,48,256]{2,1,0:T(8,128)(2,1)} %get-tuple-element.15), channel_id=1, source_target_pairs={{0,24},{8,16},{16,8},{24,0},{1,25},{9,17},{17,9},{25,1},{2,26},{10... | collective-permute-start | bytes 1474568 | tf_op jit(solution)/shard_map/ppermute | solution.py:371
  122.9 0.0 collective-permute-start.10
  122.9 0.2 broadcast_in_dim.2
  123.1 0.0 copy-done.5
  123.2 0.0 collective-permute-done.8
  123.3 11.6 %collective-permute-done.9 = bf16[20,48,256]{2,1,0:T(8,128)(2,1)S(1)} collective-permute-done((bf16[20,48,256]{2,1,0:T(8,128)(2,1)}, bf16[20,48,256]{2,1,0:T(8,128)(2,1)S(1)}, u32[]{:S(2)}, u32[]{:S(2)}) %collective-permute-start.9) | collective-permute-done | bytes 491552 | tf_op jit(solution)/shard_map/ppermute | solution.py:371
  134.9 0.0 copy-start.1
  134.9 10.5 %collective-permute-done.10 = bf16[20,48,256]{2,1,0:T(8,128)(2,1)S(1)} collective-permute-done((bf16[20,48,256]{2,1,0:T(8,128)(2,1)}, bf16[20,48,256]{2,1,0:T(8,128)(2,1)S(1)}, u32[]{:S(2)}, u32[]{:S(2)}) %collective-permute-start.10) | collective-permute-done | bytes 491552 | tf_op jit(solution)/shard_map/ppermute | solution.py:371
  145.4 0.0 copy-done.1
  145.4 0.8 constant_dynamic-update-slice_fusion.3
  (5 shorter events, 0.1 us)
Async XLA Ops:
  0.0 5.9 %copy-start = (bf16[20,192,256]{2,1,0:T(8,128)(2,1)S(1)}, bf16[20,192,256]{2,1,0:T(8,128)(2,1)}, u32[]{:S(2)}) copy-start(bf16[20,192,256]{2,1,0:T(8,128)(2,1)} %param.6) | copy-start | bytes 5898244
  2.8 7.7 %collective-permute-start.3 = (bf16[20,48,256]{2,1,0:T(8,128)(2,1)S(1)}, bf16[20,48,256]{2,1,0:T(8,128)(2,1)S(1)}, u32[]{:S(2)}, u32[]{:S(2)}) collective-permute-start(bf16[20,48,256]{2,1,0:T(8,128)(2,1)S(1)} %get-tuple-element.20), channel_id=1, source_target_pairs={{0,8},{8,0},{16,24},{24,16},{1,9},{9,1},{17,25},{25,17},{2,10},{10... | collective-permute-start | bytes 1474568 | tf_op jit(solution)/shard_map/ppermute | solution.py:342
  3.3 14.9 %collective-permute-start.4 = (bf16[20,48,256]{2,1,0:T(8,128)(2,1)}, bf16[20,48,256]{2,1,0:T(8,128)(2,1)}, u32[]{:S(2)}, u32[]{:S(2)}) collective-permute-start(bf16[20,48,256]{2,1,0:T(8,128)(2,1)} %get-tuple-element.22), channel_id=1, source_target_pairs={{0,16},{8,24},{16,0},{24,8},{1,17},{9,25},{17,1},{25,9},{2,18},{10... | collective-permute-start | bytes 1474568 | tf_op jit(solution)/shard_map/ppermute | solution.py:342
  5.7 3.1 %copy-start.9 = (s32[192]{0:T(256)S(1)}, s32[192]{0:T(256)}, u32[]{:S(2)}) copy-start(s32[192]{0:T(256)} %param.10) | copy-start | bytes 2308
  5.7 22.6 %collective-permute-start.5 = (bf16[20,48,256]{2,1,0:T(8,128)(2,1)}, bf16[20,48,256]{2,1,0:T(8,128)(2,1)}, u32[]{:S(2)}, u32[]{:S(2)}) collective-permute-start(bf16[20,48,256]{2,1,0:T(8,128)(2,1)} %get-tuple-element.19), channel_id=1, source_target_pairs={{0,24},{8,16},{16,8},{24,0},{1,25},{9,17},{17,9},{25,1},{2,26},{10... | collective-permute-start | bytes 1474568 | tf_op jit(solution)/shard_map/ppermute | solution.py:342
  6.8 32.7 %copy-start.7 = (s32[192,16]{0,1:T(8,128)S(1)}, s32[192,16]{0,1:T(8,128)}, u32[]{:S(2)}) copy-start(s32[192,16]{0,1:T(8,128)} %param.11) | copy-start | bytes 36868
  6.8 97.3 %collective-permute-start = (bf16[20,48,256]{2,1,0:T(8,128)(2,1)S(1)}, bf16[20,48,256]{2,1,0:T(8,128)(2,1)S(1)}, u32[]{:S(2)}, u32[]{:S(2)}) collective-permute-start(bf16[20,48,256]{2,1,0:T(8,128)(2,1)S(1)} %get-tuple-element.24), channel_id=1, source_target_pairs={{0,8},{8,0},{16,24},{24,16},{1,9},{9,1},{17,25},{25,17},{2,10},{10... | collective-permute-start | bytes 1474568 | tf_op jit(solution)/shard_map/ppermute | solution.py:342
  6.9 97.1 %collective-permute-start.1 = (bf16[20,48,256]{2,1,0:T(8,128)(2,1)S(1)}, bf16[20,48,256]{2,1,0:T(8,128)(2,1)S(1)}, u32[]{:S(2)}, u32[]{:S(2)}) collective-permute-start(bf16[20,48,256]{2,1,0:T(8,128)(2,1)S(1)} %get-tuple-element.26), channel_id=1, source_target_pairs={{0,16},{8,24},{16,0},{24,8},{1,17},{9,25},{17,1},{25,9},{2,18},{10... | collective-permute-start | bytes 1474568 | tf_op jit(solution)/shard_map/ppermute | solution.py:342
  10.5 17.8 %copy-start.6 = (bf16[20,48,256]{2,1,0:T(8,128)(2,1)}, bf16[20,48,256]{2,1,0:T(8,128)(2,1)S(1)}, u32[]{:S(2)}) copy-start(bf16[20,48,256]{2,1,0:T(8,128)(2,1)S(1)} %collective-permute-done.3.refs_1_) | copy-start | bytes 1474564
  10.5 93.6 %collective-permute-start.2 = (bf16[20,48,256]{2,1,0:T(8,128)(2,1)S(1)}, bf16[20,48,256]{2,1,0:T(8,128)(2,1)S(1)}, u32[]{:S(2)}, u32[]{:S(2)}) collective-permute-start(bf16[20,48,256]{2,1,0:T(8,128)(2,1)S(1)} %get-tuple-element.23), channel_id=1, source_target_pairs={{0,24},{8,16},{16,8},{24,0},{1,25},{9,17},{17,9},{25,1},{2,26},{10... | collective-permute-start | bytes 1474568 | tf_op jit(solution)/shard_map/ppermute | solution.py:342
  34.8 11.7 %collective-permute-start.6 = (bf16[1920,128]{1,0:T(8,128)(2,1)}, bf16[1920,128]{1,0:T(8,128)(2,1)S(1)}, u32[]{:S(2)}, u32[]{:S(2)}) collective-permute-start(bf16[1920,128]{1,0:T(8,128)(2,1)} %get-tuple-element.11), channel_id=1, source_target_pairs={{0,8},{8,16},{16,24},{24,25},{25,17},{17,9},{9,1},{1,2},{2,10},{10... | collective-permute-start | bytes 1474568 | tf_op jit(solution)/shard_map/ppermute | solution.py:364
  35.0 11.6 %collective-permute-start.7 = (bf16[1920,128]{1,0:T(8,128)(2,1)}, bf16[1920,128]{1,0:T(8,128)(2,1)}, u32[]{:S(2)}, u32[]{:S(2)}) collective-permute-start(bf16[1920,128]{1,0:T(8,128)(2,1)} %get-tuple-element.11), channel_id=1, source_target_pairs={{0,7},{8,0},{16,8},{24,16},{25,24},{17,25},{9,17},{1,9},{2,1},{10,... | collective-permute-start | bytes 1474568 | tf_op jit(solution)/shard_map/ppermute | solution.py:365
  46.5 0.8 copy-start.8
  104.1 0.8 copy-start.2
  104.1 1.0 copy-start.3
  104.1 1.1 copy-start.4
  112.9 10.3 %copy-start.5 = (bf16[20,48,256]{2,1,0:T(8,128)(2,1)S(1)}, bf16[20,48,256]{2,1,0:T(8,128)(2,1)}, u32[]{:S(2)}) copy-start(bf16[20,48,256]{2,1,0:T(8,128)(2,1)} %get-tuple-element.13) | copy-start | bytes 1474564
  112.9 10.3 %collective-permute-start.8 = (bf16[20,48,256]{2,1,0:T(8,128)(2,1)}, bf16[20,48,256]{2,1,0:T(8,128)(2,1)S(1)}, u32[]{:S(2)}, u32[]{:S(2)}) collective-permute-start(bf16[20,48,256]{2,1,0:T(8,128)(2,1)} %get-tuple-element.14), channel_id=1, source_target_pairs={{0,8},{8,0},{16,24},{24,16},{1,9},{9,1},{17,25},{25,17},{2,10},{10... | collective-permute-start | bytes 1474568 | tf_op jit(solution)/shard_map/ppermute | solution.py:371
  120.5 14.3 %collective-permute-start.9 = (bf16[20,48,256]{2,1,0:T(8,128)(2,1)}, bf16[20,48,256]{2,1,0:T(8,128)(2,1)S(1)}, u32[]{:S(2)}, u32[]{:S(2)}) collective-permute-start(bf16[20,48,256]{2,1,0:T(8,128)(2,1)} %get-tuple-element.15), channel_id=1, source_target_pairs={{0,24},{8,16},{16,8},{24,0},{1,25},{9,17},{17,9},{25,1},{2,26},{10... | collective-permute-start | bytes 1474568 | tf_op jit(solution)/shard_map/ppermute | solution.py:371
  122.9 22.5 %collective-permute-start.10 = (bf16[20,48,256]{2,1,0:T(8,128)(2,1)}, bf16[20,48,256]{2,1,0:T(8,128)(2,1)S(1)}, u32[]{:S(2)}, u32[]{:S(2)}) collective-permute-start(bf16[20,48,256]{2,1,0:T(8,128)(2,1)} %get-tuple-element.16), channel_id=1, source_target_pairs={{0,16},{8,24},{16,0},{24,8},{1,17},{9,25},{17,1},{25,9},{2,18},{10... | collective-permute-start | bytes 1474568 | tf_op jit(solution)/shard_map/ppermute | solution.py:371
  134.9 10.5 %copy-start.1 = (bf16[20,192,256]{2,1,0:T(8,128)(2,1)}, bf16[20,192,256]{2,1,0:T(8,128)(2,1)S(1)}, u32[]{:S(2)}) copy-start(bf16[20,192,256]{2,1,0:T(8,128)(2,1)S(1)} %constant_dynamic-update-slice_fusion) | copy-start | bytes 5898244
where the time goes:
time: 147 us; the launch traced here: 146 us
  Pallas kernels  70.9 us (48%)
  waiting for transfers between devices  45.2 us (31%)
  starting transfers between devices  20 us (14%)
  local copies, waits for them, and re-layouts  8.35 us (6%)
  other arithmetic  1.73 us (1%)
    pallas_call x1, Pallas kernels, blends(): pl.pallas_call(functools.partial(blend_kernel, members=members, neighbour...  56.7 us
    ppermute x3, waiting for transfers between devices, on_device(): came = lax.ppermute(out_parts[d], 'mem', peers[d])  22.1 us
    ppermute x6, waiting for transfers between devices, gathered(): parts = {d: lax.ppermute(piece(x, d), 'mem', peers[d]) for d in far_first}  17.8 us
    ppermute x3, starting transfers between devices, on_device(): came = lax.ppermute(out_parts[d], 'mem', peers[d])  10.1 us
    pallas_call x1, Pallas kernels, apply_blend(): pl.pallas_call(functools.partial(apply_kernel, groups=groups, share=share...  7.68 us
    pallas_call x1, Pallas kernels, packed_grams(): pl.pallas_call(functools.partial(gram_kernel, groups=groups, share=share,...  6.49 us
    ppermute x1, waiting for transfers between devices, on_device(): left = lax.ppermute(send, ('mem', 'lon'), forward)  5.31 us
    ppermute x6, starting transfers between devices, gathered(): parts = {d: lax.ppermute(piece(x, d), 'mem', peers[d]) for d in far_first}  5.17 us
  transfers between devices with their start and end apart: 11, of which 5 were waited for; matrix products, arithmetic and copies ran while one was open for 3% of the time, Pallas kernels for 43%

commit v1 on v0

--- a/solution.py
+++ b/solution.py
@@ -122,8 +122,9 @@
     full = (members, LANES)
     lane = lax.broadcasted_iota(jnp.int32, full, 1)
     row = lax.broadcasted_iota(jnp.int32, full, 0)
-    valid = lane < members
     eye = (lane == row).astype(F32)
+    in_matrix = lax.broadcasted_iota(jnp.int32, (1, LANES), 1) < members
+    share_row = jnp.where(in_matrix, 1.0 / (members - 1), 0.0)
     left_half = lax.broadcasted_iota(jnp.int32, (half, LANES), 1) < half
     pad_rows = jnp.zeros((LANES - half, LANES), F32)
     pad_depth = jnp.zeros((LANES - members, LANES), BF16)
@@ -136,7 +137,7 @@
             lhs, jnp.concatenate([rhs, pad_depth], axis=0), preferred_element_type=F32
         )
 
-    def one_block(b):
+    def localized_sum(b):
         packed = None
         for n in range(neighbours):
             start = pl.multiple_of(row_ref[b * neighbours + n], 8)
@@ -146,46 +147,70 @@
         low_rows = jnp.where(
             left_half, turned[half:members], pltpu.roll(packed, LANES - half, axis=1)
         )
-        summed = jnp.concatenate([packed, low_rows], axis=0)
-        matrix = eye + jnp.where(valid, summed, 0.0) * (1.0 / (members - 1))
         pull = turned[pull_lane : pull_lane + 8]
         pull_row = (pull[0:1] + pull[2:3]) + pltpu.roll(pull[1:2] + pull[3:4], half, axis=1)
-
-        frob = jnp.sqrt(total(matrix * matrix))
-        scaled = matrix * (1.0 / frob)
-        y = total(scaled * eye) * (1.0 / members)
-        y_rest = scaled - y * eye
-        p, p_rest = y, y_rest
-        z, z_rest = None, None
-        for sweep in range(SWEEPS):
+        return jnp.concatenate([packed, low_rows], axis=0) * share_row, pull_row
+
+    def block_group(i, carry):
+        group = range(unroll)
+        ids = [i * unroll + u for u in group]
+        sums = [localized_sum(b) for b in ids]
+        gram = [g for g, _ in sums]
+        trace = [total(g * eye) for g in gram]
+        square = [total(g * g) for g in gram]
+        frob2 = [square[u] + 2.0 * trace[u] + float(members) for u in group]
+        inv = [lax.rsqrt(f) for f in frob2]
+        mean = [t * (1.0 / members) for t in trace]
+        y = [(1.0 + mean[u]) * inv[u] for u in group]
+        y_rest = [(gram[u] - mean[u] * eye) * inv[u] for u in group]
+        p = [-0.5 * v for v in y]
+        p_rest = [-0.5 * v for v in y_rest]
+        s = [1.5 + v for v in p]
+        y_low = [v.astype(BF16) for v in y_rest]
+        p_low = [v.astype(BF16) for v in p_rest]
+        prod = [times(y_low[u], p_low[u]) for u in group]
+        z = [-0.5 * v for v in s]
+        z_rest = [-0.5 * v for v in p_rest]
+        y_rest = [(s[u] * y_rest[u] + y[u] * p_rest[u]) + prod[u] for u in group]
+        y = [s[u] * y[u] for u in group]
+        for sweep in range(1, SWEEPS):
             last = sweep == SWEEPS - 1
-            y_low = y_rest.astype(BF16)
-            if sweep > 0:
-                z_low = z_rest.astype(BF16)
-                p = z * y
-                p_rest = z * y_rest + y * z_rest + times(z_low, y_low)
-            p_low = p_rest.astype(BF16)
-            s = 1.5 - 0.5 * p
-            if sweep == 0:
-                y_rest = s * y_rest - 0.5 * (y * p_rest + times(y_low, p_low))
-                z, z_rest = s, -0.5 * p_rest
-                y = s * y
-            elif not last:
-                both = times(jnp.concatenate([y_low, z_low], axis=0), p_low)
-                y_rest = s * y_rest - 0.5 * (y * p_rest + both[:members])
-                z_rest = s * z_rest - 0.5 * (z * p_rest + both[members:])
-                y, z = s * y, s * z
+            y_low = [v.astype(BF16) for v in y_rest]
+            z_low = [v.astype(BF16) for v in z_rest]
+            prod = [times(z_low[u], y_low[u]) for u in group]
+            p = [z[u] * y[u] for u in group]
+            p_rest = [(z[u] * y_rest[u] + y[u] * z_rest[u]) + prod[u] for u in group]
+            s = [1.5 + v for v in p]
+            p_low = [v.astype(BF16) for v in p_rest]
+            if last:
+                prod = [times(z_low[u], p_low[u]) for u in group]
+                z_rest = [(s[u] * z_rest[u] + z[u] * p_rest[u]) + prod[u] for u in group]
             else:
-                z_rest = s * z_rest - 0.5 * (z * p_rest + times(z_low, p_low))
-                z = s * z
-        root = (z * eye + z_rest) * lax.rsqrt(frob)
-        inner = jnp.sum(root * pull_row, axis=1, keepdims=True)
-        shift = jnp.sum(root * inner, axis=0, keepdims=True) * (1.0 / (members - 1))
-        blend_ref[pl.ds(pl.multiple_of(b * members, 16), members), :] = (root + shift).astype(BF16)
-
-    def block_group(i, carry):
-        for u in range(unroll):
-            one_block(i * unroll + u)
+                prod = [
+                    times(jnp.concatenate([y_low[u], z_low[u]], axis=0), p_low[u])
+                    for u in group
+                ]
+                y_rest = [
+                    (s[u] * y_rest[u] + y[u] * p_rest[u]) + prod[u][:members] for u in group
+                ]
+                z_rest = [
+                    (s[u] * z_rest[u] + z[u] * p_rest[u]) + prod[u][members:] for u in group
+                ]
+                y = [s[u] * y[u] for u in group]
+            z = [s[u] * z[u] for u in group]
+        root = [z[u] * eye + z_rest[u] for u in group]
+        norm = [-2.0 * jnp.sqrt(v) for v in inv]
+        inner = [
+            jnp.sum(root[u] * sums[u][1], axis=1, keepdims=True) for u in group
+        ]
+        shift = [
+            jnp.sum(root[u] * inner[u], axis=0, keepdims=True)
+            * (norm[u] * norm[u] * (1.0 / (members - 1)))
+            for u in group
+        ]
+        for u in group:
+            at = pl.ds(pl.multiple_of(ids[u] * members, 16), members)
+            blend_ref[at, :] = (norm[u] * root[u] + shift[u]).astype(BF16)
         return carry
 
     lax.fori_loop(0, blocks // unroll, block_group, 0)
@@ -195,7 +220,7 @@
     blocks, neighbours = rows.shape
     return pl.pallas_call(
         functools.partial(
-            blend_kernel, members=members, neighbours=neighbours, blocks=blocks, unroll=4
+            blend_kernel, members=members, neighbours=neighbours, blocks=blocks, unroll=12
         ),
         out_shape=jax.ShapeDtypeStruct((blocks * members, LANES), BF16),
         in_specs=[smem(), smem(), vmem(), vmem(), vmem()],

time: 147 us -> 102 us (0.69)
  Pallas kernels: 70.9 us -> 26.2 us
    pallas_call x1, Pallas kernels: 56.7 us -> 12 us  [blends(): pl.pallas_call(functools.partial(blend_kernel, members=members, neighbour...]
  transfers between devices with their start and end apart: 11 -> 11, of which waited for: 5 -> 5; matrix products, arithmetic and copies ran while one was open for 3% -> 5% of each run, Pallas kernels for 43% -> 18%
where the time goes in v1:
time: 102 us
  waiting for transfers between devices  45.2 us (44%)
  Pallas kernels  26.2 us (26%)
  starting transfers between devices  19.9 us (20%)
  local copies, waits for them, and re-layouts  8.35 us (8%)
  other arithmetic  1.73 us (2%)
    ppermute x3, waiting for transfers between devices, on_device(): came = lax.ppermute(out_parts[d], 'mem', peers[d])  22.1 us
    ppermute x6, waiting for transfers between devices, gathered(): parts = {d: lax.ppermute(piece(x, d), 'mem', peers[d]) for d in far_first}  17.8 us
    pallas_call x1, Pallas kernels, blends(): pl.pallas_call(functools.partial(blend_kernel, members=members, neighbour...  12 us
    ppermute x3, starting transfers between devices, on_device(): came = lax.ppermute(out_parts[d], 'mem', peers[d])  10.1 us
    pallas_call x1, Pallas kernels, apply_blend(): pl.pallas_call(functools.partial(apply_kernel, groups=groups, share=share...  7.68 us
    pallas_call x1, Pallas kernels, packed_grams(): pl.pallas_call(functools.partial(gram_kernel, groups=groups, share=share,...  6.49 us
    ppermute x1, waiting for transfers between devices, on_device(): left = lax.ppermute(send, ('mem', 'lon'), forward)  5.31 us
    ppermute x6, starting transfers between devices, gathered(): parts = {d: lax.ppermute(piece(x, d), 'mem', peers[d]) for d in far_first}  5.17 us
  transfers between devices with their start and end apart: 11, of which 5 were waited for; matrix products, arithmetic and copies ran while one was open for 5% of the time, Pallas kernels for 18%

profile of v1, /device:TPU:0, one launch (start us, length us, event | category | flops | bytes accessed | tf_op | source)
XLA Modules:
  0.0 101.5 jit_solution(12836292446244417654)
XLA Ops:
  0.0 0.0 copy-start
  0.0 2.8 %constant_dynamic-slice_fusion = (bf16[20,48,256]{2,1,0:T(8,128)(2,1)}, bf16[20,48,256]{2,1,0:T(8,128)(2,1)S(1)}, bf16[20,48,256]{2,1,0:T(8,128)(2,1)}, bf16[20,48,256]{2,1,0:T(8,128)(2,1)}) fusion(bf16[20,192,256]{2,1,0:T(8,128)(2,1)} %param.7, s32[]{:T(128)S(6)} %select_n.45, s32[]{:T(128)S(6)} %select_n.43, s32[]{:T(128)S(6)} %select_n.42, s32[]{:T(128)S(6)} %select_n.44), kind=kLoop, calls=%fused_computation.11 | loop fusion | bytes 3932176 | tf_op jit(solution)/shard_map/dynamic_slice | solution.py:364
  2.8 0.5 collective-permute-start.3
  3.3 2.5 %collective-permute-start.4 = (bf16[20,48,256]{2,1,0:T(8,128)(2,1)}, bf16[20,48,256]{2,1,0:T(8,128)(2,1)}, u32[]{:S(2)}, u32[]{:S(2)}) collective-permute-start(bf16[20,48,256]{2,1,0:T(8,128)(2,1)} %get-tuple-element.22), channel_id=1, source_target_pairs={{0,16},{8,24},{16,0},{24,8},{1,17},{9,25},{17,1},{25,9},{2,18},{10... | collective-permute-start | bytes 1474568 | tf_op jit(solution)/shard_map/ppermute | solution.py:367
  5.7 0.0 copy-start.9
  5.7 0.1 collective-permute-start.5
  5.9 0.0 copy-done
  5.9 0.9 constant_dynamic-slice_fusion.4
  6.8 0.0 copy-start.7
  6.8 0.1 collective-permute-start
  6.9 1.9 %collective-permute-start.1 = (bf16[20,48,256]{2,1,0:T(8,128)(2,1)S(1)}, bf16[20,48,256]{2,1,0:T(8,128)(2,1)S(1)}, u32[]{:S(2)}, u32[]{:S(2)}) collective-permute-start(bf16[20,48,256]{2,1,0:T(8,128)(2,1)S(1)} %get-tuple-element.26), channel_id=1, source_target_pairs={{0,16},{8,24},{16,0},{24,8},{1,17},{9,25},{17,1},{25,9},{2,18},{10... | collective-permute-start | bytes 1474568 | tf_op jit(solution)/shard_map/ppermute | solution.py:367
  8.8 0.0 copy-done.9
  8.8 0.1 dynamic_slice.45
  8.9 1.5 %dynamic-slice_multiply_fusion = (f32[48,256]{1,0:T(8,128)}, f32[48,256]{1,0:T(8,128)}) fusion(f32[192,256]{1,0:T(8,128)} %param.8, s32[]{:T(128)S(6)} %select_n.42, f32[192,256]{1,0:T(8,128)} %param.9, s32[48]{0:T(128)S(1)} %dynamic_slice.45), kind=kLoop, calls=%fused_computation | loop fusion | flops 36864 | bytes 196804 | tf_op jit(solution)/shard_map/mul | solution.py:378
  10.4 0.0 collective-permute-done.3.refs_1_
  10.5 0.0 copy-start.6
  10.5 0.1 collective-permute-start.2
  10.5 7.6 %collective-permute-done.4.refs_2_ = bf16[20,48,256]{2,1,0:T(8,128)(2,1)} collective-permute-done((bf16[20,48,256]{2,1,0:T(8,128)(2,1)}, bf16[20,48,256]{2,1,0:T(8,128)(2,1)}, u32[]{:S(2)}, u32[]{:S(2)}) %collective-permute-start.4) | collective-permute-done | bytes 491552 | tf_op jit(solution)/shard_map/ppermute | solution.py:367
  18.1 10.2 %collective-permute-done.5.refs_3_ = bf16[20,48,256]{2,1,0:T(8,128)(2,1)} collective-permute-done((bf16[20,48,256]{2,1,0:T(8,128)(2,1)}, bf16[20,48,256]{2,1,0:T(8,128)(2,1)}, u32[]{:S(2)}, u32[]{:S(2)}) %collective-permute-start.5) | collective-permute-done | bytes 491552 | tf_op jit(solution)/shard_map/ppermute | solution.py:367
  28.3 0.0 copy-done.6
  28.3 6.5 %packed_grams.1 = (f32[1920,128]{1,0:T(8,128)}, bf16[1920,128]{1,0:T(8,128)(2,1)}) custom-call(s32[1]{0:T(128)} %bitcast.mem_ref, bf16[20,48,256]{2,1,0:T(8,128)(2,1)} %get-tuple-element.21.refs_0_, bf16[20,48,256]{2,1,0:T(8,128)(2,1)} %copy-done.6, bf16[20,48,256]{2,1,0:T(8,128)(2,1)} %collective-permute-done.4.refs_2_, ...), custom_call_target="tpu_custom_call" | custom-call | flops 251658240 | bytes 1966080 | tf_op jit(solution)/shard_map/packed_grams/pallas_call | solution.py:94
  34.8 0.2 collective-permute-start.6
  35.0 4.5 %collective-permute-start.7 = (bf16[1920,128]{1,0:T(8,128)(2,1)}, bf16[1920,128]{1,0:T(8,128)(2,1)}, u32[]{:S(2)}, u32[]{:S(2)}) collective-permute-start(bf16[1920,128]{1,0:T(8,128)(2,1)} %get-tuple-element.11), channel_id=1, source_target_pairs={{0,7},{8,0},{16,8},{24,16},{25,24},{17,25},{9,17},{1,9},{2,1},{10,... | collective-permute-start | bytes 1474568 | tf_op jit(solution)/shard_map/ppermute | solution.py:390
  39.5 0.0 copy-done.7
  39.5 0.1 add_multiply_fusion
  39.6 0.1 copy.7
  39.7 0.7 reshape.20.row_ref
  40.4 0.1 add_divide_fusion
  40.5 0.1 copy.8
  40.5 0.7 reshape.21.taper_ref
  41.2 5.3 %collective-permute-done.6.left_ref = bf16[1920,128]{1,0:T(8,128)(2,1)S(1)} collective-permute-done((bf16[1920,128]{1,0:T(8,128)(2,1)}, bf16[1920,128]{1,0:T(8,128)(2,1)S(1)}, u32[]{:S(2)}, u32[]{:S(2)}) %collective-permute-start.6) | collective-permute-done | bytes 491552 | tf_op jit(solution)/shard_map/ppermute | solution.py:389
  46.5 0.0 copy-start.8
  46.5 0.0 collective-permute-done.7.right_ref
  46.5 0.8 copy-done.8
  47.3 12.0 %blends.1.refs_4_ = bf16[3840,128]{1,0:T(8,128)(2,1)} custom-call(s32[768]{0:T(1024)} %reshape.20.row_ref, f32[768]{0:T(1024)} %reshape.21.taper_ref, bf16[1920,128]{1,0:T(8,128)(2,1)} %copy-done.8, f32[1920,128]{1,0:T(8,128)} %get-tuple-element.12.own_ref, bf16[1920,128]{1,0:T(8,128)(2,1)} %collective-permute-done.7.right_ref), custom_call_target="tpu_custom_call" | custom-call | flops 943718400 | bytes 3932160 | tf_op jit(solution)/shard_map/blends/pallas_call | solution.py:221
  59.3 0.0 collective-permute-done.refs_1_
  59.4 0.0 copy-start.2
  59.4 0.0 collective-permute-done.1.refs_2_
  59.4 0.0 copy-start.3
  59.4 0.0 collective-permute-done.2.refs_3_
  59.4 0.0 copy-start.4
  59.4 0.7 copy-done.2
  60.1 0.2 copy-done.3
  60.3 0.1 copy-done.4
  60.5 7.7 %apply_blend.1 = (bf16[20,48,256]{2,1,0:T(8,128)(2,1)}, bf16[20,48,256]{2,1,0:T(8,128)(2,1)}, bf16[20,48,256]{2,1,0:T(8,128)(2,1)}, bf16[20,48,256]{2,1,0:T(8,128)(2,1)}) custom-call(s32[1]{0:T(128)} %bitcast.mem_ref, bf16[20,48,256]{2,1,0:T(8,128)(2,1)} %get-tuple-element.25.refs_0_, bf16[20,48,256]{2,1,0:T(8,128)(2,1)} %copy-done.2, ...), custom_call_target="tpu_custom_call" | custom-call | flops 251658240 | bytes 3932160 | tf_op jit(solution)/shard_map/apply_blend/pallas_call | solution.py:306
  68.2 0.0 copy-start.5
  68.2 7.7 %collective-permute-start.8 = (bf16[20,48,256]{2,1,0:T(8,128)(2,1)}, bf16[20,48,256]{2,1,0:T(8,128)(2,1)S(1)}, u32[]{:S(2)}, u32[]{:S(2)}) collective-permute-start(bf16[20,48,256]{2,1,0:T(8,128)(2,1)} %get-tuple-element.14), channel_id=1, source_target_pairs={{0,8},{8,0},{16,24},{24,16},{1,9},{9,1},{17,25},{25,17},{2,10},{10... | collective-permute-start | bytes 1474568 | tf_op jit(solution)/shard_map/ppermute | solution.py:396
  75.8 2.4 %collective-permute-start.9 = (bf16[20,48,256]{2,1,0:T(8,128)(2,1)}, bf16[20,48,256]{2,1,0:T(8,128)(2,1)S(1)}, u32[]{:S(2)}, u32[]{:S(2)}) collective-permute-start(bf16[20,48,256]{2,1,0:T(8,128)(2,1)} %get-tuple-element.15), channel_id=1, source_target_pairs={{0,24},{8,16},{16,8},{24,0},{1,25},{9,17},{17,9},{25,1},{2,26},{10... | collective-permute-start | bytes 1474568 | tf_op jit(solution)/shard_map/ppermute | solution.py:396
  78.2 0.0 collective-permute-start.10
  78.2 0.2 broadcast_in_dim.2
  78.4 0.0 copy-done.5
  78.5 0.0 collective-permute-done.8
  78.5 11.6 %collective-permute-done.9 = bf16[20,48,256]{2,1,0:T(8,128)(2,1)S(1)} collective-permute-done((bf16[20,48,256]{2,1,0:T(8,128)(2,1)}, bf16[20,48,256]{2,1,0:T(8,128)(2,1)S(1)}, u32[]{:S(2)}, u32[]{:S(2)}) %collective-permute-start.9) | collective-permute-done | bytes 491552 | tf_op jit(solution)/shard_map/ppermute | solution.py:396
  90.2 0.0 copy-start.1
  90.2 10.5 %collective-permute-done.10 = bf16[20,48,256]{2,1,0:T(8,128)(2,1)S(1)} collective-permute-done((bf16[20,48,256]{2,1,0:T(8,128)(2,1)}, bf16[20,48,256]{2,1,0:T(8,128)(2,1)S(1)}, u32[]{:S(2)}, u32[]{:S(2)}) %collective-permute-start.10) | collective-permute-done | bytes 491552 | tf_op jit(solution)/shard_map/ppermute | solution.py:396
  100.7 0.0 copy-done.1
  100.7 0.8 constant_dynamic-update-slice_fusion.3
  (5 shorter events, 0.1 us)
Async XLA Ops:
  0.0 5.9 %copy-start = (bf16[20,192,256]{2,1,0:T(8,128)(2,1)S(1)}, bf16[20,192,256]{2,1,0:T(8,128)(2,1)}, u32[]{:S(2)}) copy-start(bf16[20,192,256]{2,1,0:T(8,128)(2,1)} %param.6) | copy-start | bytes 5898244
  2.8 7.7 %collective-permute-start.3 = (bf16[20,48,256]{2,1,0:T(8,128)(2,1)S(1)}, bf16[20,48,256]{2,1,0:T(8,128)(2,1)S(1)}, u32[]{:S(2)}, u32[]{:S(2)}) collective-permute-start(bf16[20,48,256]{2,1,0:T(8,128)(2,1)S(1)} %get-tuple-element.20), channel_id=1, source_target_pairs={{0,8},{8,0},{16,24},{24,16},{1,9},{9,1},{17,25},{25,17},{2,10},{10... | collective-permute-start | bytes 1474568 | tf_op jit(solution)/shard_map/ppermute | solution.py:367
  3.3 14.9 %collective-permute-start.4 = (bf16[20,48,256]{2,1,0:T(8,128)(2,1)}, bf16[20,48,256]{2,1,0:T(8,128)(2,1)}, u32[]{:S(2)}, u32[]{:S(2)}) collective-permute-start(bf16[20,48,256]{2,1,0:T(8,128)(2,1)} %get-tuple-element.22), channel_id=1, source_target_pairs={{0,16},{8,24},{16,0},{24,8},{1,17},{9,25},{17,1},{25,9},{2,18},{10... | collective-permute-start | bytes 1474568 | tf_op jit(solution)/shard_map/ppermute | solution.py:367
  5.7 3.1 %copy-start.9 = (s32[192]{0:T(256)S(1)}, s32[192]{0:T(256)}, u32[]{:S(2)}) copy-start(s32[192]{0:T(256)} %param.10) | copy-start | bytes 2308
  5.7 22.6 %collective-permute-start.5 = (bf16[20,48,256]{2,1,0:T(8,128)(2,1)}, bf16[20,48,256]{2,1,0:T(8,128)(2,1)}, u32[]{:S(2)}, u32[]{:S(2)}) collective-permute-start(bf16[20,48,256]{2,1,0:T(8,128)(2,1)} %get-tuple-element.19), channel_id=1, source_target_pairs={{0,24},{8,16},{16,8},{24,0},{1,25},{9,17},{17,9},{25,1},{2,26},{10... | collective-permute-start | bytes 1474568 | tf_op jit(solution)/shard_map/ppermute | solution.py:367
  6.8 32.7 %copy-start.7 = (s32[192,16]{0,1:T(8,128)S(1)}, s32[192,16]{0,1:T(8,128)}, u32[]{:S(2)}) copy-start(s32[192,16]{0,1:T(8,128)} %param.11) | copy-start | bytes 36868
  6.8 52.6 %collective-permute-start = (bf16[20,48,256]{2,1,0:T(8,128)(2,1)S(1)}, bf16[20,48,256]{2,1,0:T(8,128)(2,1)S(1)}, u32[]{:S(2)}, u32[]{:S(2)}) collective-permute-start(bf16[20,48,256]{2,1,0:T(8,128)(2,1)S(1)} %get-tuple-element.24), channel_id=1, source_target_pairs={{0,8},{8,0},{16,24},{24,16},{1,9},{9,1},{17,25},{25,17},{2,10},{10... | collective-permute-start | bytes 1474568 | tf_op jit(solution)/shard_map/ppermute | solution.py:367
  6.9 52.4 %collective-permute-start.1 = (bf16[20,48,256]{2,1,0:T(8,128)(2,1)S(1)}, bf16[20,48,256]{2,1,0:T(8,128)(2,1)S(1)}, u32[]{:S(2)}, u32[]{:S(2)}) collective-permute-start(bf16[20,48,256]{2,1,0:T(8,128)(2,1)S(1)} %get-tuple-element.26), channel_id=1, source_target_pairs={{0,16},{8,24},{16,0},{24,8},{1,17},{9,25},{17,1},{25,9},{2,18},{10... | collective-permute-start | bytes 1474568 | tf_op jit(solution)/shard_map/ppermute | solution.py:367
  10.5 17.8 %copy-start.6 = (bf16[20,48,256]{2,1,0:T(8,128)(2,1)}, bf16[20,48,256]{2,1,0:T(8,128)(2,1)S(1)}, u32[]{:S(2)}) copy-start(bf16[20,48,256]{2,1,0:T(8,128)(2,1)S(1)} %collective-permute-done.3.refs_1_) | copy-start | bytes 1474564
  10.5 48.9 %collective-permute-start.2 = (bf16[20,48,256]{2,1,0:T(8,128)(2,1)S(1)}, bf16[20,48,256]{2,1,0:T(8,128)(2,1)S(1)}, u32[]{:S(2)}, u32[]{:S(2)}) collective-permute-start(bf16[20,48,256]{2,1,0:T(8,128)(2,1)S(1)} %get-tuple-element.23), channel_id=1, source_target_pairs={{0,24},{8,16},{16,8},{24,0},{1,25},{9,17},{17,9},{25,1},{2,26},{10... | collective-permute-start | bytes 1474568 | tf_op jit(solution)/shard_map/ppermute | solution.py:367
  34.8 11.7 %collective-permute-start.6 = (bf16[1920,128]{1,0:T(8,128)(2,1)}, bf16[1920,128]{1,0:T(8,128)(2,1)S(1)}, u32[]{:S(2)}, u32[]{:S(2)}) collective-permute-start(bf16[1920,128]{1,0:T(8,128)(2,1)} %get-tuple-element.11), channel_id=1, source_target_pairs={{0,8},{8,16},{16,24},{24,25},{25,17},{17,9},{9,1},{1,2},{2,10},{10... | collective-permute-start | bytes 1474568 | tf_op jit(solution)/shard_map/ppermute | solution.py:389
  35.0 11.6 %collective-permute-start.7 = (bf16[1920,128]{1,0:T(8,128)(2,1)}, bf16[1920,128]{1,0:T(8,128)(2,1)}, u32[]{:S(2)}, u32[]{:S(2)}) collective-permute-start(bf16[1920,128]{1,0:T(8,128)(2,1)} %get-tuple-element.11), channel_id=1, source_target_pairs={{0,7},{8,0},{16,8},{24,16},{25,24},{17,25},{9,17},{1,9},{2,1},{10,... | collective-permute-start | bytes 1474568 | tf_op jit(solution)/shard_map/ppermute | solution.py:390
  46.5 0.8 copy-start.8
  59.4 0.8 copy-start.2
  59.4 1.0 copy-start.3
  59.4 1.1 %copy-start.4 = (bf16[20,48,256]{2,1,0:T(8,128)(2,1)}, bf16[20,48,256]{2,1,0:T(8,128)(2,1)S(1)}, u32[]{:S(2)}) copy-start(bf16[20,48,256]{2,1,0:T(8,128)(2,1)S(1)} %collective-permute-done.2.refs_3_) | copy-start | bytes 1474564
  68.2 10.3 %copy-start.5 = (bf16[20,48,256]{2,1,0:T(8,128)(2,1)S(1)}, bf16[20,48,256]{2,1,0:T(8,128)(2,1)}, u32[]{:S(2)}) copy-start(bf16[20,48,256]{2,1,0:T(8,128)(2,1)} %get-tuple-element.13) | copy-start | bytes 1474564
  68.2 10.3 %collective-permute-start.8 = (bf16[20,48,256]{2,1,0:T(8,128)(2,1)}, bf16[20,48,256]{2,1,0:T(8,128)(2,1)S(1)}, u32[]{:S(2)}, u32[]{:S(2)}) collective-permute-start(bf16[20,48,256]{2,1,0:T(8,128)(2,1)} %get-tuple-element.14), channel_id=1, source_target_pairs={{0,8},{8,0},{16,24},{24,16},{1,9},{9,1},{17,25},{25,17},{2,10},{10... | collective-permute-start | bytes 1474568 | tf_op jit(solution)/shard_map/ppermute | solution.py:396
  75.8 14.3 %collective-permute-start.9 = (bf16[20,48,256]{2,1,0:T(8,128)(2,1)}, bf16[20,48,256]{2,1,0:T(8,128)(2,1)S(1)}, u32[]{:S(2)}, u32[]{:S(2)}) collective-permute-start(bf16[20,48,256]{2,1,0:T(8,128)(2,1)} %get-tuple-element.15), channel_id=1, source_target_pairs={{0,24},{8,16},{16,8},{24,0},{1,25},{9,17},{17,9},{25,1},{2,26},{10... | collective-permute-start | bytes 1474568 | tf_op jit(solution)/shard_map/ppermute | solution.py:396
  78.2 22.5 %collective-permute-start.10 = (bf16[20,48,256]{2,1,0:T(8,128)(2,1)}, bf16[20,48,256]{2,1,0:T(8,128)(2,1)S(1)}, u32[]{:S(2)}, u32[]{:S(2)}) collective-permute-start(bf16[20,48,256]{2,1,0:T(8,128)(2,1)} %get-tuple-element.16), channel_id=1, source_target_pairs={{0,16},{8,24},{16,0},{24,8},{1,17},{9,25},{17,1},{25,9},{2,18},{10... | collective-permute-start | bytes 1474568 | tf_op jit(solution)/shard_map/ppermute | solution.py:396
  90.2 10.5 %copy-start.1 = (bf16[20,192,256]{2,1,0:T(8,128)(2,1)}, bf16[20,192,256]{2,1,0:T(8,128)(2,1)S(1)}, u32[]{:S(2)}) copy-start(bf16[20,192,256]{2,1,0:T(8,128)(2,1)S(1)} %constant_dynamic-update-slice_fusion) | copy-start | bytes 5898244

commit v2 on v1

--- a/solution.py
+++ b/solution.py
@@ -7,12 +7,19 @@
 from jax.experimental.pallas import tpu as pltpu
 from jax.sharding import PartitionSpec as P
 
+
 RADIUS = 48
 SWEEPS = 5
 LANES = 128
 F32 = jnp.float32
 BF16 = jnp.bfloat16
 VMEM_BYTES = 56 * 1024 * 1024
+CHUNKS = 2
+GROUP = 12
+
+
+def group_of(blocks):
+    return max(u for u in range(1, GROUP + 1) if blocks % u == 0)
 
 
 def vmem():
@@ -27,14 +34,14 @@
     return pltpu.CompilerParams(vmem_limit_bytes=VMEM_BYTES)
 
 
-def gram_kernel(mem_ref, *refs, groups, share, blocks, width, unroll):
+def gram_kernel(mem_ref, *refs, groups, share, blocks, width, unroll, first):
     parts = refs[:groups]
     scale_ref, weight_ref, own_ref, send_ref, rows_ref = refs[groups:]
     members = groups * share
     half = members // 2
     tiles = width // LANES
     mem = mem_ref[0]
-    scale = scale_ref[...]
+    scale = scale_ref[first : first + blocks, :]
     for d in range(groups):
         base = (mem ^ d) * (share * blocks)
 
@@ -58,7 +65,7 @@
             spread = jnp.concatenate(
                 [rows_ref[t, pl.ds(b, members, stride=blocks), :] for t in range(tiles)], axis=1
             )
-            weights = jnp.broadcast_to(weight_ref[pl.ds(b, 1), :], (spare, width))
+            weights = jnp.broadcast_to(weight_ref[pl.ds(first + b, 1), :], (spare, width))
             right = jnp.concatenate([spread, spread[half:], weights], axis=0).astype(BF16)
             product = lax.dot_general(
                 spread.astype(BF16), right, (((1,), (1,)), ((), ())), preferred_element_type=F32
@@ -84,7 +91,7 @@
     lax.fori_loop(0, blocks // 2, finish, 0, unroll=2)
 
 
-def packed_grams(mem, parts, scale, weighted):
+def packed_grams(mem, parts, scale, weighted, first):
     groups = len(parts)
     share, blocks, width = parts[0].shape
     members = groups * share
@@ -93,7 +100,13 @@
     flat = (blocks * half, LANES)
     return pl.pallas_call(
         functools.partial(
-            gram_kernel, groups=groups, share=share, blocks=blocks, width=width, unroll=4
+            gram_kernel,
+            groups=groups,
+            share=share,
+            blocks=blocks,
+            width=width,
+            unroll=group_of(blocks),
+            first=first,
         ),
         out_shape=(jax.ShapeDtypeStruct(flat, F32), jax.ShapeDtypeStruct(flat, BF16)),
         in_specs=[smem()] + [vmem()] * (groups + 2),
@@ -110,15 +123,15 @@
 
 
 def blend_kernel(
-    row_ref, taper_ref, left_ref, own_ref, right_ref, blend_ref, window_ref, *, members, neighbours, blocks, unroll
+    row_ref, taper_ref, *refs, members, neighbours, blocks, unroll, first
 ):
+    *pieces, blend_ref, window_ref = refs
     half = members // 2
     pull_lane = members + half
-    halo = left_ref.shape[0]
-    count = own_ref.shape[0]
-    window_ref[pl.ds(0, halo), :] = left_ref[...].astype(F32)
-    window_ref[pl.ds(halo, count), :] = own_ref[...]
-    window_ref[pl.ds(halo + count, halo), :] = right_ref[...].astype(F32)
+    filled = 0
+    for piece in pieces:
+        window_ref[pl.ds(filled, piece.shape[0]), :] = piece[...].astype(F32)
+        filled += piece.shape[0]
     full = (members, LANES)
     lane = lax.broadcasted_iota(jnp.int32, full, 1)
     row = lax.broadcasted_iota(jnp.int32, full, 0)
@@ -140,8 +153,8 @@
     def localized_sum(b):
         packed = None
         for n in range(neighbours):
-            start = pl.multiple_of(row_ref[b * neighbours + n], 8)
-            term = taper_ref[b * neighbours + n] * window_ref[pl.ds(start, half), :]
+            start = pl.multiple_of(row_ref[first + b, n], 8)
+            term = taper_ref[first + b, n] * window_ref[pl.ds(start, half), :]
             packed = term if packed is None else packed + term
         turned = jnp.concatenate([packed, pad_rows], axis=0).T
         low_rows = jnp.where(
@@ -216,26 +229,30 @@
     lax.fori_loop(0, blocks // unroll, block_group, 0)
 
 
-def blends(rows, tapers, left, own, right, members):
-    blocks, neighbours = rows.shape
+def blends(rows, tapers, window, members, first, blocks):
+    neighbours = rows.shape[1]
+    window_rows = sum(piece.shape[0] for piece in window)
     return pl.pallas_call(
         functools.partial(
-            blend_kernel, members=members, neighbours=neighbours, blocks=blocks, unroll=12
+            blend_kernel,
+            members=members,
+            neighbours=neighbours,
+            blocks=blocks,
+            unroll=group_of(blocks),
+            first=first,
         ),
         out_shape=jax.ShapeDtypeStruct((blocks * members, LANES), BF16),
-        in_specs=[smem(), smem(), vmem(), vmem(), vmem()],
+        in_specs=[smem(), smem()] + [vmem()] * len(window),
         out_specs=vmem(),
-        scratch_shapes=[
-            pltpu.VMEM((left.shape[0] + own.shape[0] + right.shape[0], LANES), F32)
-        ],
+        scratch_shapes=[pltpu.VMEM((window_rows, LANES), F32)],
         compiler_params=params(),
         cost_estimate=pl.CostEstimate(
             flops=blocks * 24 * members * members * LANES,
-            bytes_accessed=4 * own.shape[0] * LANES * 4,
+            bytes_accessed=3 * window_rows * LANES,
             transcendentals=0,
         ),
         name="blends",
-    )(rows.reshape(-1), tapers.reshape(-1), left, own, right)
+    )(rows, tapers, *window)
 
 
 def apply_kernel(mem_ref, *refs, groups, share, blocks, width, unroll):
@@ -305,7 +322,7 @@
     part = jax.ShapeDtypeStruct((share, blocks, width), BF16)
     return pl.pallas_call(
         functools.partial(
-            apply_kernel, groups=groups, share=share, blocks=blocks, width=width, unroll=4
+            apply_kernel, groups=groups, share=share, blocks=blocks, width=width, unroll=group_of(blocks)
         ),
         out_shape=(part,) * groups,
         in_specs=[smem()] + [vmem()] * (groups + 1),
@@ -360,16 +377,28 @@
     forward = [(holder(g), holder(g + 1)) for g in ring]
     backward = [(holder(g), holder(g - 1)) for g in ring]
 
-    def piece(x, d):
-        return lax.dynamic_slice_in_dim(x, ((mem ^ d) ^ flip) * blocks, blocks, 1)
-
-    def gathered(x):
-        parts = {d: lax.ppermute(piece(x, d), "mem", peers[d]) for d in far_first}
-        parts[0] = piece(x, 0)
-        return [parts[d] for d in range(groups)]
+    size = blocks // CHUNKS
+    chunks = range(CHUNKS)
+    last = None
+
+    def piece(x, d, c):
+        nonlocal last
+        if last is not None:
+            x, _ = lax.optimization_barrier((x, last))
+        start = ((mem ^ d) ^ flip) * blocks + c * size
+        last = lax.dynamic_slice_in_dim(x, start, size, 1)
+        return last
 
     def own_rows(x):
         return lax.dynamic_slice_in_dim(x, mine * blocks, blocks, 0)
+
+    def exchanged(x, c):
+        parts = {d: lax.ppermute(piece(x, d, c), "mem", peers[d]) for d in far_first}
+        parts[0] = piece(x, 0, c)
+        return [parts[d] for d in range(groups)]
+
+    spread_parts = [exchanged(scaled_sensor_spread, c) for c in chunks]
+    field_parts = [exchanged(prior_fields, c) for c in chunks]
 
     mem_scalar = mem.astype(jnp.int32).reshape(1)
     slot_ids = jnp.arange(width, dtype=jnp.int32)
@@ -380,21 +409,30 @@
     block_ids = lon * lon_rows + mine * blocks + local_ids
     offset_raw = jnp.mod(own_rows(adjacent_tiles) - block_ids[:, None], total_blocks)
     offset = jnp.where(offset_raw > total_blocks // 2, offset_raw - total_blocks, offset_raw)
-    window_rows = (local_ids[:, None] + RADIUS + offset) * half
+    window_rows = (local_ids[:, None] % size + RADIUS + offset) * half
     tapers = taper_of(offset)
 
-    spread_parts = gathered(scaled_sensor_spread)
-    field_parts = gathered(prior_fields)
-    own, send = packed_grams(mem_scalar, spread_parts, obs_scale, weighted)
-    left = lax.ppermute(send, ("mem", "lon"), forward)
-    right = lax.ppermute(send, ("mem", "lon"), backward)
-    blend = blends(window_rows, tapers, left, own, right, members)
-    out_parts = apply_blend(mem_scalar, field_parts, blend)
+    left, own, right = [], [], []
+    for c in chunks:
+        here, packed = packed_grams(
+            mem_scalar, spread_parts[c], obs_scale, weighted, c * size
+        )
+        own.append(here)
+        left.append(lax.ppermute(packed, ("mem", "lon"), forward))
+        right.append(lax.ppermute(packed, ("mem", "lon"), backward))
+    window = left + own + right
+
+    came = []
+    for c in chunks:
+        blend = blends(window_rows, tapers, window[c : c + 2 * CHUNKS + 1], members, c * size, size)
+        out_parts = apply_blend(mem_scalar, field_parts[c], blend)
+        came.append((0, c, out_parts[0]))
+        for d in far_first:
+            came.append((d, c, lax.ppermute(out_parts[d], "mem", peers[d])))
     result = jnp.zeros(prior_fields.shape, BF16)
-    result = lax.dynamic_update_slice_in_dim(result, out_parts[0], mine * blocks, 1)
-    for d in reversed(far_first):
-        came = lax.ppermute(out_parts[d], "mem", peers[d])
-        result = lax.dynamic_update_slice_in_dim(result, came, ((mem ^ d) ^ flip) * blocks, 1)
+    for d, c, part in sorted(came, key=lambda item: (item[1], item[0] > 0, item[0] >= groups // 2)):
+        start = ((mem ^ d) ^ flip) * blocks + c * size
+        result = lax.dynamic_update_slice_in_dim(result, part, start, 1)
     return result
 
 

time: 102 us -> 98.2 us (0.963)
  waiting for transfers between devices: 45.2 us -> 32.2 us
  local copies, waits for them, and re-layouts: 8.35 us -> 16.1 us
  Pallas kernels: 26.2 us -> 28.9 us
  starting transfers between devices: 19.9 us -> 17.2 us
  other arithmetic: 1.73 us -> 2.96 us
    ppermute x11 -> x22, waiting for transfers between devices: 45.2 us -> 32.2 us  [the longest x6 15.5 us: on_device(): came.append((d, c, lax.ppermute(out_parts[d], 'mem', peers[d])))]
    dynamic_slice x2 -> x16, local copies, waits for them, and re-layouts: 3.7 us -> 11.1 us  [piece(): last = lax.dynamic_slice_in_dim(x, start, size, 1)]
    ppermute x11 -> x22, starting transfers between devices: 19.9 us -> 17.2 us  [the longest x12 7.6 us: exchanged(): lax.ppermute(piece(x, d, c), 'mem', peers[d])]
    pallas_call x1 -> x2, Pallas kernels: 12 us -> 14.5 us  [blends(): pl.pallas_call(functools.partial(blend_kernel, members=members, neighbour...]
    unnamed x20 -> x33, local copies, waits for them, and re-layouts: 1.92 us -> 3.79 us
    reshape x2 -> x0, local copies, waits for them, and re-layouts: 1.35 us -> none  [the longest x1 0.68 us: blends(): tapers.reshape(-1)]
    pallas_call x1 -> x2, Pallas kernels: 6.49 us -> 6.83 us  [packed_grams(): pl.pallas_call(functools.partial(gram_kernel, groups=groups, share=share,...]
    pallas_call x1 -> x2, Pallas kernels: 7.68 us -> 7.62 us  [apply_blend(): pl.pallas_call(functools.partial(apply_kernel, groups=groups, share=share...]
  transfers between devices with their start and end apart: 11 -> 22, of which waited for: 5 -> 5; matrix products, arithmetic and copies ran while one was open for 5% -> 15% of each run, Pallas kernels for 18% -> 30%
where the time goes in v2:
time: 98.2 us; the launch traced here: 97.7 us
  waiting for transfers between devices  32.2 us (33%)
  Pallas kernels  28.9 us (29%)
  starting transfers between devices  17.2 us (18%)
  local copies, waits for them, and re-layouts  16.1 us (16%)
  other arithmetic  2.96 us (3%)
    ppermute x6, waiting for transfers between devices, on_device(): came.append((d, c, lax.ppermute(out_parts[d], 'mem', peers[d])))  15.5 us
    pallas_call x2, Pallas kernels, blends(): pl.pallas_call(functools.partial(blend_kernel, members=members, neighbour...  14.5 us
    dynamic_slice x16, local copies, waits for them, and re-layouts, piece(): last = lax.dynamic_slice_in_dim(x, start, size, 1)  11.1 us
    ppermute x12, waiting for transfers between devices, exchanged(): lax.ppermute(piece(x, d, c), 'mem', peers[d])  8.42 us
    ppermute x2, waiting for transfers between devices, on_device(): left.append(lax.ppermute(packed, ('mem', 'lon'), forward))  8.23 us
    pallas_call x2, Pallas kernels, apply_blend(): pl.pallas_call(functools.partial(apply_kernel, groups=groups, share=share...  7.62 us
    ppermute x12, starting transfers between devices, exchanged(): lax.ppermute(piece(x, d, c), 'mem', peers[d])  7.6 us
    pallas_call x2, Pallas kernels, packed_grams(): pl.pallas_call(functools.partial(gram_kernel, groups=groups, share=share,...  6.83 us
  transfers between devices with their start and end apart: 22, of which 5 were waited for; matrix products, arithmetic and copies ran while one was open for 15% of the time, Pallas kernels for 30%

profile of v2, /device:TPU:0, one launch (start us, length us, event | category | flops | bytes accessed | tf_op | source)
XLA Modules:
  0.0 97.7 jit_solution(7687202936017896927)
XLA Ops:
  0.0 1.5 %copy-done = bf16[20,192,256]{2,1,0:T(8,128)(2,1)S(1)} copy-done((bf16[20,192,256]{2,1,0:T(8,128)(2,1)S(1)}, bf16[20,192,256]{2,1,0:T(8,128)(2,1)}, u32[]{:S(2)}) %copy-start) | copy-done | bytes 1966104
  1.6 2.5 %collective-permute-start.5 = (bf16[20,24,256]{2,1,0:T(8,128)(2,1)S(1)}, bf16[20,24,256]{2,1,0:T(8,128)(2,1)}, u32[]{:S(2)}, u32[]{:S(2)}) collective-permute-start(bf16[20,24,256]{2,1,0:T(8,128)(2,1)S(1)} %constant_dynamic-slice_fusion.15), channel_id=1, source_target_pairs={{0,24},{8,16},{16,8},{24,0},{1,25},{9,17},{17,9},{25,1},{2,26},{10... | collective-permute-start | bytes 737288 | tf_op jit(solution)/shard_map/ppermute | solution.py:396
  4.1 0.7 constant_dynamic-slice_fusion.14
  4.8 0.7 collective-permute-start.3
  5.5 0.7 constant_dynamic-slice_fusion.13.refs_0_
  6.2 0.7 constant_dynamic-slice_fusion.12
  6.9 0.0 collective-permute-start.8
  6.9 0.7 constant_dynamic-slice_fusion.11
  7.6 1.4 %collective-permute-start.9 = (bf16[20,24,256]{2,1,0:T(8,128)(2,1)}, bf16[20,24,256]{2,1,0:T(8,128)(2,1)}, u32[]{:S(2)}, u32[]{:S(2)}) collective-permute-start(bf16[20,24,256]{2,1,0:T(8,128)(2,1)} %constant_dynamic-slice_fusion.11), channel_id=1, source_target_pairs={{0,24},{8,16},{16,8},{24,0},{1,25},{9,17},{17,9},{25,1},{2,26},{10... | collective-permute-start | bytes 737288 | tf_op jit(solution)/shard_map/ppermute | solution.py:396
  9.0 0.7 constant_dynamic-slice_fusion.10
  9.7 0.8 collective-permute-start.7
  10.5 0.7 constant_dynamic-slice_fusion.9.refs_0_
  11.2 1.0 constant_dynamic-slice_fusion.8
  12.2 1.7 %constant_dynamic-slice_fusion.7 = bf16[20,24,256]{2,1,0:T(8,128)(2,1)} fusion(bf16[20,192,256]{2,1,0:T(8,128)(2,1)} %param.6, s32[]{:T(128)S(6)} %select_n.74), kind=kLoop, calls=%fused_computation.23 | loop fusion | bytes 491524 | tf_op jit(solution)/shard_map/dynamic_slice | solution.py:389
  13.9 1.6 %constant_dynamic-slice_fusion.6 = bf16[20,24,256]{2,1,0:T(8,128)(2,1)} fusion(bf16[20,192,256]{2,1,0:T(8,128)(2,1)} %param.6, s32[]{:T(128)S(6)} %select_n.75), kind=kLoop, calls=%fused_computation.22 | loop fusion | bytes 491524 | tf_op jit(solution)/shard_map/dynamic_slice | solution.py:389
  15.5 0.7 constant_dynamic-slice_fusion.5.refs_0_
  16.3 0.0 collective-permute-done.3.refs_1_
  16.3 0.1 collective-permute-start.4
  16.4 0.1 constant_dynamic-slice_fusion.4
  16.5 0.1 dynamic_slice.73
  16.6 1.6 %dynamic-slice_multiply_fusion = (f32[48,256]{1,0:T(8,128)}, f32[48,256]{1,0:T(8,128)}) fusion(f32[192,256]{1,0:T(8,128)} %param.8, s32[]{:T(128)S(6)} %select_n.76, f32[192,256]{1,0:T(8,128)} %param.9, s32[48]{0:T(128)S(1)} %dynamic_slice.73), kind=kLoop, calls=%fused_computation.1 | loop fusion | flops 36864 | bytes 196804 | tf_op jit(solution)/shard_map/mul | solution.py:407
  18.1 0.1 collective-permute-start
  18.2 8.3 %collective-permute-done.4.refs_2_ = bf16[20,24,256]{2,1,0:T(8,128)(2,1)} collective-permute-done((bf16[20,24,256]{2,1,0:T(8,128)(2,1)S(1)}, bf16[20,24,256]{2,1,0:T(8,128)(2,1)}, u32[]{:S(2)}, u32[]{:S(2)}) %collective-permute-start.4) | collective-permute-done | bytes 245792 | tf_op jit(solution)/shard_map/ppermute | solution.py:396
  26.5 2.0 %collective-permute-start.2 = (bf16[20,24,256]{2,1,0:T(8,128)(2,1)}, bf16[20,24,256]{2,1,0:T(8,128)(2,1)}, u32[]{:S(2)}, u32[]{:S(2)}) collective-permute-start(bf16[20,24,256]{2,1,0:T(8,128)(2,1)} %constant_dynamic-slice_fusion.7), channel_id=1, source_target_pairs={{0,24},{8,16},{16,8},{24,0},{1,25},{9,17},{17,9},{25,1},{2,26},{10... | collective-permute-start | bytes 737288 | tf_op jit(solution)/shard_map/ppermute | solution.py:396
  28.5 3.4 %packed_grams.2 = (f32[960,128]{1,0:T(8,128)}, bf16[960,128]{1,0:T(8,128)(2,1)}) custom-call(s32[1]{0:T(128)} %bitcast.mem_ref, bf16[20,24,256]{2,1,0:T(8,128)(2,1)} %constant_dynamic-slice_fusion.13.refs_0_, bf16[20,24,256]{2,1,0:T(8,128)(2,1)} %collective-permute-done.3.refs_1_, bf16[20,24,256]{2,1,0:T(8,128)(2,1)} %collective-permute-done.4.refs_2_, ...), custom_call_target="tpu_custom_call" | custom-call | flops 125829120 | bytes 983040 | tf_op jit(solution)/shard_map/packed_grams/pallas_call | solution.py:101
  31.9 0.0 collective-permute-done.7.refs_1_
  31.9 4.6 %collective-permute-start.11 = (bf16[960,128]{1,0:T(8,128)(2,1)}, bf16[960,128]{1,0:T(8,128)(2,1)S(1)}, u32[]{:S(2)}, u32[]{:S(2)}) collective-permute-start(bf16[960,128]{1,0:T(8,128)(2,1)} %get-tuple-element.43), channel_id=1, source_target_pairs={{0,7},{8,0},{16,8},{24,16},{25,24},{17,25},{9,17},{1,9},{2,1},{10,... | collective-permute-start | bytes 737288 | tf_op jit(solution)/shard_map/ppermute | solution.py:422
  36.5 0.0 collective-permute-done.9.refs_3_
  36.5 0.0 collective-permute-start.6
  36.5 0.0 collective-permute-done.8.refs_2_
  36.5 3.4 %packed_grams.3 = (f32[960,128]{1,0:T(8,128)}, bf16[960,128]{1,0:T(8,128)(2,1)}) custom-call(s32[1]{0:T(128)} %bitcast.mem_ref, bf16[20,24,256]{2,1,0:T(8,128)(2,1)} %constant_dynamic-slice_fusion.9.refs_0_, bf16[20,24,256]{2,1,0:T(8,128)(2,1)} %collective-permute-done.7.refs_1_, bf16[20,24,256]{2,1,0:T(8,128)(2,1)} %collective-permute-done.8.refs_2_, ...), custom_call_target="tpu_custom_call" | custom-call | flops 125829120 | bytes 983040 | tf_op jit(solution)/shard_map/packed_grams/pallas_call | solution.py:101
  39.9 0.1 copy.8
  40.0 0.7 add_multiply_fusion.row_ref
  40.7 0.1 collective-permute-start.16
  40.8 8.2 %collective-permute-done.10.refs_1_.refs_0_ = bf16[960,128]{1,0:T(8,128)(2,1)S(1)} collective-permute-done((bf16[960,128]{1,0:T(8,128)(2,1)}, bf16[960,128]{1,0:T(8,128)(2,1)S(1)}, u32[]{:S(2)}, u32[]{:S(2)}) %collective-permute-start.10) | collective-permute-done | bytes 245792 | tf_op jit(solution)/shard_map/ppermute | solution.py:421
  49.0 0.1 collective-permute-start.15
  49.1 0.1 collective-permute-start.18
  49.2 0.7 add_divide_fusion.taper_ref
  49.9 7.2 %blends.2.refs_4_ = bf16[1920,128]{1,0:T(8,128)(2,1)} custom-call(s32[48,16]{1,0:T(8,128)} %add_multiply_fusion.row_ref, f32[48,16]{1,0:T(8,128)} %add_divide_fusion.taper_ref, bf16[960,128]{1,0:T(8,128)(2,1)} %collective-permute-done.6.refs_0_, bf16[960,128]{1,0:T(8,128)(2,1)} %copy-done.4, f32[960,128]{1,0:T(8,128)} %get-tuple-element.45.refs_2_.refs_1_, ...), custom_call_target="tpu_custom_call" | custom-call | flops 471859200 | bytes 1843200 | tf_op jit(solution)/shard_map/blends/pallas_call | solution.py:235
  57.2 0.1 collective-permute-done.1.refs_2_
  57.3 0.7 copy-done.11
  58.0 3.8 %apply_blend.2 = (bf16[20,24,256]{2,1,0:T(8,128)(2,1)}, bf16[20,24,256]{2,1,0:T(8,128)(2,1)}, bf16[20,24,256]{2,1,0:T(8,128)(2,1)}, bf16[20,24,256]{2,1,0:T(8,128)(2,1)}) custom-call(s32[1]{0:T(128)} %bitcast.mem_ref, bf16[20,24,256]{2,1,0:T(8,128)(2,1)} %constant_dynamic-slice_fusion.5.refs_0_, bf16[20,24,256]{2,1,0:T(8,128)(2,1)} %collective-permute-done.refs_1_, ...), custom_call_target="tpu_custom_call" | custom-call | flops 125829120 | bytes 1966080 | tf_op jit(solution)/shard_map/apply_blend/pallas_call | solution.py:323
  61.8 0.4 collective-permute-start.12
  62.2 1.6 %constant_dynamic-slice_fusion.refs_0_ = bf16[20,24,256]{2,1,0:T(8,128)(2,1)} fusion(bf16[20,192,256]{2,1,0:T(8,128)(2,1)} %param.6, s32[]{:T(128)S(6)} %select_n.80), kind=kLoop, calls=%fused_computation.12 | loop fusion | bytes 491524 | tf_op jit(solution)/shard_map/dynamic_slice | solution.py:389
  63.8 0.0 collective-permute-done.18.refs_4_
  63.8 2.0 %collective-permute-start.13 = (bf16[20,24,256]{2,1,0:T(8,128)(2,1)}, bf16[20,24,256]{2,1,0:T(8,128)(2,1)S(1)}, u32[]{:S(2)}, u32[]{:S(2)}) collective-permute-start(bf16[20,24,256]{2,1,0:T(8,128)(2,1)} %get-tuple-element.49), channel_id=1, source_target_pairs={{0,16},{8,24},{16,0},{24,8},{1,17},{9,25},{17,1},{25,9},{2,18},{10... | collective-permute-start | bytes 737288 | tf_op jit(solution)/shard_map/ppermute | solution.py:431
  65.8 7.2 %blends.3.refs_4_ = bf16[1920,128]{1,0:T(8,128)(2,1)} custom-call(s32[48,16]{1,0:T(8,128)} %add_multiply_fusion.row_ref, f32[48,16]{1,0:T(8,128)} %add_divide_fusion.taper_ref, bf16[960,128]{1,0:T(8,128)(2,1)} %copy-done.4, f32[960,128]{1,0:T(8,128)} %get-tuple-element.45.refs_2_.refs_1_, f32[960,128]{1,0:T(8,128)} %get-tuple-element.46.refs_3_.refs_2_, ...), custom_call_target="tpu_custom_call" | custom-call | flops 471859200 | bytes 1843200 | tf_op jit(solution)/shard_map/blends/pallas_call | solution.py:235
  73.1 0.0 collective-permute-done.15.refs_1_
  73.1 0.0 collective-permute-done.16.refs_2_
  73.1 0.7 copy-done.9
  73.8 0.1 copy-done.7
  73.9 0.7 copy-done.8
  74.6 3.8 %apply_blend.3 = (bf16[20,24,256]{2,1,0:T(8,128)(2,1)}, bf16[20,24,256]{2,1,0:T(8,128)(2,1)}, bf16[20,24,256]{2,1,0:T(8,128)(2,1)}, bf16[20,24,256]{2,1,0:T(8,128)(2,1)}) custom-call(s32[1]{0:T(128)} %bitcast.mem_ref, bf16[20,24,256]{2,1,0:T(8,128)(2,1)} %constant_dynamic-slice_fusion.refs_0_, bf16[20,24,256]{2,1,0:T(8,128)(2,1)} %copy-done.9, ...), custom_call_target="tpu_custom_call" | custom-call | flops 125829120 | bytes 1966080 | tf_op jit(solution)/shard_map/apply_blend/pallas_call | solution.py:323
  78.4 0.0 collective-permute-start.19
  78.4 0.7 collective-permute-start.20
  79.1 1.1 %collective-permute-start.14 = (bf16[20,24,256]{2,1,0:T(8,128)(2,1)S(1)}, bf16[20,24,256]{2,1,0:T(8,128)(2,1)S(1)}, u32[]{:S(2)}, u32[]{:S(2)}) collective-permute-start(bf16[20,24,256]{2,1,0:T(8,128)(2,1)S(1)} %copy-done.13), channel_id=1, source_target_pairs={{0,24},{8,16},{16,8},{24,0},{1,25},{9,17},{17,9},{25,1},{2,26},{10... | collective-permute-start | bytes 737288 | tf_op jit(solution)/shard_map/ppermute | solution.py:431
  80.2 0.2 broadcast_in_dim.2
  80.5 0.7 collective-permute-start.21
  81.2 0.0 collective-permute-done.13
  81.2 10.4 %collective-permute-done.14 = bf16[20,24,256]{2,1,0:T(8,128)(2,1)S(1)} collective-permute-done((bf16[20,24,256]{2,1,0:T(8,128)(2,1)S(1)}, bf16[20,24,256]{2,1,0:T(8,128)(2,1)S(1)}, u32[]{:S(2)}, u32[]{:S(2)}) %collective-permute-start.14) | collective-permute-done | bytes 245792 | tf_op jit(solution)/shard_map/ppermute | solution.py:431
  91.8 0.0 collective-permute-done.20
  91.8 0.0 copy-start.2
  91.8 5.1 %collective-permute-done.21 = bf16[20,24,256]{2,1,0:T(8,128)(2,1)S(1)} collective-permute-done((bf16[20,24,256]{2,1,0:T(8,128)(2,1)S(1)}, bf16[20,24,256]{2,1,0:T(8,128)(2,1)S(1)}, u32[]{:S(2)}, u32[]{:S(2)}) %collective-permute-start.21) | collective-permute-done | bytes 245792 | tf_op jit(solution)/shard_map/ppermute | solution.py:431
  97.0 0.7 constant_dynamic-update-slice_fusion
  (50 shorter events, 0.4 us)
Async XLA Ops:
  0.0 1.5 %copy-start = (bf16[20,192,256]{2,1,0:T(8,128)(2,1)S(1)}, bf16[20,192,256]{2,1,0:T(8,128)(2,1)}, u32[]{:S(2)}) copy-start(bf16[20,192,256]{2,1,0:T(8,128)(2,1)} %param.7) | copy-start | bytes 5898244
  1.6 16.5 %collective-permute-start.5 = (bf16[20,24,256]{2,1,0:T(8,128)(2,1)S(1)}, bf16[20,24,256]{2,1,0:T(8,128)(2,1)}, u32[]{:S(2)}, u32[]{:S(2)}) collective-permute-start(bf16[20,24,256]{2,1,0:T(8,128)(2,1)S(1)} %constant_dynamic-slice_fusion.15), channel_id=1, source_target_pairs={{0,24},{8,16},{16,8},{24,0},{1,25},{9,17},{17,9},{25,1},{2,26},{10... | collective-permute-start | bytes 737288 | tf_op jit(solution)/shard_map/ppermute | solution.py:396
  4.8 11.5 %collective-permute-start.3 = (bf16[20,24,256]{2,1,0:T(8,128)(2,1)}, bf16[20,24,256]{2,1,0:T(8,128)(2,1)}, u32[]{:S(2)}, u32[]{:S(2)}) collective-permute-start(bf16[20,24,256]{2,1,0:T(8,128)(2,1)} %constant_dynamic-slice_fusion.14), channel_id=1, source_target_pairs={{0,8},{8,0},{16,24},{24,16},{1,9},{9,1},{17,25},{25,17},{2,10},{10... | collective-permute-start | bytes 737288 | tf_op jit(solution)/shard_map/ppermute | solution.py:396
  6.9 29.6 %collective-permute-start.8 = (bf16[20,24,256]{2,1,0:T(8,128)(2,1)}, bf16[20,24,256]{2,1,0:T(8,128)(2,1)}, u32[]{:S(2)}, u32[]{:S(2)}) collective-permute-start(bf16[20,24,256]{2,1,0:T(8,128)(2,1)} %constant_dynamic-slice_fusion.12), channel_id=1, source_target_pairs={{0,16},{8,24},{16,0},{24,8},{1,17},{9,25},{17,1},{25,9},{2,18},{10... | collective-permute-start | bytes 737288 | tf_op jit(solution)/shard_map/ppermute | solution.py:396
  7.6 28.9 %collective-permute-start.9 = (bf16[20,24,256]{2,1,0:T(8,128)(2,1)}, bf16[20,24,256]{2,1,0:T(8,128)(2,1)}, u32[]{:S(2)}, u32[]{:S(2)}) collective-permute-start(bf16[20,24,256]{2,1,0:T(8,128)(2,1)} %constant_dynamic-slice_fusion.11), channel_id=1, source_target_pairs={{0,24},{8,16},{16,8},{24,0},{1,25},{9,17},{17,9},{25,1},{2,26},{10... | collective-permute-start | bytes 737288 | tf_op jit(solution)/shard_map/ppermute | solution.py:396
  9.7 22.2 %collective-permute-start.7 = (bf16[20,24,256]{2,1,0:T(8,128)(2,1)}, bf16[20,24,256]{2,1,0:T(8,128)(2,1)}, u32[]{:S(2)}, u32[]{:S(2)}) collective-permute-start(bf16[20,24,256]{2,1,0:T(8,128)(2,1)} %constant_dynamic-slice_fusion.10), channel_id=1, source_target_pairs={{0,8},{8,0},{16,24},{24,16},{1,9},{9,1},{17,25},{25,17},{2,10},{10... | collective-permute-start | bytes 737288 | tf_op jit(solution)/shard_map/ppermute | solution.py:396
  10.5 5.0 %copy-start.1 = (bf16[20,192,256]{2,1,0:T(8,128)(2,1)S(1)}, bf16[20,192,256]{2,1,0:T(8,128)(2,1)}, u32[]{:S(2)}) copy-start(bf16[20,192,256]{2,1,0:T(8,128)(2,1)} %param.6) | copy-start | bytes 5898244
  10.5 5.9 %copy-start.12 = (s32[192,16]{0,1:T(8,128)S(1)}, s32[192,16]{0,1:T(8,128)}, u32[]{:S(2)}) copy-start(s32[192,16]{0,1:T(8,128)} %param.11) | copy-start | bytes 36868
  10.5 6.0 %copy-start.15 = (s32[192]{0:T(256)S(1)}, s32[192]{0:T(256)}, u32[]{:S(2)}) copy-start(s32[192]{0:T(256)} %param.10) | copy-start | bytes 2308
  16.3 10.2 %collective-permute-start.4 = (bf16[20,24,256]{2,1,0:T(8,128)(2,1)S(1)}, bf16[20,24,256]{2,1,0:T(8,128)(2,1)}, u32[]{:S(2)}, u32[]{:S(2)}) collective-permute-start(bf16[20,24,256]{2,1,0:T(8,128)(2,1)S(1)} %constant_dynamic-slice_fusion.16), channel_id=1, source_target_pairs={{0,16},{8,24},{16,0},{24,8},{1,17},{9,25},{17,1},{25,9},{2,18},{10... | collective-permute-start | bytes 737288 | tf_op jit(solution)/shard_map/ppermute | solution.py:396
  18.1 22.6 %collective-permute-start = (bf16[20,24,256]{2,1,0:T(8,128)(2,1)}, bf16[20,24,256]{2,1,0:T(8,128)(2,1)}, u32[]{:S(2)}, u32[]{:S(2)}) collective-permute-start(bf16[20,24,256]{2,1,0:T(8,128)(2,1)} %constant_dynamic-slice_fusion.6), channel_id=1, source_target_pairs={{0,8},{8,0},{16,24},{24,16},{1,9},{9,1},{17,25},{25,17},{2,10},{10... | collective-permute-start | bytes 737288 | tf_op jit(solution)/shard_map/ppermute | solution.py:396
  26.5 14.2 %collective-permute-start.2 = (bf16[20,24,256]{2,1,0:T(8,128)(2,1)}, bf16[20,24,256]{2,1,0:T(8,128)(2,1)}, u32[]{:S(2)}, u32[]{:S(2)}) collective-permute-start(bf16[20,24,256]{2,1,0:T(8,128)(2,1)} %constant_dynamic-slice_fusion.7), channel_id=1, source_target_pairs={{0,24},{8,16},{16,8},{24,0},{1,25},{9,17},{17,9},{25,1},{2,26},{10... | collective-permute-start | bytes 737288 | tf_op jit(solution)/shard_map/ppermute | solution.py:396
  31.9 17.1 %collective-permute-start.11 = (bf16[960,128]{1,0:T(8,128)(2,1)}, bf16[960,128]{1,0:T(8,128)(2,1)S(1)}, u32[]{:S(2)}, u32[]{:S(2)}) collective-permute-start(bf16[960,128]{1,0:T(8,128)(2,1)} %get-tuple-element.43), channel_id=1, source_target_pairs={{0,7},{8,0},{16,8},{24,16},{25,24},{17,25},{9,17},{1,9},{2,1},{10,... | collective-permute-start | bytes 737288 | tf_op jit(solution)/shard_map/ppermute | solution.py:422
  36.5 12.6 %collective-permute-start.6 = (bf16[960,128]{1,0:T(8,128)(2,1)}, bf16[960,128]{1,0:T(8,128)(2,1)}, u32[]{:S(2)}, u32[]{:S(2)}) collective-permute-start(bf16[960,128]{1,0:T(8,128)(2,1)} %get-tuple-element.43), channel_id=1, source_target_pairs={{0,8},{8,16},{16,24},{24,25},{25,17},{17,9},{9,1},{1,2},{2,10},{10... | collective-permute-start | bytes 737288 | tf_op jit(solution)/shard_map/ppermute | solution.py:421
  39.9 9.1 %collective-permute-start.10 = (bf16[960,128]{1,0:T(8,128)(2,1)}, bf16[960,128]{1,0:T(8,128)(2,1)S(1)}, u32[]{:S(2)}, u32[]{:S(2)}) collective-permute-start(bf16[960,128]{1,0:T(8,128)(2,1)} %get-tuple-element.44), channel_id=1, source_target_pairs={{0,8},{8,16},{16,24},{24,25},{25,17},{17,9},{9,1},{1,2},{2,10},{10... | collective-permute-start | bytes 737288 | tf_op jit(solution)/shard_map/ppermute | solution.py:421
  40.7 32.4 %collective-permute-start.17 = (bf16[20,24,256]{2,1,0:T(8,128)(2,1)S(1)}, bf16[20,24,256]{2,1,0:T(8,128)(2,1)S(1)}, u32[]{:S(2)}, u32[]{:S(2)}) collective-permute-start(bf16[20,24,256]{2,1,0:T(8,128)(2,1)S(1)} %constant_dynamic-slice_fusion.2), channel_id=1, source_target_pairs={{0,24},{8,16},{16,8},{24,0},{1,25},{9,17},{17,9},{25,1},{2,26},{10... | collective-permute-start | bytes 737288 | tf_op jit(solution)/shard_map/ppermute | solution.py:396
  40.7 32.4 %collective-permute-start.16 = (bf16[20,24,256]{2,1,0:T(8,128)(2,1)S(1)}, bf16[20,24,256]{2,1,0:T(8,128)(2,1)S(1)}, u32[]{:S(2)}, u32[]{:S(2)}) collective-permute-start(bf16[20,24,256]{2,1,0:T(8,128)(2,1)S(1)} %constant_dynamic-slice_fusion.3), channel_id=1, source_target_pairs={{0,16},{8,24},{16,0},{24,8},{1,17},{9,25},{17,1},{25,9},{2,18},{10... | collective-permute-start | bytes 737288 | tf_op jit(solution)/shard_map/ppermute | solution.py:396
  49.0 0.9 copy-start.4
  49.0 8.2 %collective-permute-start.1 = (bf16[20,24,256]{2,1,0:T(8,128)(2,1)S(1)}, bf16[20,24,256]{2,1,0:T(8,128)(2,1)S(1)}, u32[]{:S(2)}, u32[]{:S(2)}) collective-permute-start(bf16[20,24,256]{2,1,0:T(8,128)(2,1)S(1)} %constant_dynamic-slice_fusion.8), channel_id=1, source_target_pairs={{0,16},{8,24},{16,0},{24,8},{1,17},{9,25},{17,1},{25,9},{2,18},{10... | collective-permute-start | bytes 737288 | tf_op jit(solution)/shard_map/ppermute | solution.py:396
  49.0 0.9 copy-start.3
  49.0 24.0 %collective-permute-start.15 = (bf16[20,24,256]{2,1,0:T(8,128)(2,1)S(1)}, bf16[20,24,256]{2,1,0:T(8,128)(2,1)S(1)}, u32[]{:S(2)}, u32[]{:S(2)}) collective-permute-start(bf16[20,24,256]{2,1,0:T(8,128)(2,1)S(1)} %constant_dynamic-slice_fusion.1), channel_id=1, source_target_pairs={{0,8},{8,0},{16,24},{24,16},{1,9},{9,1},{17,25},{25,17},{2,10},{10... | collective-permute-start | bytes 737288 | tf_op jit(solution)/shard_map/ppermute | solution.py:396
  49.1 14.7 %collective-permute-start.18 = (bf16[960,128]{1,0:T(8,128)(2,1)}, bf16[960,128]{1,0:T(8,128)(2,1)S(1)}, u32[]{:S(2)}, u32[]{:S(2)}) collective-permute-start(bf16[960,128]{1,0:T(8,128)(2,1)} %get-tuple-element.44), channel_id=1, source_target_pairs={{0,7},{8,0},{16,8},{24,16},{25,24},{17,25},{9,17},{1,9},{2,1},{10,... | collective-permute-start | bytes 737288 | tf_op jit(solution)/shard_map/ppermute | solution.py:422
  57.3 0.7 copy-start.11
  61.8 18.7 %collective-permute-start.12 = (bf16[20,24,256]{2,1,0:T(8,128)(2,1)}, bf16[20,24,256]{2,1,0:T(8,128)(2,1)S(1)}, u32[]{:S(2)}, u32[]{:S(2)}) collective-permute-start(bf16[20,24,256]{2,1,0:T(8,128)(2,1)} %get-tuple-element.48), channel_id=1, source_target_pairs={{0,8},{8,0},{16,24},{24,16},{1,9},{9,1},{17,25},{25,17},{2,10},{10... | collective-permute-start | bytes 737288 | tf_op jit(solution)/shard_map/ppermute | solution.py:431
  63.8 15.3 %copy-start.13 = (bf16[20,24,256]{2,1,0:T(8,128)(2,1)S(1)}, bf16[20,24,256]{2,1,0:T(8,128)(2,1)}, u32[]{:S(2)}) copy-start(bf16[20,24,256]{2,1,0:T(8,128)(2,1)} %get-tuple-element.50) | copy-start | bytes 737284
  63.8 2.0 %copy-start.10 = (bf16[960,128]{1,0:T(8,128)(2,1)}, bf16[960,128]{1,0:T(8,128)(2,1)S(1)}, u32[]{:S(2)}) copy-start(bf16[960,128]{1,0:T(8,128)(2,1)S(1)} %collective-permute-done.18.refs_4_) | copy-start | bytes 737284
  63.8 17.4 %collective-permute-start.13 = (bf16[20,24,256]{2,1,0:T(8,128)(2,1)}, bf16[20,24,256]{2,1,0:T(8,128)(2,1)S(1)}, u32[]{:S(2)}, u32[]{:S(2)}) collective-permute-start(bf16[20,24,256]{2,1,0:T(8,128)(2,1)} %get-tuple-element.49), channel_id=1, source_target_pairs={{0,16},{8,24},{16,0},{24,8},{1,17},{9,25},{17,1},{25,9},{2,18},{10... | collective-permute-start | bytes 737288 | tf_op jit(solution)/shard_map/ppermute | solution.py:431
  73.1 7.4 %copy-start.5 = (bf16[20,24,256]{2,1,0:T(8,128)(2,1)S(1)}, bf16[20,24,256]{2,1,0:T(8,128)(2,1)}, u32[]{:S(2)}) copy-start(bf16[20,24,256]{2,1,0:T(8,128)(2,1)} %get-tuple-element.47) | copy-start | bytes 737284
  73.1 0.7 copy-start.9
  73.1 0.8 copy-start.7
  73.9 0.7 copy-start.8
  78.4 2.1 %copy-start.14 = (bf16[20,24,256]{2,1,0:T(8,128)(2,1)S(1)}, bf16[20,24,256]{2,1,0:T(8,128)(2,1)}, u32[]{:S(2)}) copy-start(bf16[20,24,256]{2,1,0:T(8,128)(2,1)} %get-tuple-element.58) | copy-start | bytes 737284
  78.4 13.4 %collective-permute-start.19 = (bf16[20,24,256]{2,1,0:T(8,128)(2,1)}, bf16[20,24,256]{2,1,0:T(8,128)(2,1)S(1)}, u32[]{:S(2)}, u32[]{:S(2)}) collective-permute-start(bf16[20,24,256]{2,1,0:T(8,128)(2,1)} %get-tuple-element.56), channel_id=1, source_target_pairs={{0,8},{8,0},{16,24},{24,16},{1,9},{9,1},{17,25},{25,17},{2,10},{10... | collective-permute-start | bytes 737288 | tf_op jit(solution)/shard_map/ppermute | solution.py:431
  78.4 13.4 %collective-permute-start.20 = (bf16[20,24,256]{2,1,0:T(8,128)(2,1)}, bf16[20,24,256]{2,1,0:T(8,128)(2,1)S(1)}, u32[]{:S(2)}, u32[]{:S(2)}) collective-permute-start(bf16[20,24,256]{2,1,0:T(8,128)(2,1)} %get-tuple-element.57), channel_id=1, source_target_pairs={{0,16},{8,24},{16,0},{24,8},{1,17},{9,25},{17,1},{25,9},{2,18},{10... | collective-permute-start | bytes 737288 | tf_op jit(solution)/shard_map/ppermute | solution.py:431
  79.1 12.6 %collective-permute-start.14 = (bf16[20,24,256]{2,1,0:T(8,128)(2,1)S(1)}, bf16[20,24,256]{2,1,0:T(8,128)(2,1)S(1)}, u32[]{:S(2)}, u32[]{:S(2)}) collective-permute-start(bf16[20,24,256]{2,1,0:T(8,128)(2,1)S(1)} %copy-done.13), channel_id=1, source_target_pairs={{0,24},{8,16},{16,8},{24,0},{1,25},{9,17},{17,9},{25,1},{2,26},{10... | collective-permute-start | bytes 737288 | tf_op jit(solution)/shard_map/ppermute | solution.py:431
  80.2 11.5 %copy-start.6 = (bf16[20,24,256]{2,1,0:T(8,128)(2,1)S(1)}, bf16[20,24,256]{2,1,0:T(8,128)(2,1)}, u32[]{:S(2)}) copy-start(bf16[20,24,256]{2,1,0:T(8,128)(2,1)} %get-tuple-element.55) | copy-start | bytes 737284
  80.5 16.5 %collective-permute-start.21 = (bf16[20,24,256]{2,1,0:T(8,128)(2,1)S(1)}, bf16[20,24,256]{2,1,0:T(8,128)(2,1)S(1)}, u32[]{:S(2)}, u32[]{:S(2)}) collective-permute-start(bf16[20,24,256]{2,1,0:T(8,128)(2,1)S(1)} %copy-done.14), channel_id=1, source_target_pairs={{0,24},{8,16},{16,8},{24,0},{1,25},{9,17},{17,9},{25,1},{2,26},{10... | collective-permute-start | bytes 737288 | tf_op jit(solution)/shard_map/ppermute | solution.py:431
  91.8 5.1 %copy-start.2 = (bf16[20,192,256]{2,1,0:T(8,128)(2,1)}, bf16[20,192,256]{2,1,0:T(8,128)(2,1)S(1)}, u32[]{:S(2)}) copy-start(bf16[20,192,256]{2,1,0:T(8,128)(2,1)S(1)} %constant_dynamic-update-slice_fusion.1) | copy-start | bytes 5898244

commit v3 on v2

--- a/solution.py
+++ b/solution.py
@@ -13,9 +13,10 @@
 LANES = 128
 F32 = jnp.float32
 BF16 = jnp.bfloat16
-VMEM_BYTES = 56 * 1024 * 1024
+VMEM_BYTES = 16 * 1024 * 1024
 CHUNKS = 2
 GROUP = 12
+PAD = 1
 
 
 def group_of(blocks):
@@ -40,14 +41,15 @@
     members = groups * share
     half = members // 2
     tiles = width // LANES
+    pitch = rows_ref.shape[1] // members
     mem = mem_ref[0]
     scale = scale_ref[first : first + blocks, :]
     for d in range(groups):
-        base = (mem ^ d) * (share * blocks)
+        base = (mem ^ d) * (share * pitch)
 
         def scale_member(k, carry, part=parts[d], base=base):
             value = (part[k].astype(F32) * scale).astype(BF16).astype(F32)
-            start = pl.multiple_of(base + k * blocks, 8)
+            start = base + k * pitch
             for t in range(tiles):
                 rows_ref[t, pl.ds(start, blocks), :] = value[:, t * LANES : (t + 1) * LANES]
             return carry
@@ -63,7 +65,7 @@
         for u in range(unroll):
             b = i * unroll + u
             spread = jnp.concatenate(
-                [rows_ref[t, pl.ds(b, members, stride=blocks), :] for t in range(tiles)], axis=1
+                [rows_ref[t, pl.ds(b, members, stride=pitch), :] for t in range(tiles)], axis=1
             )
             weights = jnp.broadcast_to(weight_ref[pl.ds(first + b, 1), :], (spare, width))
             right = jnp.concatenate([spread, spread[half:], weights], axis=0).astype(BF16)
@@ -111,7 +113,7 @@
         out_shape=(jax.ShapeDtypeStruct(flat, F32), jax.ShapeDtypeStruct(flat, BF16)),
         in_specs=[smem()] + [vmem()] * (groups + 2),
         out_specs=(vmem(), vmem()),
-        scratch_shapes=[pltpu.VMEM((width // LANES, members * blocks, LANES), F32)],
+        scratch_shapes=[pltpu.VMEM((width // LANES, members * (blocks + PAD), LANES), F32)],
         compiler_params=params(),
         cost_estimate=pl.CostEstimate(
             flops=2 * blocks * members * width * LANES,
@@ -262,6 +264,7 @@
     center_ref, rows_ref = refs[2 * groups + 1 :]
     members = groups * share
     tiles = width // LANES
+    pitch = rows_ref.shape[1] // members
     mem = mem_ref[0]
     zero = jnp.zeros((blocks, width), F32)
     center = zero
@@ -272,11 +275,11 @@
     center = center * (1.0 / members)
     center_ref[...] = center
     for d in range(groups):
-        base = (mem ^ d) * (share * blocks)
+        base = (mem ^ d) * (share * pitch)
 
         def perturb(k, carry, part=parts[d], base=base):
             value = (part[k].astype(F32) - center_ref[...]).astype(BF16).astype(F32)
-            start = pl.multiple_of(base + k * blocks, 8)
+            start = base + k * pitch
             for t in range(tiles):
                 rows_ref[t, pl.ds(start, blocks), :] = value[:, t * LANES : (t + 1) * LANES]
             return carry
@@ -288,7 +291,7 @@
     def block_group(i, carry):
         for u in range(unroll):
             b = i * unroll + u
-            at = pl.ds(b, members, stride=blocks)
+            at = pl.ds(b, members, stride=pitch)
             anomalies = jnp.concatenate([rows_ref[t, at, :] for t in range(tiles)], axis=1)
             mixed = jnp.dot(
                 blend_ref[pl.ds(pl.multiple_of(b * members, 16), members), :],
@@ -302,10 +305,10 @@
     lax.fori_loop(0, blocks // unroll, block_group, 0)
 
     for d in range(groups):
-        base = (mem ^ d) * (share * blocks)
+        base = (mem ^ d) * (share * pitch)
 
         def finish(k, carry, out=outs[d], base=base):
-            start = pl.multiple_of(base + k * blocks, 8)
+            start = base + k * pitch
             mixed = jnp.concatenate(
                 [rows_ref[t, pl.ds(start, blocks), :] for t in range(tiles)], axis=1
             )
@@ -329,7 +332,7 @@
         out_specs=(vmem(),) * groups,
         scratch_shapes=[
             pltpu.VMEM((blocks, width), F32),
-            pltpu.VMEM((width // LANES, members * blocks, LANES), F32),
+            pltpu.VMEM((width // LANES, members * (blocks + PAD), LANES), F32),
         ],
         compiler_params=params(),
         cost_estimate=pl.CostEstimate(

time: 98.2 us -> 91.1 us (0.928)
  Pallas kernels: 28.9 us -> 21.1 us
  local copies, waits for them, and re-layouts: 16.1 us -> 18.1 us
  other arithmetic: 2.96 us -> 1.11 us
  waiting for transfers between devices: 32.2 us -> 33.3 us
    pallas_call x2, Pallas kernels: 7.62 us -> 3.66 us  [apply_blend(): pl.pallas_call(functools.partial(apply_kernel, groups=groups, share=share...]
    pallas_call x2, Pallas kernels: 14.5 us -> 12.3 us  [blends(): pl.pallas_call(functools.partial(blend_kernel, members=members, neighbour...]
    pallas_call x2, Pallas kernels: 6.83 us -> 5.07 us  [packed_grams(): pl.pallas_call(functools.partial(gram_kernel, groups=groups, share=share,...]
    unnamed x33 -> x19, local copies, waits for them, and re-layouts: 3.79 us -> 4.9 us
  transfers between devices with their start and end apart: 22 -> 22, of which waited for: 5 -> 5; matrix products, arithmetic and copies ran while one was open for 15% -> 14% of each run, Pallas kernels for 30% -> 23%
where the time goes in v3:
time: 91.1 us; the launch traced here: 90.6 us
  waiting for transfers between devices  33.3 us (37%)
  Pallas kernels  21.1 us (23%)
  local copies, waits for them, and re-layouts  18.1 us (20%)
  starting transfers between devices  16.8 us (18%)
  other arithmetic  1.11 us (1%)
    ppermute x6, waiting for transfers between devices, on_device(): came.append((d, c, lax.ppermute(out_parts[d], 'mem', peers[d])))  15.5 us
    pallas_call x2, Pallas kernels, blends(): pl.pallas_call(functools.partial(blend_kernel, members=members, neighbour...  12.3 us
    dynamic_slice x16, local copies, waits for them, and re-layouts, piece(): last = lax.dynamic_slice_in_dim(x, start, size, 1)  12 us
    ppermute x12, waiting for transfers between devices, exchanged(): lax.ppermute(piece(x, d, c), 'mem', peers[d])  9.05 us
    ppermute x2, waiting for transfers between devices, on_device(): left.append(lax.ppermute(packed, ('mem', 'lon'), forward))  8.74 us
    ppermute x12, starting transfers between devices, exchanged(): lax.ppermute(piece(x, d, c), 'mem', peers[d])  7.56 us
    pallas_call x2, Pallas kernels, packed_grams(): pl.pallas_call(functools.partial(gram_kernel, groups=groups, share=share,...  5.07 us
    unnamed x19, local copies, waits for them, and re-layouts  4.9 us
  transfers between devices with their start and end apart: 22, of which 5 were waited for; matrix products, arithmetic and copies ran while one was open for 14% of the time, Pallas kernels for 23%

profile of v3, /device:TPU:0, one launch (start us, length us, event | category | flops | bytes accessed | tf_op | source)
XLA Modules:
  0.0 90.6 jit_solution(16774104654589950887)
XLA Ops:
  0.0 1.5 %copy-done = bf16[20,192,256]{2,1,0:T(8,128)(2,1)S(1)} copy-done((bf16[20,192,256]{2,1,0:T(8,128)(2,1)S(1)}, bf16[20,192,256]{2,1,0:T(8,128)(2,1)}, u32[]{:S(2)}) %copy-start) | copy-done | bytes 1966104
  1.6 0.7 constant_dynamic-slice_fusion.15
  2.3 2.4 %collective-permute-start.5 = (bf16[20,24,256]{2,1,0:T(8,128)(2,1)}, bf16[20,24,256]{2,1,0:T(8,128)(2,1)S(1)}, u32[]{:S(2)}, u32[]{:S(2)}) collective-permute-start(bf16[20,24,256]{2,1,0:T(8,128)(2,1)} %constant_dynamic-slice_fusion.15), channel_id=1, source_target_pairs={{0,24},{8,16},{16,8},{24,0},{1,25},{9,17},{17,9},{25,1},{2,26},{10... | collective-permute-start | bytes 737288 | tf_op jit(solution)/shard_map/ppermute | solution.py:399
  4.7 0.7 constant_dynamic-slice_fusion.14
  5.4 0.7 collective-permute-start.3
  6.2 0.7 constant_dynamic-slice_fusion.12
  6.9 0.0 collective-permute-start.8
  6.9 0.7 constant_dynamic-slice_fusion.11
  7.6 1.4 %collective-permute-start.9 = (bf16[20,24,256]{2,1,0:T(8,128)(2,1)}, bf16[20,24,256]{2,1,0:T(8,128)(2,1)}, u32[]{:S(2)}, u32[]{:S(2)}) collective-permute-start(bf16[20,24,256]{2,1,0:T(8,128)(2,1)} %constant_dynamic-slice_fusion.11), channel_id=1, source_target_pairs={{0,24},{8,16},{16,8},{24,0},{1,25},{9,17},{17,9},{25,1},{2,26},{10... | collective-permute-start | bytes 737288 | tf_op jit(solution)/shard_map/ppermute | solution.py:399
  9.0 0.7 constant_dynamic-slice_fusion.10
  9.7 0.8 collective-permute-start.7
  10.5 1.8 %constant_dynamic-slice_fusion.8 = bf16[20,24,256]{2,1,0:T(8,128)(2,1)} fusion(bf16[20,192,256]{2,1,0:T(8,128)(2,1)} %param.6, s32[]{:T(128)S(6)} %select_n.73), kind=kLoop, calls=%fused_computation.24 | loop fusion | bytes 491524 | tf_op jit(solution)/shard_map/dynamic_slice | solution.py:392
  12.3 1.6 %constant_dynamic-slice_fusion.7 = bf16[20,24,256]{2,1,0:T(8,128)(2,1)} fusion(bf16[20,192,256]{2,1,0:T(8,128)(2,1)} %param.6, s32[]{:T(128)S(6)} %select_n.74), kind=kLoop, calls=%fused_computation.23 | loop fusion | bytes 491524 | tf_op jit(solution)/shard_map/dynamic_slice | solution.py:392
  14.0 1.7 %constant_dynamic-slice_fusion.6 = bf16[20,24,256]{2,1,0:T(8,128)(2,1)} fusion(bf16[20,192,256]{2,1,0:T(8,128)(2,1)} %param.6, s32[]{:T(128)S(6)} %select_n.75), kind=kLoop, calls=%fused_computation.22 | loop fusion | bytes 491524 | tf_op jit(solution)/shard_map/dynamic_slice | solution.py:392
  15.6 0.7 constant_dynamic-slice_fusion.3
  16.4 0.7 constant_dynamic-slice_fusion.2
  17.1 0.7 constant_dynamic-slice_fusion.1
  17.8 0.7 copy-done.1
  18.5 0.1 constant_dynamic-slice_fusion.4
  18.6 0.1 dynamic_slice.73
  18.7 0.9 %dynamic-slice_multiply_fusion = (f32[48,256]{1,0:T(8,128)S(1)}, f32[48,256]{1,0:T(8,128)S(1)}) fusion(f32[192,256]{1,0:T(8,128)} %param.8, s32[]{:T(128)S(6)} %select_n.76, f32[192,256]{1,0:T(8,128)} %param.9, s32[48]{0:T(128)S(1)} %dynamic_slice.73), kind=kLoop, calls=%fused_computation.1 | loop fusion | flops 36864 | bytes 196804 | tf_op jit(solution)/shard_map/mul | solution.py:410
  19.6 0.2 collective-permute-start
  19.8 7.5 %collective-permute-done.4.refs_2_ = bf16[20,24,256]{2,1,0:T(8,128)(2,1)S(1)} collective-permute-done((bf16[20,24,256]{2,1,0:T(8,128)(2,1)S(1)}, bf16[20,24,256]{2,1,0:T(8,128)(2,1)S(1)}, u32[]{:S(2)}, u32[]{:S(2)}) %collective-permute-start.4) | collective-permute-done | bytes 245792 | tf_op jit(solution)/shard_map/ppermute | solution.py:399
  27.2 0.7 copy-done.3
  27.9 2.0 %collective-permute-start.2 = (bf16[20,24,256]{2,1,0:T(8,128)(2,1)}, bf16[20,24,256]{2,1,0:T(8,128)(2,1)}, u32[]{:S(2)}, u32[]{:S(2)}) collective-permute-start(bf16[20,24,256]{2,1,0:T(8,128)(2,1)} %constant_dynamic-slice_fusion.7), channel_id=1, source_target_pairs={{0,24},{8,16},{16,8},{24,0},{1,25},{9,17},{17,9},{25,1},{2,26},{10... | collective-permute-start | bytes 737288 | tf_op jit(solution)/shard_map/ppermute | solution.py:399
  29.9 0.9 %copy-done.2 = bf16[20,24,256]{2,1,0:T(8,128)(2,1)S(1)} copy-done((bf16[20,24,256]{2,1,0:T(8,128)(2,1)S(1)}, bf16[20,24,256]{2,1,0:T(8,128)(2,1)}, u32[]{:S(2)}) %copy-start.2) | copy-done | bytes 245784
  30.9 0.9 %copy-done.4 = bf16[20,24,256]{2,1,0:T(8,128)(2,1)S(1)} copy-done((bf16[20,24,256]{2,1,0:T(8,128)(2,1)S(1)}, bf16[20,24,256]{2,1,0:T(8,128)(2,1)}, u32[]{:S(2)}) %copy-start.4) | copy-done | bytes 245784
  31.8 1.9 %packed_grams.2 = (f32[960,128]{1,0:T(8,128)S(1)}, bf16[960,128]{1,0:T(8,128)(2,1)}) custom-call(s32[1]{0:T(128)} %bitcast.mem_ref, bf16[20,24,256]{2,1,0:T(8,128)(2,1)S(1)} %constant_dynamic-slice_fusion.13.refs_0_, bf16[20,24,256]{2,1,0:T(8,128)(2,1)S(1)} %copy-done.2, bf16[20,24,256]{2,1,0:T(8,128)(2,1)S(1)} %copy-done.4, ...), custom_call_target="tpu_custom_call" | custom-call | flops 125829120 | bytes 983040 | tf_op jit(solution)/shard_map/packed_grams/pallas_call | solution.py:103
  33.8 0.0 collective-permute-done.7.refs_1_
  33.8 4.6 %collective-permute-start.11 = (bf16[960,128]{1,0:T(8,128)(2,1)}, bf16[960,128]{1,0:T(8,128)(2,1)}, u32[]{:S(2)}, u32[]{:S(2)}) collective-permute-start(bf16[960,128]{1,0:T(8,128)(2,1)} %get-tuple-element.43), channel_id=1, source_target_pairs={{0,7},{8,0},{16,8},{24,16},{25,24},{17,25},{9,17},{1,9},{2,1},{10,... | collective-permute-start | bytes 737288 | tf_op jit(solution)/shard_map/ppermute | solution.py:425
  38.3 0.0 collective-permute-done.9.refs_3_
  38.3 0.0 collective-permute-start.6
  38.3 0.0 collective-permute-done.8.refs_2_
  38.3 3.1 %packed_grams.3 = (f32[960,128]{1,0:T(8,128)S(1)}, bf16[960,128]{1,0:T(8,128)(2,1)}) custom-call(s32[1]{0:T(128)} %bitcast.mem_ref, bf16[20,24,256]{2,1,0:T(8,128)(2,1)S(1)} %constant_dynamic-slice_fusion.9.refs_0_, bf16[20,24,256]{2,1,0:T(8,128)(2,1)} %collective-permute-done.7.refs_1_, bf16[20,24,256]{2,1,0:T(8,128)(2,1)} %collective-permute-done.8.refs_2_, ...), custom_call_target="tpu_custom_call" | custom-call | flops 125829120 | bytes 983040 | tf_op jit(solution)/shard_map/packed_grams/pallas_call | solution.py:103
  41.5 0.1 copy.8
  41.6 0.1 add_multiply_fusion.row_ref
  41.7 0.0 collective-permute-done.refs_1_
  41.7 0.1 collective-permute-start.17
  41.8 0.1 collective-permute-start.16
  41.8 8.7 %collective-permute-done.10.refs_1_.refs_0_ = bf16[960,128]{1,0:T(8,128)(2,1)S(1)} collective-permute-done((bf16[960,128]{1,0:T(8,128)(2,1)}, bf16[960,128]{1,0:T(8,128)(2,1)S(1)}, u32[]{:S(2)}, u32[]{:S(2)}) %collective-permute-start.10) | collective-permute-done | bytes 245792 | tf_op jit(solution)/shard_map/ppermute | solution.py:424
  50.6 0.0 collective-permute-start.15
  50.6 0.1 collective-permute-start.18
  50.7 0.1 add_divide_fusion.taper_ref
  50.8 6.2 %blends.2.refs_4_ = bf16[1920,128]{1,0:T(8,128)(2,1)S(1)} custom-call(s32[48,16]{1,0:T(8,128)S(1)} %add_multiply_fusion.row_ref, f32[48,16]{1,0:T(8,128)S(1)} %add_divide_fusion.taper_ref, bf16[960,128]{1,0:T(8,128)(2,1)} %collective-permute-done.6.refs_0_, bf16[960,128]{1,0:T(8,128)(2,1)S(1)} %collective-permute-done.10.refs_1_.refs_0_, ...), custom_call_target="tpu_custom_call" | custom-call | flops 471859200 | bytes 1843200 | tf_op jit(solution)/shard_map/blends/pallas_call | solution.py:237
  57.0 1.5 %collective-permute-done.1.refs_2_ = bf16[20,24,256]{2,1,0:T(8,128)(2,1)S(1)} collective-permute-done((bf16[20,24,256]{2,1,0:T(8,128)(2,1)}, bf16[20,24,256]{2,1,0:T(8,128)(2,1)S(1)}, u32[]{:S(2)}, u32[]{:S(2)}) %collective-permute-start.1) | collective-permute-done | bytes 245792 | tf_op jit(solution)/shard_map/ppermute | solution.py:399
  58.5 2.4 %apply_blend.2 = (bf16[20,24,256]{2,1,0:T(8,128)(2,1)S(1)}, bf16[20,24,256]{2,1,0:T(8,128)(2,1)S(1)}, bf16[20,24,256]{2,1,0:T(8,128)(2,1)S(1)}, bf16[20,24,256]{2,1,0:T(8,128)(2,1)S(1)}) custom-call(s32[1]{0:T(128)} %bitcast.mem_ref, bf16[20,24,256]{2,1,0:T(8,128)(2,1)S(1)} %constant_dynamic-slice_fusion.5.refs_0_, ...), custom_call_target="tpu_custom_call" | custom-call | flops 125829120 | bytes 1966080 | tf_op jit(solution)/shard_map/apply_blend/pallas_call | solution.py:326
  60.9 0.1 collective-permute-start.12
  61.0 1.0 %constant_dynamic-slice_fusion.refs_0_ = bf16[20,24,256]{2,1,0:T(8,128)(2,1)S(1)} fusion(bf16[20,192,256]{2,1,0:T(8,128)(2,1)} %param.6, s32[]{:T(128)S(6)} %select_n.80), kind=kLoop, calls=%fused_computation.12 | loop fusion | bytes 491524 | tf_op jit(solution)/shard_map/dynamic_slice | solution.py:392
  61.9 2.1 %collective-permute-start.13 = (bf16[20,24,256]{2,1,0:T(8,128)(2,1)S(1)}, bf16[20,24,256]{2,1,0:T(8,128)(2,1)S(1)}, u32[]{:S(2)}, u32[]{:S(2)}) collective-permute-start(bf16[20,24,256]{2,1,0:T(8,128)(2,1)S(1)} %get-tuple-element.49), channel_id=1, source_target_pairs={{0,16},{8,24},{16,0},{24,8},{1,17},{9,25},{17,1},{25,9},{2,18},{10... | collective-permute-start | bytes 737288 | tf_op jit(solution)/shard_map/ppermute | solution.py:434
  64.1 6.2 %blends.3.refs_4_ = bf16[1920,128]{1,0:T(8,128)(2,1)S(1)} custom-call(s32[48,16]{1,0:T(8,128)S(1)} %add_multiply_fusion.row_ref, f32[48,16]{1,0:T(8,128)S(1)} %add_divide_fusion.taper_ref, bf16[960,128]{1,0:T(8,128)(2,1)S(1)} %collective-permute-done.10.refs_1_.refs_0_, f32[960,128]{1,0:T(8,128)S(1)} %get-tuple-element.45.refs_2_.refs_1_, ...), custom_call_target="tpu_custom_call" | custom-call | flops 471859200 | bytes 1843200 | tf_op jit(solution)/shard_map/blends/pallas_call | solution.py:237
  70.2 0.0 collective-permute-done.15.refs_1_
  70.3 0.0 collective-permute-done.17.refs_3_
  70.3 1.3 %apply_blend.3 = (bf16[20,24,256]{2,1,0:T(8,128)(2,1)S(1)}, bf16[20,24,256]{2,1,0:T(8,128)(2,1)S(1)}, bf16[20,24,256]{2,1,0:T(8,128)(2,1)S(1)}, bf16[20,24,256]{2,1,0:T(8,128)(2,1)S(1)}) custom-call(s32[1]{0:T(128)} %bitcast.mem_ref, bf16[20,24,256]{2,1,0:T(8,128)(2,1)S(1)} %constant_dynamic-slice_fusion.refs_0_, ...), custom_call_target="tpu_custom_call" | custom-call | flops 125829120 | bytes 1966080 | tf_op jit(solution)/shard_map/apply_blend/pallas_call | solution.py:326
  71.6 0.3 collective-permute-start.19
  71.9 0.3 collective-permute-start.20
  72.2 1.4 %collective-permute-start.14 = (bf16[20,24,256]{2,1,0:T(8,128)(2,1)S(1)}, bf16[20,24,256]{2,1,0:T(8,128)(2,1)S(1)}, u32[]{:S(2)}, u32[]{:S(2)}) collective-permute-start(bf16[20,24,256]{2,1,0:T(8,128)(2,1)S(1)} %get-tuple-element.50), channel_id=1, source_target_pairs={{0,24},{8,16},{16,8},{24,0},{1,25},{9,17},{17,9},{25,1},{2,26},{10... | collective-permute-start | bytes 737288 | tf_op jit(solution)/shard_map/ppermute | solution.py:434
  73.5 0.2 broadcast_in_dim.2
  73.8 0.5 collective-permute-start.21
  74.2 0.0 collective-permute-done.13
  74.3 10.3 %collective-permute-done.14 = bf16[20,24,256]{2,1,0:T(8,128)(2,1)S(1)} collective-permute-done((bf16[20,24,256]{2,1,0:T(8,128)(2,1)S(1)}, bf16[20,24,256]{2,1,0:T(8,128)(2,1)S(1)}, u32[]{:S(2)}, u32[]{:S(2)}) %collective-permute-start.14) | collective-permute-done | bytes 245792 | tf_op jit(solution)/shard_map/ppermute | solution.py:434
  84.7 0.0 collective-permute-done.19
  84.8 0.0 copy-start.6
  84.8 5.1 %collective-permute-done.21 = bf16[20,24,256]{2,1,0:T(8,128)(2,1)S(1)} collective-permute-done((bf16[20,24,256]{2,1,0:T(8,128)(2,1)S(1)}, bf16[20,24,256]{2,1,0:T(8,128)(2,1)S(1)}, u32[]{:S(2)}, u32[]{:S(2)}) %collective-permute-start.21) | collective-permute-done | bytes 245792 | tf_op jit(solution)/shard_map/ppermute | solution.py:434
  89.9 0.7 constant_dynamic-update-slice_fusion
  (36 shorter events, 0.3 us)
Async XLA Ops:
  0.0 1.5 %copy-start = (bf16[20,192,256]{2,1,0:T(8,128)(2,1)S(1)}, bf16[20,192,256]{2,1,0:T(8,128)(2,1)}, u32[]{:S(2)}) copy-start(bf16[20,192,256]{2,1,0:T(8,128)(2,1)} %param.7) | copy-start | bytes 5898244
  2.3 17.3 %collective-permute-start.5 = (bf16[20,24,256]{2,1,0:T(8,128)(2,1)}, bf16[20,24,256]{2,1,0:T(8,128)(2,1)S(1)}, u32[]{:S(2)}, u32[]{:S(2)}) collective-permute-start(bf16[20,24,256]{2,1,0:T(8,128)(2,1)} %constant_dynamic-slice_fusion.15), channel_id=1, source_target_pairs={{0,24},{8,16},{16,8},{24,0},{1,25},{9,17},{17,9},{25,1},{2,26},{10... | collective-permute-start | bytes 737288 | tf_op jit(solution)/shard_map/ppermute | solution.py:399
  5.4 12.4 %collective-permute-start.3 = (bf16[20,24,256]{2,1,0:T(8,128)(2,1)}, bf16[20,24,256]{2,1,0:T(8,128)(2,1)S(1)}, u32[]{:S(2)}, u32[]{:S(2)}) collective-permute-start(bf16[20,24,256]{2,1,0:T(8,128)(2,1)} %constant_dynamic-slice_fusion.14), channel_id=1, source_target_pairs={{0,8},{8,0},{16,24},{24,16},{1,9},{9,1},{17,25},{25,17},{2,10},{10... | collective-permute-start | bytes 737288 | tf_op jit(solution)/shard_map/ppermute | solution.py:399
  6.9 31.4 %collective-permute-start.8 = (bf16[20,24,256]{2,1,0:T(8,128)(2,1)}, bf16[20,24,256]{2,1,0:T(8,128)(2,1)}, u32[]{:S(2)}, u32[]{:S(2)}) collective-permute-start(bf16[20,24,256]{2,1,0:T(8,128)(2,1)} %constant_dynamic-slice_fusion.12), channel_id=1, source_target_pairs={{0,16},{8,24},{16,0},{24,8},{1,17},{9,25},{17,1},{25,9},{2,18},{10... | collective-permute-start | bytes 737288 | tf_op jit(solution)/shard_map/ppermute | solution.py:399
  7.6 30.7 %collective-permute-start.9 = (bf16[20,24,256]{2,1,0:T(8,128)(2,1)}, bf16[20,24,256]{2,1,0:T(8,128)(2,1)}, u32[]{:S(2)}, u32[]{:S(2)}) collective-permute-start(bf16[20,24,256]{2,1,0:T(8,128)(2,1)} %constant_dynamic-slice_fusion.11), channel_id=1, source_target_pairs={{0,24},{8,16},{16,8},{24,0},{1,25},{9,17},{17,9},{25,1},{2,26},{10... | collective-permute-start | bytes 737288 | tf_op jit(solution)/shard_map/ppermute | solution.py:399
  9.7 24.1 %collective-permute-start.7 = (bf16[20,24,256]{2,1,0:T(8,128)(2,1)}, bf16[20,24,256]{2,1,0:T(8,128)(2,1)}, u32[]{:S(2)}, u32[]{:S(2)}) collective-permute-start(bf16[20,24,256]{2,1,0:T(8,128)(2,1)} %constant_dynamic-slice_fusion.10), channel_id=1, source_target_pairs={{0,8},{8,0},{16,24},{24,16},{1,9},{9,1},{17,25},{25,17},{2,10},{10... | collective-permute-start | bytes 737288 | tf_op jit(solution)/shard_map/ppermute | solution.py:399
  10.5 5.2 %copy-start.5 = (bf16[20,192,256]{2,1,0:T(8,128)(2,1)S(1)}, bf16[20,192,256]{2,1,0:T(8,128)(2,1)}, u32[]{:S(2)}) copy-start(bf16[20,192,256]{2,1,0:T(8,128)(2,1)} %param.6) | copy-start | bytes 5898244
  10.5 8.0 %copy-start.7 = (s32[192,16]{0,1:T(8,128)S(1)}, s32[192,16]{0,1:T(8,128)}, u32[]{:S(2)}) copy-start(s32[192,16]{0,1:T(8,128)} %param.11) | copy-start | bytes 36868
  10.5 8.1 %copy-start.8 = (s32[192]{0:T(256)S(1)}, s32[192]{0:T(256)}, u32[]{:S(2)}) copy-start(s32[192]{0:T(256)} %param.10) | copy-start | bytes 2308
  17.8 0.7 copy-start.1
  18.5 8.7 %collective-permute-start.4 = (bf16[20,24,256]{2,1,0:T(8,128)(2,1)S(1)}, bf16[20,24,256]{2,1,0:T(8,128)(2,1)S(1)}, u32[]{:S(2)}, u32[]{:S(2)}) collective-permute-start(bf16[20,24,256]{2,1,0:T(8,128)(2,1)S(1)} %constant_dynamic-slice_fusion.16), channel_id=1, source_target_pairs={{0,16},{8,24},{16,0},{24,8},{1,17},{9,25},{17,1},{25,9},{2,18},{10... | collective-permute-start | bytes 737288 | tf_op jit(solution)/shard_map/ppermute | solution.py:399
  19.6 22.1 %collective-permute-start = (bf16[20,24,256]{2,1,0:T(8,128)(2,1)}, bf16[20,24,256]{2,1,0:T(8,128)(2,1)}, u32[]{:S(2)}, u32[]{:S(2)}) collective-permute-start(bf16[20,24,256]{2,1,0:T(8,128)(2,1)} %constant_dynamic-slice_fusion.6), channel_id=1, source_target_pairs={{0,8},{8,0},{16,24},{24,16},{1,9},{9,1},{17,25},{25,17},{2,10},{10... | collective-permute-start | bytes 737288 | tf_op jit(solution)/shard_map/ppermute | solution.py:399
  27.2 0.7 copy-start.3
  27.9 13.8 %collective-permute-start.2 = (bf16[20,24,256]{2,1,0:T(8,128)(2,1)}, bf16[20,24,256]{2,1,0:T(8,128)(2,1)}, u32[]{:S(2)}, u32[]{:S(2)}) collective-permute-start(bf16[20,24,256]{2,1,0:T(8,128)(2,1)} %constant_dynamic-slice_fusion.7), channel_id=1, source_target_pairs={{0,24},{8,16},{16,8},{24,0},{1,25},{9,17},{17,9},{25,1},{2,26},{10... | collective-permute-start | bytes 737288 | tf_op jit(solution)/shard_map/ppermute | solution.py:399
  29.9 0.9 %copy-start.2 = (bf16[20,24,256]{2,1,0:T(8,128)(2,1)S(1)}, bf16[20,24,256]{2,1,0:T(8,128)(2,1)}, u32[]{:S(2)}) copy-start(bf16[20,24,256]{2,1,0:T(8,128)(2,1)} %copy-done.1) | copy-start | bytes 737284
  30.9 0.9 %copy-start.4 = (bf16[20,24,256]{2,1,0:T(8,128)(2,1)S(1)}, bf16[20,24,256]{2,1,0:T(8,128)(2,1)}, u32[]{:S(2)}) copy-start(bf16[20,24,256]{2,1,0:T(8,128)(2,1)} %copy-done.3) | copy-start | bytes 737284
  33.8 16.8 %collective-permute-start.11 = (bf16[960,128]{1,0:T(8,128)(2,1)}, bf16[960,128]{1,0:T(8,128)(2,1)}, u32[]{:S(2)}, u32[]{:S(2)}) collective-permute-start(bf16[960,128]{1,0:T(8,128)(2,1)} %get-tuple-element.43), channel_id=1, source_target_pairs={{0,7},{8,0},{16,8},{24,16},{25,24},{17,25},{9,17},{1,9},{2,1},{10,... | collective-permute-start | bytes 737288 | tf_op jit(solution)/shard_map/ppermute | solution.py:425
  38.3 12.3 %collective-permute-start.6 = (bf16[960,128]{1,0:T(8,128)(2,1)}, bf16[960,128]{1,0:T(8,128)(2,1)}, u32[]{:S(2)}, u32[]{:S(2)}) collective-permute-start(bf16[960,128]{1,0:T(8,128)(2,1)} %get-tuple-element.43), channel_id=1, source_target_pairs={{0,8},{8,16},{16,24},{24,25},{25,17},{17,9},{9,1},{1,2},{2,10},{10... | collective-permute-start | bytes 737288 | tf_op jit(solution)/shard_map/ppermute | solution.py:424
  41.5 9.1 %collective-permute-start.10 = (bf16[960,128]{1,0:T(8,128)(2,1)}, bf16[960,128]{1,0:T(8,128)(2,1)S(1)}, u32[]{:S(2)}, u32[]{:S(2)}) collective-permute-start(bf16[960,128]{1,0:T(8,128)(2,1)} %get-tuple-element.44), channel_id=1, source_target_pairs={{0,8},{8,16},{16,24},{24,25},{25,17},{17,9},{9,1},{1,2},{2,10},{10... | collective-permute-start | bytes 737288 | tf_op jit(solution)/shard_map/ppermute | solution.py:424
  41.7 28.6 %collective-permute-start.17 = (bf16[20,24,256]{2,1,0:T(8,128)(2,1)}, bf16[20,24,256]{2,1,0:T(8,128)(2,1)S(1)}, u32[]{:S(2)}, u32[]{:S(2)}) collective-permute-start(bf16[20,24,256]{2,1,0:T(8,128)(2,1)} %constant_dynamic-slice_fusion.2), channel_id=1, source_target_pairs={{0,24},{8,16},{16,8},{24,0},{1,25},{9,17},{17,9},{25,1},{2,26},{10... | collective-permute-start | bytes 737288 | tf_op jit(solution)/shard_map/ppermute | solution.py:399
  41.8 28.5 %collective-permute-start.16 = (bf16[20,24,256]{2,1,0:T(8,128)(2,1)}, bf16[20,24,256]{2,1,0:T(8,128)(2,1)S(1)}, u32[]{:S(2)}, u32[]{:S(2)}) collective-permute-start(bf16[20,24,256]{2,1,0:T(8,128)(2,1)} %constant_dynamic-slice_fusion.3), channel_id=1, source_target_pairs={{0,16},{8,24},{16,0},{24,8},{1,17},{9,25},{17,1},{25,9},{2,18},{10... | collective-permute-start | bytes 737288 | tf_op jit(solution)/shard_map/ppermute | solution.py:399
  50.6 7.9 %collective-permute-start.1 = (bf16[20,24,256]{2,1,0:T(8,128)(2,1)}, bf16[20,24,256]{2,1,0:T(8,128)(2,1)S(1)}, u32[]{:S(2)}, u32[]{:S(2)}) collective-permute-start(bf16[20,24,256]{2,1,0:T(8,128)(2,1)} %constant_dynamic-slice_fusion.8), channel_id=1, source_target_pairs={{0,16},{8,24},{16,0},{24,8},{1,17},{9,25},{17,1},{25,9},{2,18},{10... | collective-permute-start | bytes 737288 | tf_op jit(solution)/shard_map/ppermute | solution.py:399
  50.6 19.7 %collective-permute-start.15 = (bf16[20,24,256]{2,1,0:T(8,128)(2,1)}, bf16[20,24,256]{2,1,0:T(8,128)(2,1)S(1)}, u32[]{:S(2)}, u32[]{:S(2)}) collective-permute-start(bf16[20,24,256]{2,1,0:T(8,128)(2,1)} %constant_dynamic-slice_fusion.1), channel_id=1, source_target_pairs={{0,8},{8,0},{16,24},{24,16},{1,9},{9,1},{17,25},{25,17},{2,10},{10... | collective-permute-start | bytes 737288 | tf_op jit(solution)/shard_map/ppermute | solution.py:399
  50.6 11.3 %collective-permute-start.18 = (bf16[960,128]{1,0:T(8,128)(2,1)}, bf16[960,128]{1,0:T(8,128)(2,1)S(1)}, u32[]{:S(2)}, u32[]{:S(2)}) collective-permute-start(bf16[960,128]{1,0:T(8,128)(2,1)} %get-tuple-element.44), channel_id=1, source_target_pairs={{0,7},{8,0},{16,8},{24,16},{25,24},{17,25},{9,17},{1,9},{2,1},{10,... | collective-permute-start | bytes 737288 | tf_op jit(solution)/shard_map/ppermute | solution.py:425
  60.9 12.9 %collective-permute-start.12 = (bf16[20,24,256]{2,1,0:T(8,128)(2,1)S(1)}, bf16[20,24,256]{2,1,0:T(8,128)(2,1)S(1)}, u32[]{:S(2)}, u32[]{:S(2)}) collective-permute-start(bf16[20,24,256]{2,1,0:T(8,128)(2,1)S(1)} %get-tuple-element.48), channel_id=1, source_target_pairs={{0,8},{8,0},{16,24},{24,16},{1,9},{9,1},{17,25},{25,17},{2,10},{10... | collective-permute-start | bytes 737288 | tf_op jit(solution)/shard_map/ppermute | solution.py:434
  61.9 12.3 %collective-permute-start.13 = (bf16[20,24,256]{2,1,0:T(8,128)(2,1)S(1)}, bf16[20,24,256]{2,1,0:T(8,128)(2,1)S(1)}, u32[]{:S(2)}, u32[]{:S(2)}) collective-permute-start(bf16[20,24,256]{2,1,0:T(8,128)(2,1)S(1)} %get-tuple-element.49), channel_id=1, source_target_pairs={{0,16},{8,24},{16,0},{24,8},{1,17},{9,25},{17,1},{25,9},{2,18},{10... | collective-permute-start | bytes 737288 | tf_op jit(solution)/shard_map/ppermute | solution.py:434
  71.6 13.1 %collective-permute-start.19 = (bf16[20,24,256]{2,1,0:T(8,128)(2,1)S(1)}, bf16[20,24,256]{2,1,0:T(8,128)(2,1)S(1)}, u32[]{:S(2)}, u32[]{:S(2)}) collective-permute-start(bf16[20,24,256]{2,1,0:T(8,128)(2,1)S(1)} %get-tuple-element.56), channel_id=1, source_target_pairs={{0,8},{8,0},{16,24},{24,16},{1,9},{9,1},{17,25},{25,17},{2,10},{10... | collective-permute-start | bytes 737288 | tf_op jit(solution)/shard_map/ppermute | solution.py:434
  71.9 12.9 %collective-permute-start.20 = (bf16[20,24,256]{2,1,0:T(8,128)(2,1)S(1)}, bf16[20,24,256]{2,1,0:T(8,128)(2,1)S(1)}, u32[]{:S(2)}, u32[]{:S(2)}) collective-permute-start(bf16[20,24,256]{2,1,0:T(8,128)(2,1)S(1)} %get-tuple-element.57), channel_id=1, source_target_pairs={{0,16},{8,24},{16,0},{24,8},{1,17},{9,25},{17,1},{25,9},{2,18},{10... | collective-permute-start | bytes 737288 | tf_op jit(solution)/shard_map/ppermute | solution.py:434
  72.2 12.5 %collective-permute-start.14 = (bf16[20,24,256]{2,1,0:T(8,128)(2,1)S(1)}, bf16[20,24,256]{2,1,0:T(8,128)(2,1)S(1)}, u32[]{:S(2)}, u32[]{:S(2)}) collective-permute-start(bf16[20,24,256]{2,1,0:T(8,128)(2,1)S(1)} %get-tuple-element.50), channel_id=1, source_target_pairs={{0,24},{8,16},{16,8},{24,0},{1,25},{9,17},{17,9},{25,1},{2,26},{10... | collective-permute-start | bytes 737288 | tf_op jit(solution)/shard_map/ppermute | solution.py:434
  73.8 16.1 %collective-permute-start.21 = (bf16[20,24,256]{2,1,0:T(8,128)(2,1)S(1)}, bf16[20,24,256]{2,1,0:T(8,128)(2,1)S(1)}, u32[]{:S(2)}, u32[]{:S(2)}) collective-permute-start(bf16[20,24,256]{2,1,0:T(8,128)(2,1)S(1)} %get-tuple-element.58), channel_id=1, source_target_pairs={{0,24},{8,16},{16,8},{24,0},{1,25},{9,17},{17,9},{25,1},{2,26},{10... | collective-permute-start | bytes 737288 | tf_op jit(solution)/shard_map/ppermute | solution.py:434
  84.8 5.1 %copy-start.6 = (bf16[20,192,256]{2,1,0:T(8,128)(2,1)}, bf16[20,192,256]{2,1,0:T(8,128)(2,1)S(1)}, u32[]{:S(2)}) copy-start(bf16[20,192,256]{2,1,0:T(8,128)(2,1)S(1)} %constant_dynamic-update-slice_fusion.1) | copy-start | bytes 5898244

commit v4 on v3

--- a/solution.py
+++ b/solution.py
@@ -14,6 +14,7 @@
 F32 = jnp.float32
 BF16 = jnp.bfloat16
 VMEM_BYTES = 16 * 1024 * 1024
+CROWDED_BYTES = 66_000_000
 CHUNKS = 2
 GROUP = 12
 PAD = 1
@@ -31,18 +32,54 @@
     return pl.BlockSpec(memory_space=pltpu.SMEM)
 
 
-def params():
-    return pltpu.CompilerParams(vmem_limit_bytes=VMEM_BYTES)
-
-
-def gram_kernel(mem_ref, *refs, groups, share, blocks, width, unroll, first):
+def params(vmem_bytes=VMEM_BYTES):
+    return pltpu.CompilerParams(vmem_limit_bytes=vmem_bytes)
+
+
+def flip_of(groups):
+    return (lax.axis_index("lon") % 2) * (groups - 1)
+
+
+def pick_kernel(whole_ref, *refs, wanted, groups, size):
+    outs, sems = refs[: len(wanted)], refs[len(wanted)]
+    mem = lax.axis_index("mem")
+    flip = flip_of(groups)
+    copies = []
+    for i, (d, c) in enumerate(wanted):
+        start = ((mem ^ d) ^ flip) * (whole_ref.shape[1] // groups) + c * size
+        rows = pl.ds(pl.multiple_of(start, 8), size)
+        copies.append(pltpu.make_async_copy(whole_ref.at[:, rows, :], outs[i], sems.at[i]))
+        copies[-1].start()
+    for copy in copies:
+        copy.wait()
+
+
+def picked(x, wanted, groups, size):
+    share, _, width = x.shape
+    return pl.pallas_call(
+        functools.partial(pick_kernel, wanted=tuple(wanted), groups=groups, size=size),
+        out_shape=[jax.ShapeDtypeStruct((share, size, width), x.dtype)] * len(wanted),
+        in_specs=[pl.BlockSpec(memory_space=pltpu.HBM)],
+        out_specs=[vmem()] * len(wanted),
+        scratch_shapes=[pltpu.SemaphoreType.DMA((len(wanted),))],
+        compiler_params=params(CROWDED_BYTES),
+        cost_estimate=pl.CostEstimate(
+            flops=0,
+            bytes_accessed=4 * share * size * width * len(wanted),
+            transcendentals=0,
+        ),
+        name="picked",
+    )(x)
+
+
+def gram_kernel(*refs, groups, share, blocks, width, unroll, first):
     parts = refs[:groups]
     scale_ref, weight_ref, own_ref, send_ref, rows_ref = refs[groups:]
     members = groups * share
     half = members // 2
     tiles = width // LANES
     pitch = rows_ref.shape[1] // members
-    mem = mem_ref[0]
+    mem = lax.axis_index("mem")
     scale = scale_ref[first : first + blocks, :]
     for d in range(groups):
         base = (mem ^ d) * (share * pitch)
@@ -93,7 +130,7 @@
     lax.fori_loop(0, blocks // 2, finish, 0, unroll=2)
 
 
-def packed_grams(mem, parts, scale, weighted, first):
+def packed_grams(parts, scale, weighted, first):
     groups = len(parts)
     share, blocks, width = parts[0].shape
     members = groups * share
@@ -111,7 +148,7 @@
             first=first,
         ),
         out_shape=(jax.ShapeDtypeStruct(flat, F32), jax.ShapeDtypeStruct(flat, BF16)),
-        in_specs=[smem()] + [vmem()] * (groups + 2),
+        in_specs=[vmem()] * (groups + 2),
         out_specs=(vmem(), vmem()),
         scratch_shapes=[pltpu.VMEM((width // LANES, members * (blocks + PAD), LANES), F32)],
         compiler_params=params(),
@@ -121,7 +158,7 @@
             transcendentals=0,
         ),
         name="packed_grams",
-    )(mem, *parts, scale, weighted)
+    )(*parts, scale, weighted)
 
 
 def blend_kernel(
@@ -257,7 +294,7 @@
     )(rows, tapers, *window)
 
 
-def apply_kernel(mem_ref, *refs, groups, share, blocks, width, unroll):
+def apply_kernel(*refs, groups, share, blocks, width, unroll):
     parts = refs[:groups]
     blend_ref = refs[groups]
     outs = refs[groups + 1 : 2 * groups + 1]
@@ -265,7 +302,7 @@
     members = groups * share
     tiles = width // LANES
     pitch = rows_ref.shape[1] // members
-    mem = mem_ref[0]
+    mem = lax.axis_index("mem")
     zero = jnp.zeros((blocks, width), F32)
     center = zero
     for d in range(groups):
@@ -318,7 +355,7 @@
         lax.fori_loop(0, share, finish, 0, unroll=4)
 
 
-def apply_blend(mem, parts, blend):
+def apply_blend(parts, blend):
     groups = len(parts)
     share, blocks, width = parts[0].shape
     members = groups * share
@@ -328,7 +365,7 @@
             apply_kernel, groups=groups, share=share, blocks=blocks, width=width, unroll=group_of(blocks)
         ),
         out_shape=(part,) * groups,
-        in_specs=[smem()] + [vmem()] * (groups + 1),
+        in_specs=[vmem()] * (groups + 1),
         out_specs=(vmem(),) * groups,
         scratch_shapes=[
             pltpu.VMEM((blocks, width), F32),
@@ -341,7 +378,7 @@
             transcendentals=0,
         ),
         name="apply_blend",
-    )(mem, *parts, blend)
+    )(*parts, blend)
 
 
 def taper_of(offset):
@@ -367,7 +404,7 @@
     assert groups & (groups - 1) == 0 and blocks == RADIUS
     mem = lax.axis_index("mem")
     lon = lax.axis_index("lon")
-    flip = (lon % 2) * (groups - 1)
+    flip = flip_of(groups)
     mine = mem ^ flip
     peers = [[(i, i ^ d) for i in range(groups)] for d in range(groups)]
     far_first = sorted(range(1, groups), key=lambda d: (d < groups // 2, d))
@@ -384,26 +421,32 @@
     chunks = range(CHUNKS)
     last = None
 
-    def piece(x, d, c):
+    def pieces(x, wanted):
         nonlocal last
-        if last is not None:
-            x, _ = lax.optimization_barrier((x, last))
-        start = ((mem ^ d) ^ flip) * blocks + c * size
-        last = lax.dynamic_slice_in_dim(x, start, size, 1)
-        return last
+        taken = {}
+        for d, c in wanted:
+            if last is not None:
+                x, _ = lax.optimization_barrier((x, last))
+            start = ((mem ^ d) ^ flip) * blocks + c * size
+            last = taken[d, c] = lax.dynamic_slice_in_dim(x, start, size, 1)
+        return taken
 
     def own_rows(x):
         return lax.dynamic_slice_in_dim(x, mine * blocks, blocks, 0)
 
-    def exchanged(x, c):
-        parts = {d: lax.ppermute(piece(x, d, c), "mem", peers[d]) for d in far_first}
-        parts[0] = piece(x, 0, c)
+    def exchanged(taken, c):
+        parts = {d: lax.ppermute(taken[d, c], "mem", peers[d]) for d in far_first}
+        parts[0] = taken[0, c]
         return [parts[d] for d in range(groups)]
 
-    spread_parts = [exchanged(scaled_sensor_spread, c) for c in chunks]
-    field_parts = [exchanged(prior_fields, c) for c in chunks]
-
-    mem_scalar = mem.astype(jnp.int32).reshape(1)
+    order = far_first + [0]
+    everything = [(d, c) for c in chunks for d in order]
+    (last,) = picked(scaled_sensor_spread, everything[:1], groups, size)
+    spread_taken = {everything[0]: last} | pieces(scaled_sensor_spread, everything[1:])
+    field_taken = pieces(prior_fields, everything)
+    spread_parts = [exchanged(spread_taken, c) for c in chunks]
+    field_parts = [exchanged(field_taken, c) for c in chunks]
+
     slot_ids = jnp.arange(width, dtype=jnp.int32)
     live = (slot_ids[None, :] < own_rows(active_sensor_number)[:, None]).astype(F32)
     obs_scale = jnp.sqrt(own_rows(inverse_error_variance) * live)
@@ -418,7 +461,7 @@
     left, own, right = [], [], []
     for c in chunks:
         here, packed = packed_grams(
-            mem_scalar, spread_parts[c], obs_scale, weighted, c * size
+            spread_parts[c], obs_scale, weighted, c * size
         )
         own.append(here)
         left.append(lax.ppermute(packed, ("mem", "lon"), forward))
@@ -428,7 +471,7 @@
     came = []
     for c in chunks:
         blend = blends(window_rows, tapers, window[c : c + 2 * CHUNKS + 1], members, c * size, size)
-        out_parts = apply_blend(mem_scalar, field_parts[c], blend)
+        out_parts = apply_blend(field_parts[c], blend)
         came.append((0, c, out_parts[0]))
         for d in far_first:
             came.append((d, c, lax.ppermute(out_parts[d], "mem", peers[d])))

time: 91.1 us -> 93.6 us (1.027)
  local copies, waits for them, and re-layouts: 18.1 us -> 21.4 us
  Pallas kernels: 21.1 us -> 19.8 us
    dynamic_slice x16 -> x15, local copies, waits for them, and re-layouts: 12 us -> 20.1 us  [pieces(): last = taken[d, c] = lax.dynamic_slice_in_dim(x, start, size, 1)]
    unnamed x19 -> x9, local copies, waits for them, and re-layouts: 4.9 us -> 0.1 us
    pallas_call x2, Pallas kernels: 5.07 us -> 3.2 us  [packed_grams(): pl.pallas_call(functools.partial(gram_kernel, groups=groups, share=share,...]
    pallas_call x0 -> x1, Pallas kernels: none -> 1.65 us  [picked(): pl.pallas_call(functools.partial(pick_kernel, wanted=tuple(wanted), group...]
    ppermute x12, starting transfers between devices: 7.56 us -> 5.95 us  [exchanged(): parts = {d: lax.ppermute(taken[d, c], 'mem', peers[d]) for d in far_first}]
    ppermute x12, waiting for transfers between devices: 9.05 us -> 7.54 us  [exchanged(): parts = {d: lax.ppermute(taken[d, c], 'mem', peers[d]) for d in far_first}]
    ppermute x6, starting transfers between devices: 4.6 us -> 5.69 us  [on_device(): came.append((d, c, lax.ppermute(out_parts[d], 'mem', peers[d])))]
    pallas_call x2, Pallas kernels: 3.66 us -> 2.62 us  [apply_blend(): pl.pallas_call(functools.partial(apply_kernel, groups=groups, share=share...]
  transfers between devices with their start and end apart: 22 -> 22, of which waited for: 5 -> 6; matrix products, arithmetic and copies ran while one was open for 14% -> 22% of each run, Pallas kernels for 23% -> 20%
where the time goes in v4:
time: 93.6 us; the launch traced here: 93 us
  waiting for transfers between devices  33 us (35%)
  local copies, waits for them, and re-layouts  21.4 us (23%)
  Pallas kernels  19.8 us (21%)
  starting transfers between devices  17.3 us (18%)
  other arithmetic  1.11 us (1%)
    dynamic_slice x15, local copies, waits for them, and re-layouts, pieces(): last = taken[d, c] = lax.dynamic_slice_in_dim(x, start, size, 1)  20.1 us
    ppermute x6, waiting for transfers between devices, on_device(): came.append((d, c, lax.ppermute(out_parts[d], 'mem', peers[d])))  15.9 us
    pallas_call x2, Pallas kernels, blends(): pl.pallas_call(functools.partial(blend_kernel, members=members, neighbour...  12.3 us
    ppermute x2, waiting for transfers between devices, on_device(): left.append(lax.ppermute(packed, ('mem', 'lon'), forward))  9.52 us
    ppermute x12, waiting for transfers between devices, exchanged(): parts = {d: lax.ppermute(taken[d, c], 'mem', peers[d]) for d in far_first}  7.54 us
    ppermute x12, starting transfers between devices, exchanged(): parts = {d: lax.ppermute(taken[d, c], 'mem', peers[d]) for d in far_first}  5.95 us
    ppermute x6, starting transfers between devices, on_device(): came.append((d, c, lax.ppermute(out_parts[d], 'mem', peers[d])))  5.69 us
    ppermute x2, starting transfers between devices, on_device(): right.append(lax.ppermute(packed, ('mem', 'lon'), backward))  5.62 us
  transfers between devices with their start and end apart: 22, of which 6 were waited for; matrix products, arithmetic and copies ran while one was open for 22% of the time, Pallas kernels for 20%

profile of v4, /device:TPU:0, one launch (start us, length us, event | category | flops | bytes accessed | tf_op | source)
XLA Modules:
  0.0 93.0 jit_solution(1887761794138235155)
XLA Ops:
  0.0 1.7 %picked.1 = bf16[20,24,256]{2,1,0:T(8,128)(2,1)} custom-call(bf16[20,192,256]{2,1,0:T(8,128)(2,1)} %whole_ref.1), custom_call_target="tpu_custom_call" | custom-call | bytes 491520 | tf_op jit(solution)/shard_map/picked/pallas_call | solution.py:59
  1.7 1.0 %constant_dynamic-slice_fusion.15 = bf16[20,24,256]{2,1,0:T(8,128)(2,1)S(1)} fusion(bf16[20,192,256]{2,1,0:T(8,128)(2,1)} %whole_ref.1, s32[]{:T(128)S(6)} %select_n.72), kind=kLoop, calls=%fused_computation.31 | loop fusion | bytes 491524 | tf_op jit(solution)/shard_map/dynamic_slice | solution.py:431
  2.6 2.5 %collective-permute-start.5 = (bf16[20,24,256]{2,1,0:T(8,128)(2,1)S(1)}, bf16[20,24,256]{2,1,0:T(8,128)(2,1)S(1)}, u32[]{:S(2)}, u32[]{:S(2)}) collective-permute-start(bf16[20,24,256]{2,1,0:T(8,128)(2,1)S(1)} %constant_dynamic-slice_fusion.15), channel_id=1, source_target_pairs={{0,24},{8,16},{16,8},{24,0},{1,25},{9,17},{17,9},{25,1},{2,26},{10... | collective-permute-start | bytes 737288 | tf_op jit(solution)/shard_map/ppermute | solution.py:438
  5.1 1.0 %constant_dynamic-slice_fusion.14 = bf16[20,24,256]{2,1,0:T(8,128)(2,1)S(1)} fusion(bf16[20,192,256]{2,1,0:T(8,128)(2,1)} %whole_ref.1, s32[]{:T(128)S(6)} %select_n.73), kind=kLoop, calls=%fused_computation.30 | loop fusion | bytes 491524 | tf_op jit(solution)/shard_map/dynamic_slice | solution.py:431
  6.1 0.7 collective-permute-start.3
  6.8 1.0 %constant_dynamic-slice_fusion.13.refs_0_ = bf16[20,24,256]{2,1,0:T(8,128)(2,1)S(1)} fusion(bf16[20,192,256]{2,1,0:T(8,128)(2,1)} %whole_ref.1, s32[]{:T(128)S(6)} %select_n.74), kind=kLoop, calls=%fused_computation.29 | loop fusion | bytes 491524 | tf_op jit(solution)/shard_map/dynamic_slice | solution.py:431
  7.8 1.7 %constant_dynamic-slice_fusion.12 = bf16[20,24,256]{2,1,0:T(8,128)(2,1)} fusion(bf16[20,192,256]{2,1,0:T(8,128)(2,1)} %whole_ref.1, s32[]{:T(128)S(6)} %select_n.75), kind=kLoop, calls=%fused_computation.28 | loop fusion | bytes 491524 | tf_op jit(solution)/shard_map/dynamic_slice | solution.py:431
  9.5 0.0 collective-permute-start.8
  9.5 1.0 %constant_dynamic-slice_fusion.11 = bf16[20,24,256]{2,1,0:T(8,128)(2,1)S(1)} fusion(bf16[20,192,256]{2,1,0:T(8,128)(2,1)} %whole_ref.1, s32[]{:T(128)S(6)} %select_n.76), kind=kLoop, calls=%fused_computation.27 | loop fusion | bytes 491524 | tf_op jit(solution)/shard_map/dynamic_slice | solution.py:431
  10.4 1.5 %collective-permute-start.9 = (bf16[20,24,256]{2,1,0:T(8,128)(2,1)S(1)}, bf16[20,24,256]{2,1,0:T(8,128)(2,1)S(1)}, u32[]{:S(2)}, u32[]{:S(2)}) collective-permute-start(bf16[20,24,256]{2,1,0:T(8,128)(2,1)S(1)} %constant_dynamic-slice_fusion.11), channel_id=1, source_target_pairs={{0,24},{8,16},{16,8},{24,0},{1,25},{9,17},{17,9},{25,1},{2,26},{10... | collective-permute-start | bytes 737288 | tf_op jit(solution)/shard_map/ppermute | solution.py:438
  11.9 1.7 %constant_dynamic-slice_fusion.10 = bf16[20,24,256]{2,1,0:T(8,128)(2,1)} fusion(bf16[20,192,256]{2,1,0:T(8,128)(2,1)} %whole_ref.1, s32[]{:T(128)S(6)} %select_n.77), kind=kLoop, calls=%fused_computation.26 | loop fusion | bytes 491524 | tf_op jit(solution)/shard_map/dynamic_slice | solution.py:431
  13.6 0.7 collective-permute-start.7
  14.3 1.0 %constant_dynamic-slice_fusion.9.refs_0_ = bf16[20,24,256]{2,1,0:T(8,128)(2,1)S(1)} fusion(bf16[20,192,256]{2,1,0:T(8,128)(2,1)} %whole_ref.1, s32[]{:T(128)S(6)} %select_n.78), kind=kLoop, calls=%fused_computation.25 | loop fusion | bytes 491524 | tf_op jit(solution)/shard_map/dynamic_slice | solution.py:431
  15.3 1.7 %constant_dynamic-slice_fusion.8 = bf16[20,24,256]{2,1,0:T(8,128)(2,1)} fusion(bf16[20,192,256]{2,1,0:T(8,128)(2,1)} %param.6, s32[]{:T(128)S(6)} %select_n.79), kind=kLoop, calls=%fused_computation.24 | loop fusion | bytes 491524 | tf_op jit(solution)/shard_map/dynamic_slice | solution.py:431
  17.0 1.7 %constant_dynamic-slice_fusion.7 = bf16[20,24,256]{2,1,0:T(8,128)(2,1)} fusion(bf16[20,192,256]{2,1,0:T(8,128)(2,1)} %param.6, s32[]{:T(128)S(6)} %select_n.72), kind=kLoop, calls=%fused_computation.23 | loop fusion | bytes 491524 | tf_op jit(solution)/shard_map/dynamic_slice | solution.py:431
  18.7 1.7 %constant_dynamic-slice_fusion.6 = bf16[20,24,256]{2,1,0:T(8,128)(2,1)} fusion(bf16[20,192,256]{2,1,0:T(8,128)(2,1)} %param.6, s32[]{:T(128)S(6)} %select_n.73), kind=kLoop, calls=%fused_computation.22 | loop fusion | bytes 491524 | tf_op jit(solution)/shard_map/dynamic_slice | solution.py:431
  20.3 1.0 %constant_dynamic-slice_fusion.5.refs_0_ = bf16[20,24,256]{2,1,0:T(8,128)(2,1)S(1)} fusion(bf16[20,192,256]{2,1,0:T(8,128)(2,1)} %param.6, s32[]{:T(128)S(6)} %select_n.74), kind=kLoop, calls=%fused_computation.21 | loop fusion | bytes 491524 | tf_op jit(solution)/shard_map/dynamic_slice | solution.py:431
  21.3 1.7 %constant_dynamic-slice_fusion.3 = bf16[20,24,256]{2,1,0:T(8,128)(2,1)} fusion(bf16[20,192,256]{2,1,0:T(8,128)(2,1)} %param.6, s32[]{:T(128)S(6)} %select_n.75), kind=kLoop, calls=%fused_computation.15 | loop fusion | bytes 491524 | tf_op jit(solution)/shard_map/dynamic_slice | solution.py:431
  23.0 1.7 %constant_dynamic-slice_fusion.2 = bf16[20,24,256]{2,1,0:T(8,128)(2,1)} fusion(bf16[20,192,256]{2,1,0:T(8,128)(2,1)} %param.6, s32[]{:T(128)S(6)} %select_n.76), kind=kLoop, calls=%fused_computation.14 | loop fusion | bytes 491524 | tf_op jit(solution)/shard_map/dynamic_slice | solution.py:431
  24.6 1.7 %constant_dynamic-slice_fusion.1 = bf16[20,24,256]{2,1,0:T(8,128)(2,1)} fusion(bf16[20,192,256]{2,1,0:T(8,128)(2,1)} %param.6, s32[]{:T(128)S(6)} %select_n.77), kind=kLoop, calls=%fused_computation.13 | loop fusion | bytes 491524 | tf_op jit(solution)/shard_map/dynamic_slice | solution.py:431
  26.3 0.0 collective-permute-start.4
  26.3 0.1 constant_dynamic-slice_fusion.4
  26.4 0.1 dynamic_slice.69
  26.5 0.9 dynamic-slice_multiply_fusion
  27.4 0.2 collective-permute-start
  27.6 6.6 %collective-permute-done.4.refs_2_ = bf16[20,24,256]{2,1,0:T(8,128)(2,1)S(1)} collective-permute-done((bf16[20,24,256]{2,1,0:T(8,128)(2,1)S(1)}, bf16[20,24,256]{2,1,0:T(8,128)(2,1)S(1)}, u32[]{:S(2)}, u32[]{:S(2)}) %collective-permute-start.4) | collective-permute-done | bytes 245792 | tf_op jit(solution)/shard_map/ppermute | solution.py:438
  34.2 0.0 collective-permute-start.2
  34.2 1.9 %packed_grams.2 = (f32[960,128]{1,0:T(8,128)S(1)}, bf16[960,128]{1,0:T(8,128)(2,1)}) custom-call(bf16[20,24,256]{2,1,0:T(8,128)(2,1)S(1)} %constant_dynamic-slice_fusion.13.refs_0_, bf16[20,24,256]{2,1,0:T(8,128)(2,1)S(1)} %collective-permute-done.3.refs_1_, bf16[20,24,256]{2,1,0:T(8,128)(2,1)S(1)} %collective-permute-done.4.refs_2_, ...), custom_call_target="tpu_custom_call" | custom-call | flops 125829120 | bytes 983040 | tf_op jit(solution)/shard_map/packed_grams/pallas_call | solution.py:140
  36.1 4.6 %collective-permute-start.11 = (bf16[960,128]{1,0:T(8,128)(2,1)}, bf16[960,128]{1,0:T(8,128)(2,1)S(1)}, u32[]{:S(2)}, u32[]{:S(2)}) collective-permute-start(bf16[960,128]{1,0:T(8,128)(2,1)} %get-tuple-element.43), channel_id=1, source_target_pairs={{0,7},{8,0},{16,8},{24,16},{25,24},{17,25},{9,17},{1,9},{2,1},{10,... | collective-permute-start | bytes 737288 | tf_op jit(solution)/shard_map/ppermute | solution.py:468
  40.7 0.0 collective-permute-done.9.refs_3_
  40.7 1.3 %packed_grams.3 = (f32[960,128]{1,0:T(8,128)S(1)}, bf16[960,128]{1,0:T(8,128)(2,1)S(1)}) custom-call(bf16[20,24,256]{2,1,0:T(8,128)(2,1)S(1)} %constant_dynamic-slice_fusion.9.refs_0_, bf16[20,24,256]{2,1,0:T(8,128)(2,1)S(1)} %collective-permute-done.7.refs_1_, bf16[20,24,256]{2,1,0:T(8,128)(2,1)S(1)} %collective-permute-done.8.refs_2_, ...), custom_call_target="tpu_custom_call" | custom-call | flops 125829120 | bytes 983040 | tf_op jit(solution)/shard_map/packed_grams/pallas_call | solution.py:140
  41.9 0.1 collective-permute-start.10
  42.0 0.1 copy.8
  42.1 0.1 add_multiply_fusion.row_ref
  42.2 0.1 collective-permute-start.17
  42.3 0.3 collective-permute-done.2.refs_3_
  42.6 0.3 collective-permute-start.16
  42.9 9.5 %collective-permute-done.10.refs_1_.refs_0_ = bf16[960,128]{1,0:T(8,128)(2,1)S(1)} collective-permute-done((bf16[960,128]{1,0:T(8,128)(2,1)S(1)}, bf16[960,128]{1,0:T(8,128)(2,1)S(1)}, u32[]{:S(2)}, u32[]{:S(2)}) %collective-permute-start.10) | collective-permute-done | bytes 245792 | tf_op jit(solution)/shard_map/ppermute | solution.py:467
  52.4 0.0 collective-permute-start.1
  52.4 0.0 collective-permute-done.6.refs_0_
  52.4 1.1 %collective-permute-start.18 = (bf16[960,128]{1,0:T(8,128)(2,1)S(1)}, bf16[960,128]{1,0:T(8,128)(2,1)S(1)}, u32[]{:S(2)}, u32[]{:S(2)}) collective-permute-start(bf16[960,128]{1,0:T(8,128)(2,1)S(1)} %get-tuple-element.44), channel_id=1, source_target_pairs={{0,7},{8,0},{16,8},{24,16},{25,24},{17,25},{9,17},{1,9},{2,1},{10,... | collective-permute-start | bytes 737288 | tf_op jit(solution)/shard_map/ppermute | solution.py:468
  53.5 0.1 add_divide_fusion.taper_ref
  53.6 6.2 %blends.2.refs_4_ = bf16[1920,128]{1,0:T(8,128)(2,1)S(1)} custom-call(s32[48,16]{1,0:T(8,128)S(1)} %add_multiply_fusion.row_ref, f32[48,16]{1,0:T(8,128)S(1)} %add_divide_fusion.taper_ref, bf16[960,128]{1,0:T(8,128)(2,1)S(1)} %collective-permute-done.6.refs_0_, bf16[960,128]{1,0:T(8,128)(2,1)S(1)} %collective-permute-done.10.refs_1_.refs_0_, ...), custom_call_target="tpu_custom_call" | custom-call | flops 471859200 | bytes 1843200 | tf_op jit(solution)/shard_map/blends/pallas_call | solution.py:274
  59.8 0.6 collective-permute-done.1.refs_2_
  60.4 1.3 %apply_blend.2 = (bf16[20,24,256]{2,1,0:T(8,128)(2,1)S(1)}, bf16[20,24,256]{2,1,0:T(8,128)(2,1)S(1)}, bf16[20,24,256]{2,1,0:T(8,128)(2,1)S(1)}, bf16[20,24,256]{2,1,0:T(8,128)(2,1)S(1)}) custom-call(bf16[20,24,256]{2,1,0:T(8,128)(2,1)S(1)} %constant_dynamic-slice_fusion.5.refs_0_, bf16[20,24,256]{2,1,0:T(8,128)(2,1)S(1)} %collective-permute-done.refs_1_, ...), custom_call_target="tpu_custom_call" | custom-call | flops 125829120 | bytes 1966080 | tf_op jit(solution)/shard_map/apply_blend/pallas_call | solution.py:363
  61.7 1.5 %collective-permute-start.12 = (bf16[20,24,256]{2,1,0:T(8,128)(2,1)S(1)}, bf16[20,24,256]{2,1,0:T(8,128)(2,1)S(1)}, u32[]{:S(2)}, u32[]{:S(2)}) collective-permute-start(bf16[20,24,256]{2,1,0:T(8,128)(2,1)S(1)} %get-tuple-element.48), channel_id=1, source_target_pairs={{0,8},{8,0},{16,24},{24,16},{1,9},{9,1},{17,25},{25,17},{2,10},{10... | collective-permute-start | bytes 737288 | tf_op jit(solution)/shard_map/ppermute | solution.py:477
  63.2 1.0 %constant_dynamic-slice_fusion.refs_0_ = bf16[20,24,256]{2,1,0:T(8,128)(2,1)S(1)} fusion(bf16[20,192,256]{2,1,0:T(8,128)(2,1)} %param.6, s32[]{:T(128)S(6)} %select_n.78), kind=kLoop, calls=%fused_computation.12 | loop fusion | bytes 491524 | tf_op jit(solution)/shard_map/dynamic_slice | solution.py:431
  64.2 2.1 %collective-permute-start.13 = (bf16[20,24,256]{2,1,0:T(8,128)(2,1)S(1)}, bf16[20,24,256]{2,1,0:T(8,128)(2,1)S(1)}, u32[]{:S(2)}, u32[]{:S(2)}) collective-permute-start(bf16[20,24,256]{2,1,0:T(8,128)(2,1)S(1)} %get-tuple-element.49), channel_id=1, source_target_pairs={{0,16},{8,24},{16,0},{24,8},{1,17},{9,25},{17,1},{25,9},{2,18},{10... | collective-permute-start | bytes 737288 | tf_op jit(solution)/shard_map/ppermute | solution.py:477
  66.3 6.2 %blends.3.refs_4_ = bf16[1920,128]{1,0:T(8,128)(2,1)S(1)} custom-call(s32[48,16]{1,0:T(8,128)S(1)} %add_multiply_fusion.row_ref, f32[48,16]{1,0:T(8,128)S(1)} %add_divide_fusion.taper_ref, bf16[960,128]{1,0:T(8,128)(2,1)S(1)} %collective-permute-done.10.refs_1_.refs_0_, f32[960,128]{1,0:T(8,128)S(1)} %get-tuple-element.45.refs_2_.refs_1_, ...), custom_call_target="tpu_custom_call" | custom-call | flops 471859200 | bytes 1843200 | tf_op jit(solution)/shard_map/blends/pallas_call | solution.py:274
  72.5 0.0 collective-permute-done.15.refs_1_
  72.5 0.0 collective-permute-done.17.refs_3_
  72.5 1.3 %apply_blend.3 = (bf16[20,24,256]{2,1,0:T(8,128)(2,1)S(1)}, bf16[20,24,256]{2,1,0:T(8,128)(2,1)S(1)}, bf16[20,24,256]{2,1,0:T(8,128)(2,1)S(1)}, bf16[20,24,256]{2,1,0:T(8,128)(2,1)S(1)}) custom-call(bf16[20,24,256]{2,1,0:T(8,128)(2,1)S(1)} %constant_dynamic-slice_fusion.refs_0_, bf16[20,24,256]{2,1,0:T(8,128)(2,1)S(1)} %collective-permute-done.15.refs_1_, ...), custom_call_target="tpu_custom_call" | custom-call | flops 125829120 | bytes 1966080 | tf_op jit(solution)/shard_map/apply_blend/pallas_call | solution.py:363
  73.9 0.1 collective-permute-start.19
  73.9 0.1 collective-permute-start.20
  74.0 1.8 %collective-permute-start.14 = (bf16[20,24,256]{2,1,0:T(8,128)(2,1)S(1)}, bf16[20,24,256]{2,1,0:T(8,128)(2,1)S(1)}, u32[]{:S(2)}, u32[]{:S(2)}) collective-permute-start(bf16[20,24,256]{2,1,0:T(8,128)(2,1)S(1)} %get-tuple-element.50), channel_id=1, source_target_pairs={{0,24},{8,16},{16,8},{24,0},{1,25},{9,17},{17,9},{25,1},{2,26},{10... | collective-permute-start | bytes 737288 | tf_op jit(solution)/shard_map/ppermute | solution.py:477
  75.8 0.2 broadcast_in_dim.2
  76.0 0.0 collective-permute-done.12
  76.0 0.1 collective-permute-start.21
  76.2 10.8 %collective-permute-done.14 = bf16[20,24,256]{2,1,0:T(8,128)(2,1)S(1)} collective-permute-done((bf16[20,24,256]{2,1,0:T(8,128)(2,1)S(1)}, bf16[20,24,256]{2,1,0:T(8,128)(2,1)S(1)}, u32[]{:S(2)}, u32[]{:S(2)}) %collective-permute-start.14) | collective-permute-done | bytes 245792 | tf_op jit(solution)/shard_map/ppermute | solution.py:477
  87.1 0.0 collective-permute-done.19
  87.1 0.0 collective-permute-done.20
  87.2 0.0 copy-start.1
  87.2 5.1 %collective-permute-done.21 = bf16[20,24,256]{2,1,0:T(8,128)(2,1)S(1)} collective-permute-done((bf16[20,24,256]{2,1,0:T(8,128)(2,1)S(1)}, bf16[20,24,256]{2,1,0:T(8,128)(2,1)S(1)}, u32[]{:S(2)}, u32[]{:S(2)}) %collective-permute-start.21) | collective-permute-done | bytes 245792 | tf_op jit(solution)/shard_map/ppermute | solution.py:477
  92.3 0.7 constant_dynamic-update-slice_fusion
  (26 shorter events, 0.2 us)
Async XLA Ops:
  0.0 26.3 %copy-start = (s32[192,16]{0,1:T(8,128)S(1)}, s32[192,16]{0,1:T(8,128)}, u32[]{:S(2)}) copy-start(s32[192,16]{0,1:T(8,128)} %param.11) | copy-start | bytes 36868
  2.6 24.7 %collective-permute-start.5 = (bf16[20,24,256]{2,1,0:T(8,128)(2,1)S(1)}, bf16[20,24,256]{2,1,0:T(8,128)(2,1)S(1)}, u32[]{:S(2)}, u32[]{:S(2)}) collective-permute-start(bf16[20,24,256]{2,1,0:T(8,128)(2,1)S(1)} %constant_dynamic-slice_fusion.15), channel_id=1, source_target_pairs={{0,24},{8,16},{16,8},{24,0},{1,25},{9,17},{17,9},{25,1},{2,26},{10... | collective-permute-start | bytes 737288 | tf_op jit(solution)/shard_map/ppermute | solution.py:438
  6.1 20.2 %collective-permute-start.3 = (bf16[20,24,256]{2,1,0:T(8,128)(2,1)S(1)}, bf16[20,24,256]{2,1,0:T(8,128)(2,1)S(1)}, u32[]{:S(2)}, u32[]{:S(2)}) collective-permute-start(bf16[20,24,256]{2,1,0:T(8,128)(2,1)S(1)} %constant_dynamic-slice_fusion.14), channel_id=1, source_target_pairs={{0,8},{8,0},{16,24},{24,16},{1,9},{9,1},{17,25},{25,17},{2,10},{10... | collective-permute-start | bytes 737288 | tf_op jit(solution)/shard_map/ppermute | solution.py:438
  9.5 31.2 %collective-permute-start.8 = (bf16[20,24,256]{2,1,0:T(8,128)(2,1)}, bf16[20,24,256]{2,1,0:T(8,128)(2,1)S(1)}, u32[]{:S(2)}, u32[]{:S(2)}) collective-permute-start(bf16[20,24,256]{2,1,0:T(8,128)(2,1)} %constant_dynamic-slice_fusion.12), channel_id=1, source_target_pairs={{0,16},{8,24},{16,0},{24,8},{1,17},{9,25},{17,1},{25,9},{2,18},{10... | collective-permute-start | bytes 737288 | tf_op jit(solution)/shard_map/ppermute | solution.py:438
  10.4 30.2 %collective-permute-start.9 = (bf16[20,24,256]{2,1,0:T(8,128)(2,1)S(1)}, bf16[20,24,256]{2,1,0:T(8,128)(2,1)S(1)}, u32[]{:S(2)}, u32[]{:S(2)}) collective-permute-start(bf16[20,24,256]{2,1,0:T(8,128)(2,1)S(1)} %constant_dynamic-slice_fusion.11), channel_id=1, source_target_pairs={{0,24},{8,16},{16,8},{24,0},{1,25},{9,17},{17,9},{25,1},{2,26},{10... | collective-permute-start | bytes 737288 | tf_op jit(solution)/shard_map/ppermute | solution.py:438
  13.6 22.5 %collective-permute-start.7 = (bf16[20,24,256]{2,1,0:T(8,128)(2,1)}, bf16[20,24,256]{2,1,0:T(8,128)(2,1)S(1)}, u32[]{:S(2)}, u32[]{:S(2)}) collective-permute-start(bf16[20,24,256]{2,1,0:T(8,128)(2,1)} %constant_dynamic-slice_fusion.10), channel_id=1, source_target_pairs={{0,8},{8,0},{16,24},{24,16},{1,9},{9,1},{17,25},{25,17},{2,10},{10... | collective-permute-start | bytes 737288 | tf_op jit(solution)/shard_map/ppermute | solution.py:438
  14.3 12.0 %copy-start.2 = (bf16[20,24,256]{2,1,0:T(8,128)(2,1)S(1)}, bf16[20,24,256]{2,1,0:T(8,128)(2,1)}, u32[]{:S(2)}) copy-start(bf16[20,24,256]{2,1,0:T(8,128)(2,1)} %picked.1) | copy-start | bytes 737284
  14.3 12.1 %copy-start.3 = (s32[192]{0:T(256)S(1)}, s32[192]{0:T(256)}, u32[]{:S(2)}) copy-start(s32[192]{0:T(256)} %param.10) | copy-start | bytes 2308
  26.3 7.9 %collective-permute-start.4 = (bf16[20,24,256]{2,1,0:T(8,128)(2,1)S(1)}, bf16[20,24,256]{2,1,0:T(8,128)(2,1)S(1)}, u32[]{:S(2)}, u32[]{:S(2)}) collective-permute-start(bf16[20,24,256]{2,1,0:T(8,128)(2,1)S(1)} %copy-done.2), channel_id=1, source_target_pairs={{0,16},{8,24},{16,0},{24,8},{1,17},{9,25},{17,1},{25,9},{2,18},{10... | collective-permute-start | bytes 737288 | tf_op jit(solution)/shard_map/ppermute | solution.py:438
  27.4 14.8 %collective-permute-start = (bf16[20,24,256]{2,1,0:T(8,128)(2,1)}, bf16[20,24,256]{2,1,0:T(8,128)(2,1)S(1)}, u32[]{:S(2)}, u32[]{:S(2)}) collective-permute-start(bf16[20,24,256]{2,1,0:T(8,128)(2,1)} %constant_dynamic-slice_fusion.6), channel_id=1, source_target_pairs={{0,8},{8,0},{16,24},{24,16},{1,9},{9,1},{17,25},{25,17},{2,10},{10... | collective-permute-start | bytes 737288 | tf_op jit(solution)/shard_map/ppermute | solution.py:438
  34.2 8.5 %collective-permute-start.2 = (bf16[20,24,256]{2,1,0:T(8,128)(2,1)}, bf16[20,24,256]{2,1,0:T(8,128)(2,1)S(1)}, u32[]{:S(2)}, u32[]{:S(2)}) collective-permute-start(bf16[20,24,256]{2,1,0:T(8,128)(2,1)} %constant_dynamic-slice_fusion.7), channel_id=1, source_target_pairs={{0,24},{8,16},{16,8},{24,0},{1,25},{9,17},{17,9},{25,1},{2,26},{10... | collective-permute-start | bytes 737288 | tf_op jit(solution)/shard_map/ppermute | solution.py:438
  36.1 16.3 %collective-permute-start.11 = (bf16[960,128]{1,0:T(8,128)(2,1)}, bf16[960,128]{1,0:T(8,128)(2,1)S(1)}, u32[]{:S(2)}, u32[]{:S(2)}) collective-permute-start(bf16[960,128]{1,0:T(8,128)(2,1)} %get-tuple-element.43), channel_id=1, source_target_pairs={{0,7},{8,0},{16,8},{24,16},{25,24},{17,25},{9,17},{1,9},{2,1},{10,... | collective-permute-start | bytes 737288 | tf_op jit(solution)/shard_map/ppermute | solution.py:468
  40.7 11.8 %collective-permute-start.6 = (bf16[960,128]{1,0:T(8,128)(2,1)}, bf16[960,128]{1,0:T(8,128)(2,1)S(1)}, u32[]{:S(2)}, u32[]{:S(2)}) collective-permute-start(bf16[960,128]{1,0:T(8,128)(2,1)} %get-tuple-element.43), channel_id=1, source_target_pairs={{0,8},{8,16},{16,24},{24,25},{25,17},{17,9},{9,1},{1,2},{2,10},{10... | collective-permute-start | bytes 737288 | tf_op jit(solution)/shard_map/ppermute | solution.py:467
  41.9 10.5 %collective-permute-start.10 = (bf16[960,128]{1,0:T(8,128)(2,1)S(1)}, bf16[960,128]{1,0:T(8,128)(2,1)S(1)}, u32[]{:S(2)}, u32[]{:S(2)}) collective-permute-start(bf16[960,128]{1,0:T(8,128)(2,1)S(1)} %get-tuple-element.44), channel_id=1, source_target_pairs={{0,8},{8,16},{16,24},{24,25},{25,17},{17,9},{9,1},{1,2},{2,10},{10... | collective-permute-start | bytes 737288 | tf_op jit(solution)/shard_map/ppermute | solution.py:467
  42.2 30.3 %collective-permute-start.17 = (bf16[20,24,256]{2,1,0:T(8,128)(2,1)}, bf16[20,24,256]{2,1,0:T(8,128)(2,1)S(1)}, u32[]{:S(2)}, u32[]{:S(2)}) collective-permute-start(bf16[20,24,256]{2,1,0:T(8,128)(2,1)} %constant_dynamic-slice_fusion.2), channel_id=1, source_target_pairs={{0,24},{8,16},{16,8},{24,0},{1,25},{9,17},{17,9},{25,1},{2,26},{10... | collective-permute-start | bytes 737288 | tf_op jit(solution)/shard_map/ppermute | solution.py:438
  42.6 29.9 %collective-permute-start.16 = (bf16[20,24,256]{2,1,0:T(8,128)(2,1)}, bf16[20,24,256]{2,1,0:T(8,128)(2,1)S(1)}, u32[]{:S(2)}, u32[]{:S(2)}) collective-permute-start(bf16[20,24,256]{2,1,0:T(8,128)(2,1)} %constant_dynamic-slice_fusion.3), channel_id=1, source_target_pairs={{0,16},{8,24},{16,0},{24,8},{1,17},{9,25},{17,1},{25,9},{2,18},{10... | collective-permute-start | bytes 737288 | tf_op jit(solution)/shard_map/ppermute | solution.py:438
  52.4 8.0 %collective-permute-start.1 = (bf16[20,24,256]{2,1,0:T(8,128)(2,1)}, bf16[20,24,256]{2,1,0:T(8,128)(2,1)S(1)}, u32[]{:S(2)}, u32[]{:S(2)}) collective-permute-start(bf16[20,24,256]{2,1,0:T(8,128)(2,1)} %constant_dynamic-slice_fusion.8), channel_id=1, source_target_pairs={{0,16},{8,24},{16,0},{24,8},{1,17},{9,25},{17,1},{25,9},{2,18},{10... | collective-permute-start | bytes 737288 | tf_op jit(solution)/shard_map/ppermute | solution.py:438
  52.4 20.1 %collective-permute-start.15 = (bf16[20,24,256]{2,1,0:T(8,128)(2,1)}, bf16[20,24,256]{2,1,0:T(8,128)(2,1)S(1)}, u32[]{:S(2)}, u32[]{:S(2)}) collective-permute-start(bf16[20,24,256]{2,1,0:T(8,128)(2,1)} %constant_dynamic-slice_fusion.1), channel_id=1, source_target_pairs={{0,8},{8,0},{16,24},{24,16},{1,9},{9,1},{17,25},{25,17},{2,10},{10... | collective-permute-start | bytes 737288 | tf_op jit(solution)/shard_map/ppermute | solution.py:438
  52.4 11.8 %collective-permute-start.18 = (bf16[960,128]{1,0:T(8,128)(2,1)S(1)}, bf16[960,128]{1,0:T(8,128)(2,1)S(1)}, u32[]{:S(2)}, u32[]{:S(2)}) collective-permute-start(bf16[960,128]{1,0:T(8,128)(2,1)S(1)} %get-tuple-element.44), channel_id=1, source_target_pairs={{0,7},{8,0},{16,8},{24,16},{25,24},{17,25},{9,17},{1,9},{2,1},{10,... | collective-permute-start | bytes 737288 | tf_op jit(solution)/shard_map/ppermute | solution.py:468
  61.7 14.3 %collective-permute-start.12 = (bf16[20,24,256]{2,1,0:T(8,128)(2,1)S(1)}, bf16[20,24,256]{2,1,0:T(8,128)(2,1)S(1)}, u32[]{:S(2)}, u32[]{:S(2)}) collective-permute-start(bf16[20,24,256]{2,1,0:T(8,128)(2,1)S(1)} %get-tuple-element.48), channel_id=1, source_target_pairs={{0,8},{8,0},{16,24},{24,16},{1,9},{9,1},{17,25},{25,17},{2,10},{10... | collective-permute-start | bytes 737288 | tf_op jit(solution)/shard_map/ppermute | solution.py:477
  64.2 12.0 %collective-permute-start.13 = (bf16[20,24,256]{2,1,0:T(8,128)(2,1)S(1)}, bf16[20,24,256]{2,1,0:T(8,128)(2,1)S(1)}, u32[]{:S(2)}, u32[]{:S(2)}) collective-permute-start(bf16[20,24,256]{2,1,0:T(8,128)(2,1)S(1)} %get-tuple-element.49), channel_id=1, source_target_pairs={{0,16},{8,24},{16,0},{24,8},{1,17},{9,25},{17,1},{25,9},{2,18},{10... | collective-permute-start | bytes 737288 | tf_op jit(solution)/shard_map/ppermute | solution.py:477
  73.9 13.2 %collective-permute-start.19 = (bf16[20,24,256]{2,1,0:T(8,128)(2,1)S(1)}, bf16[20,24,256]{2,1,0:T(8,128)(2,1)S(1)}, u32[]{:S(2)}, u32[]{:S(2)}) collective-permute-start(bf16[20,24,256]{2,1,0:T(8,128)(2,1)S(1)} %get-tuple-element.56), channel_id=1, source_target_pairs={{0,8},{8,0},{16,24},{24,16},{1,9},{9,1},{17,25},{25,17},{2,10},{10... | collective-permute-start | bytes 737288 | tf_op jit(solution)/shard_map/ppermute | solution.py:477
  73.9 13.2 %collective-permute-start.20 = (bf16[20,24,256]{2,1,0:T(8,128)(2,1)S(1)}, bf16[20,24,256]{2,1,0:T(8,128)(2,1)S(1)}, u32[]{:S(2)}, u32[]{:S(2)}) collective-permute-start(bf16[20,24,256]{2,1,0:T(8,128)(2,1)S(1)} %get-tuple-element.57), channel_id=1, source_target_pairs={{0,16},{8,24},{16,0},{24,8},{1,17},{9,25},{17,1},{25,9},{2,18},{10... | collective-permute-start | bytes 737288 | tf_op jit(solution)/shard_map/ppermute | solution.py:477
  74.0 13.0 %collective-permute-start.14 = (bf16[20,24,256]{2,1,0:T(8,128)(2,1)S(1)}, bf16[20,24,256]{2,1,0:T(8,128)(2,1)S(1)}, u32[]{:S(2)}, u32[]{:S(2)}) collective-permute-start(bf16[20,24,256]{2,1,0:T(8,128)(2,1)S(1)} %get-tuple-element.50), channel_id=1, source_target_pairs={{0,24},{8,16},{16,8},{24,0},{1,25},{9,17},{17,9},{25,1},{2,26},{10... | collective-permute-start | bytes 737288 | tf_op jit(solution)/shard_map/ppermute | solution.py:477
  76.0 16.3 %collective-permute-start.21 = (bf16[20,24,256]{2,1,0:T(8,128)(2,1)S(1)}, bf16[20,24,256]{2,1,0:T(8,128)(2,1)S(1)}, u32[]{:S(2)}, u32[]{:S(2)}) collective-permute-start(bf16[20,24,256]{2,1,0:T(8,128)(2,1)S(1)} %get-tuple-element.58), channel_id=1, source_target_pairs={{0,24},{8,16},{16,8},{24,0},{1,25},{9,17},{17,9},{25,1},{2,26},{10... | collective-permute-start | bytes 737288 | tf_op jit(solution)/shard_map/ppermute | solution.py:477
  87.2 5.1 %copy-start.1 = (bf16[20,192,256]{2,1,0:T(8,128)(2,1)}, bf16[20,192,256]{2,1,0:T(8,128)(2,1)S(1)}, u32[]{:S(2)}) copy-start(bf16[20,192,256]{2,1,0:T(8,128)(2,1)S(1)} %constant_dynamic-update-slice_fusion.1) | copy-start | bytes 5898244

commit v5 on v4

--- a/solution.py
+++ b/solution.py
@@ -72,6 +72,23 @@
     )(x)
 
 
+FOLD = 8
+
+
+def used_lanes(members):
+    return members + 5
+
+
+def low_lanes(members):
+    rows = members // 2 - FOLD
+    lane = lax.broadcasted_iota(jnp.int32, (rows, LANES), 1)
+    row = lax.broadcasted_iota(jnp.int32, (rows, LANES), 0)
+    first = used_lanes(members) - 2
+    turn = used_lanes(members) - (LANES - used_lanes(members))
+    folded = (row >= FOLD) & (row < 2 * FOLD) & (lane >= first + turn)
+    return ((lane >= first) & (lane < first + 2)) | (folded & (lane < first + 2 + turn))
+
+
 def gram_kernel(*refs, groups, share, blocks, width, unroll, first):
     parts = refs[:groups]
     scale_ref, weight_ref, own_ref, send_ref, rows_ref = refs[groups:]
@@ -93,10 +110,15 @@
 
         lax.fori_loop(0, share, scale_member, 0, unroll=4)
 
+    used = used_lanes(members)
+    spare = LANES - used
+    packed_rows = half - FOLD
     lane = lax.broadcasted_iota(jnp.int32, (half, LANES), 1)
-    pull_lane = members + half
-    from_top = (lane < members) | (lane == pull_lane) | (lane == pull_lane + 2)
-    spare = LANES - pull_lane
+    row = lax.broadcasted_iota(jnp.int32, (half, LANES), 0)
+    upper = (lane < half) & (lane > row)
+    c_diagonal = lane == row + half
+    from_bottom = (lane == members + 2) | (lane == members + 4)
+    in_use = lax.broadcasted_iota(jnp.int32, (FOLD, LANES), 1) < used
 
     def block_group(i, carry):
         for u in range(unroll):
@@ -104,30 +126,42 @@
             spread = jnp.concatenate(
                 [rows_ref[t, pl.ds(b, members, stride=pitch), :] for t in range(tiles)], axis=1
             )
-            weights = jnp.broadcast_to(weight_ref[pl.ds(first + b, 1), :], (spare, width))
-            right = jnp.concatenate([spread, spread[half:], weights], axis=0).astype(BF16)
+            weights = jnp.broadcast_to(weight_ref[pl.ds(first + b, 1), :], (8, width))
+            filler = jnp.zeros((LANES - members - 8, width), F32)
+            right = jnp.concatenate([spread, weights, filler], axis=0).astype(BF16)
             product = lax.dot_general(
                 spread.astype(BF16), right, (((1,), (1,)), ((), ())), preferred_element_type=F32
             )
-            packed = jnp.where(from_top, product[:half], product[half:])
-            own_ref[pl.ds(pl.multiple_of(b * half, 8), half), :] = packed
+            top, bottom = product[:half], product[half:]
+            diagonal = jnp.sum(jnp.where(c_diagonal, bottom, 0.0), axis=1, keepdims=True)
+            packed = jnp.where(upper, pltpu.roll(bottom, LANES - half, axis=1), top)
+            packed = jnp.where(from_bottom, bottom, packed)
+            packed = jnp.where(lane == members, diagonal, packed)
+            tail = packed[packed_rows:]
+            own_ref[pl.ds(pl.multiple_of(b * packed_rows, 8), packed_rows), :] = jnp.concatenate(
+                [
+                    jnp.where(in_use, packed[:FOLD], pltpu.roll(tail, used, axis=1)),
+                    jnp.where(
+                        in_use, packed[FOLD : 2 * FOLD], pltpu.roll(tail, used - spare, axis=1)
+                    ),
+                    packed[2 * FOLD : packed_rows],
+                ],
+                axis=0,
+            )
         return carry
 
     lax.fori_loop(0, blocks // unroll, block_group, 0)
-
-    step = 2 * half
-    lane2 = lax.broadcasted_iota(jnp.int32, (step, LANES), 1)
+    is_low = low_lanes(members)
 
     def finish(i, carry):
-        at = pl.ds(pl.multiple_of(i * step, 16), step)
+        at = pl.ds(pl.multiple_of(i * packed_rows, 16), packed_rows)
         value = own_ref[at, :]
         low = value - value.astype(BF16).astype(F32)
-        is_low = lane2 >= pull_lane + 2
         send_ref[at, :] = jnp.where(is_low, low, value).astype(BF16)
         own_ref[at, :] = jnp.where(is_low, 0.0, value)
         return carry
 
-    lax.fori_loop(0, blocks // 2, finish, 0, unroll=2)
+    lax.fori_loop(0, blocks, finish, 0, unroll=4)
 
 
 def packed_grams(parts, scale, weighted, first):
@@ -135,8 +169,10 @@
     share, blocks, width = parts[0].shape
     members = groups * share
     half = members // 2
-    assert members + half + 4 <= LANES and half % 8 == 0
-    flat = (blocks * half, LANES)
+    spare = LANES - used_lanes(members)
+    assert half % 8 == 0 and (half - FOLD) % 16 == 0 and half >= 3 * FOLD
+    assert spare >= used_lanes(members) - spare and members + 8 <= LANES
+    flat = (blocks * (half - FOLD), LANES)
     return pl.pallas_call(
         functools.partial(
             gram_kernel,
@@ -166,7 +202,9 @@
 ):
     *pieces, blend_ref, window_ref = refs
     half = members // 2
-    pull_lane = members + half
+    used = used_lanes(members)
+    spare = LANES - used
+    packed_rows = half - FOLD
     filled = 0
     for piece in pieces:
         window_ref[pl.ds(filled, piece.shape[0]), :] = piece[...].astype(F32)
@@ -177,7 +215,9 @@
     eye = (lane == row).astype(F32)
     in_matrix = lax.broadcasted_iota(jnp.int32, (1, LANES), 1) < members
     share_row = jnp.where(in_matrix, 1.0 / (members - 1), 0.0)
-    left_half = lax.broadcasted_iota(jnp.int32, (half, LANES), 1) < half
+    half_lane = lax.broadcasted_iota(jnp.int32, (half, LANES), 1)
+    half_row = lax.broadcasted_iota(jnp.int32, (half, LANES), 0)
+    in_first = lax.broadcasted_iota(jnp.int32, (FOLD, LANES), 1) < spare
     pad_rows = jnp.zeros((LANES - half, LANES), F32)
     pad_depth = jnp.zeros((LANES - members, LANES), BF16)
 
@@ -193,15 +233,23 @@
         packed = None
         for n in range(neighbours):
             start = pl.multiple_of(row_ref[first + b, n], 8)
-            term = taper_ref[first + b, n] * window_ref[pl.ds(start, half), :]
+            term = taper_ref[first + b, n] * window_ref[pl.ds(start, packed_rows), :]
             packed = term if packed is None else packed + term
+        tail = jnp.where(
+            in_first,
+            pltpu.roll(packed[:FOLD], LANES - used, axis=1),
+            pltpu.roll(packed[FOLD : 2 * FOLD], LANES - (used - spare), axis=1),
+        )
+        packed = jnp.concatenate([packed, tail], axis=0)
         turned = jnp.concatenate([packed, pad_rows], axis=0).T
-        low_rows = jnp.where(
-            left_half, turned[half:members], pltpu.roll(packed, LANES - half, axis=1)
-        )
-        pull = turned[pull_lane : pull_lane + 8]
-        pull_row = (pull[0:1] + pull[2:3]) + pltpu.roll(pull[1:2] + pull[3:4], half, axis=1)
-        return jnp.concatenate([packed, low_rows], axis=0) * share_row, pull_row
+        extra = turned[members : members + 8]
+        lower = turned[:half]
+        c_part = jnp.where(half_lane > half_row, packed, lower)
+        c_part = jnp.where(half_lane == half_row, extra[0:1], c_part)
+        top = jnp.where((half_lane > half_row) & (half_lane < half), lower, packed)
+        bottom = jnp.where(half_lane < half, turned[half:members], pltpu.roll(c_part, half, axis=1))
+        pull_row = (extra[1:2] + extra[3:4]) + pltpu.roll(extra[2:3] + extra[4:5], half, axis=1)
+        return jnp.concatenate([top, bottom], axis=0) * share_row, pull_row
 
     def block_group(i, carry):
         group = range(unroll)
@@ -455,7 +503,7 @@
     block_ids = lon * lon_rows + mine * blocks + local_ids
     offset_raw = jnp.mod(own_rows(adjacent_tiles) - block_ids[:, None], total_blocks)
     offset = jnp.where(offset_raw > total_blocks // 2, offset_raw - total_blocks, offset_raw)
-    window_rows = (local_ids[:, None] % size + RADIUS + offset) * half
+    window_rows = (local_ids[:, None] % size + RADIUS + offset) * (half - FOLD)
     tapers = taper_of(offset)
 
     left, own, right = [], [], []

time: 93.6 us -> 91 us (0.972)
  local copies, waits for them, and re-layouts: 21.4 us -> 19.3 us
  starting transfers between devices: 17.3 us -> 15.7 us
  Pallas kernels: 19.8 us -> 20.8 us
    dynamic_slice x15, local copies, waits for them, and re-layouts: 20.1 us -> 18 us  [pieces(): last = taken[d, c] = lax.dynamic_slice_in_dim(x, start, size, 1)]
    ppermute x12, waiting for transfers between devices: 7.54 us -> 8.93 us  [exchanged(): parts = {d: lax.ppermute(taken[d, c], 'mem', peers[d]) for d in far_first}]
    ppermute x2, waiting for transfers between devices: 9.52 us -> 8.26 us  [on_device(): left.append(lax.ppermute(packed, ('mem', 'lon'), forward))]
  transfers between devices with their start and end apart: 22 -> 22, of which waited for: 6 -> 5; matrix products, arithmetic and copies ran while one was open for 22% -> 21% of each run, Pallas kernels for 20% -> 21%
where the time goes in v5:
time: 91 us; the launch traced here: 90.4 us
  waiting for transfers between devices  33.1 us (36%)
  Pallas kernels  20.8 us (23%)
  local copies, waits for them, and re-layouts  19.3 us (21%)
  starting transfers between devices  15.7 us (17%)
  other arithmetic  1.11 us (1%)
    dynamic_slice x15, local copies, waits for them, and re-layouts, pieces(): last = taken[d, c] = lax.dynamic_slice_in_dim(x, start, size, 1)  18 us
    ppermute x6, waiting for transfers between devices, on_device(): came.append((d, c, lax.ppermute(out_parts[d], 'mem', peers[d])))  15.9 us
    pallas_call x2, Pallas kernels, blends(): pl.pallas_call(functools.partial(blend_kernel, members=members, neighbour...  12.9 us
    ppermute x12, waiting for transfers between devices, exchanged(): parts = {d: lax.ppermute(taken[d, c], 'mem', peers[d]) for d in far_first}  8.93 us
    ppermute x2, waiting for transfers between devices, on_device(): left.append(lax.ppermute(packed, ('mem', 'lon'), forward))  8.26 us
    ppermute x12, starting transfers between devices, exchanged(): parts = {d: lax.ppermute(taken[d, c], 'mem', peers[d]) for d in far_first}  5.77 us
    ppermute x6, starting transfers between devices, on_device(): came.append((d, c, lax.ppermute(out_parts[d], 'mem', peers[d])))  5.16 us
    ppermute x2, starting transfers between devices, on_device(): right.append(lax.ppermute(packed, ('mem', 'lon'), backward))  4.69 us
  transfers between devices with their start and end apart: 22, of which 5 were waited for; matrix products, arithmetic and copies ran while one was open for 21% of the time, Pallas kernels for 21%

profile of v5, /device:TPU:0, one launch (start us, length us, event | category | flops | bytes accessed | tf_op | source)
XLA Modules:
  0.0 90.4 jit_solution(10254308270913554053)
XLA Ops:
  0.0 1.7 %picked.1 = bf16[20,24,256]{2,1,0:T(8,128)(2,1)} custom-call(bf16[20,192,256]{2,1,0:T(8,128)(2,1)} %whole_ref.1), custom_call_target="tpu_custom_call" | custom-call | bytes 491520 | tf_op jit(solution)/shard_map/picked/pallas_call | solution.py:59
  1.7 1.0 %constant_dynamic-slice_fusion.15 = bf16[20,24,256]{2,1,0:T(8,128)(2,1)S(1)} fusion(bf16[20,192,256]{2,1,0:T(8,128)(2,1)} %whole_ref.1, s32[]{:T(128)S(6)} %select_n.72), kind=kLoop, calls=%fused_computation.31 | loop fusion | bytes 491524 | tf_op jit(solution)/shard_map/dynamic_slice | solution.py:479
  2.7 2.5 %collective-permute-start.5 = (bf16[20,24,256]{2,1,0:T(8,128)(2,1)S(1)}, bf16[20,24,256]{2,1,0:T(8,128)(2,1)S(1)}, u32[]{:S(2)}, u32[]{:S(2)}) collective-permute-start(bf16[20,24,256]{2,1,0:T(8,128)(2,1)S(1)} %constant_dynamic-slice_fusion.15), channel_id=1, source_target_pairs={{0,24},{8,16},{16,8},{24,0},{1,25},{9,17},{17,9},{25,1},{2,26},{10... | collective-permute-start | bytes 737288 | tf_op jit(solution)/shard_map/ppermute | solution.py:486
  5.1 1.0 %constant_dynamic-slice_fusion.14 = bf16[20,24,256]{2,1,0:T(8,128)(2,1)S(1)} fusion(bf16[20,192,256]{2,1,0:T(8,128)(2,1)} %whole_ref.1, s32[]{:T(128)S(6)} %select_n.73), kind=kLoop, calls=%fused_computation.30 | loop fusion | bytes 491524 | tf_op jit(solution)/shard_map/dynamic_slice | solution.py:479
  6.1 0.7 collective-permute-start.3
  6.8 1.0 %constant_dynamic-slice_fusion.13.refs_0_ = bf16[20,24,256]{2,1,0:T(8,128)(2,1)S(1)} fusion(bf16[20,192,256]{2,1,0:T(8,128)(2,1)} %whole_ref.1, s32[]{:T(128)S(6)} %select_n.74), kind=kLoop, calls=%fused_computation.29 | loop fusion | bytes 491524 | tf_op jit(solution)/shard_map/dynamic_slice | solution.py:479
  7.8 1.7 %constant_dynamic-slice_fusion.12 = bf16[20,24,256]{2,1,0:T(8,128)(2,1)} fusion(bf16[20,192,256]{2,1,0:T(8,128)(2,1)} %whole_ref.1, s32[]{:T(128)S(6)} %select_n.75), kind=kLoop, calls=%fused_computation.28 | loop fusion | bytes 491524 | tf_op jit(solution)/shard_map/dynamic_slice | solution.py:479
  9.5 0.0 collective-permute-start.8
  9.5 1.7 %constant_dynamic-slice_fusion.11 = bf16[20,24,256]{2,1,0:T(8,128)(2,1)} fusion(bf16[20,192,256]{2,1,0:T(8,128)(2,1)} %whole_ref.1, s32[]{:T(128)S(6)} %select_n.76), kind=kLoop, calls=%fused_computation.27 | loop fusion | bytes 491524 | tf_op jit(solution)/shard_map/dynamic_slice | solution.py:479
  11.1 1.4 %collective-permute-start.9 = (bf16[20,24,256]{2,1,0:T(8,128)(2,1)}, bf16[20,24,256]{2,1,0:T(8,128)(2,1)S(1)}, u32[]{:S(2)}, u32[]{:S(2)}) collective-permute-start(bf16[20,24,256]{2,1,0:T(8,128)(2,1)} %constant_dynamic-slice_fusion.11), channel_id=1, source_target_pairs={{0,24},{8,16},{16,8},{24,0},{1,25},{9,17},{17,9},{25,1},{2,26},{10... | collective-permute-start | bytes 737288 | tf_op jit(solution)/shard_map/ppermute | solution.py:486
  12.5 1.7 %constant_dynamic-slice_fusion.10 = bf16[20,24,256]{2,1,0:T(8,128)(2,1)} fusion(bf16[20,192,256]{2,1,0:T(8,128)(2,1)} %whole_ref.1, s32[]{:T(128)S(6)} %select_n.77), kind=kLoop, calls=%fused_computation.26 | loop fusion | bytes 491524 | tf_op jit(solution)/shard_map/dynamic_slice | solution.py:479
  14.2 0.7 collective-permute-start.7
  14.9 1.0 %constant_dynamic-slice_fusion.9.refs_0_ = bf16[20,24,256]{2,1,0:T(8,128)(2,1)S(1)} fusion(bf16[20,192,256]{2,1,0:T(8,128)(2,1)} %whole_ref.1, s32[]{:T(128)S(6)} %select_n.78), kind=kLoop, calls=%fused_computation.25 | loop fusion | bytes 491524 | tf_op jit(solution)/shard_map/dynamic_slice | solution.py:479
  15.9 1.0 %constant_dynamic-slice_fusion.8 = bf16[20,24,256]{2,1,0:T(8,128)(2,1)S(1)} fusion(bf16[20,192,256]{2,1,0:T(8,128)(2,1)} %param.6, s32[]{:T(128)S(6)} %select_n.79), kind=kLoop, calls=%fused_computation.24 | loop fusion | bytes 491524 | tf_op jit(solution)/shard_map/dynamic_slice | solution.py:479
  16.9 1.7 %constant_dynamic-slice_fusion.7 = bf16[20,24,256]{2,1,0:T(8,128)(2,1)} fusion(bf16[20,192,256]{2,1,0:T(8,128)(2,1)} %param.6, s32[]{:T(128)S(6)} %select_n.72), kind=kLoop, calls=%fused_computation.23 | loop fusion | bytes 491524 | tf_op jit(solution)/shard_map/dynamic_slice | solution.py:479
  18.5 1.7 %constant_dynamic-slice_fusion.6 = bf16[20,24,256]{2,1,0:T(8,128)(2,1)} fusion(bf16[20,192,256]{2,1,0:T(8,128)(2,1)} %param.6, s32[]{:T(128)S(6)} %select_n.73), kind=kLoop, calls=%fused_computation.22 | loop fusion | bytes 491524 | tf_op jit(solution)/shard_map/dynamic_slice | solution.py:479
  20.2 1.0 %constant_dynamic-slice_fusion.5.refs_0_ = bf16[20,24,256]{2,1,0:T(8,128)(2,1)S(1)} fusion(bf16[20,192,256]{2,1,0:T(8,128)(2,1)} %param.6, s32[]{:T(128)S(6)} %select_n.74), kind=kLoop, calls=%fused_computation.21 | loop fusion | bytes 491524 | tf_op jit(solution)/shard_map/dynamic_slice | solution.py:479
  21.2 1.0 %constant_dynamic-slice_fusion.3 = bf16[20,24,256]{2,1,0:T(8,128)(2,1)S(1)} fusion(bf16[20,192,256]{2,1,0:T(8,128)(2,1)} %param.6, s32[]{:T(128)S(6)} %select_n.75), kind=kLoop, calls=%fused_computation.15 | loop fusion | bytes 491524 | tf_op jit(solution)/shard_map/dynamic_slice | solution.py:479
  22.1 1.0 %constant_dynamic-slice_fusion.2 = bf16[20,24,256]{2,1,0:T(8,128)(2,1)S(1)} fusion(bf16[20,192,256]{2,1,0:T(8,128)(2,1)} %param.6, s32[]{:T(128)S(6)} %select_n.76), kind=kLoop, calls=%fused_computation.14 | loop fusion | bytes 491524 | tf_op jit(solution)/shard_map/dynamic_slice | solution.py:479
  23.1 0.1 constant_dynamic-slice_fusion.4
  23.2 1.0 %constant_dynamic-slice_fusion.1 = bf16[20,24,256]{2,1,0:T(8,128)(2,1)S(1)} fusion(bf16[20,192,256]{2,1,0:T(8,128)(2,1)} %param.6, s32[]{:T(128)S(6)} %select_n.77), kind=kLoop, calls=%fused_computation.13 | loop fusion | bytes 491524 | tf_op jit(solution)/shard_map/dynamic_slice | solution.py:479
  24.2 0.0 collective-permute-done.3.refs_1_
  24.2 0.1 collective-permute-start.4
  24.3 0.1 dynamic_slice.69
  24.4 0.1 copy.8
  24.5 0.9 %dynamic-slice_multiply_fusion = (f32[48,256]{1,0:T(8,128)S(1)}, f32[48,256]{1,0:T(8,128)S(1)}) fusion(f32[192,256]{1,0:T(8,128)} %param.8, s32[]{:T(128)S(6)} %select_n.74, f32[192,256]{1,0:T(8,128)} %param.9, s32[48]{0:T(128)S(1)} %dynamic_slice.69), kind=kLoop, calls=%fused_computation.1 | loop fusion | flops 36864 | bytes 196804 | tf_op jit(solution)/shard_map/mul | solution.py:501
  25.4 0.0 collective-permute-done.5.refs_3_
  25.4 0.2 collective-permute-start
  25.5 6.8 %collective-permute-done.4.refs_2_ = bf16[20,24,256]{2,1,0:T(8,128)(2,1)S(1)} collective-permute-done((bf16[20,24,256]{2,1,0:T(8,128)(2,1)}, bf16[20,24,256]{2,1,0:T(8,128)(2,1)S(1)}, u32[]{:S(2)}, u32[]{:S(2)}) %collective-permute-start.4) | collective-permute-done | bytes 245792 | tf_op jit(solution)/shard_map/ppermute | solution.py:486
  32.3 0.0 collective-permute-start.2
  32.3 1.8 %packed_grams.2 = (f32[768,128]{1,0:T(8,128)S(1)}, bf16[768,128]{1,0:T(8,128)(2,1)S(1)}) custom-call(bf16[20,24,256]{2,1,0:T(8,128)(2,1)S(1)} %constant_dynamic-slice_fusion.13.refs_0_, bf16[20,24,256]{2,1,0:T(8,128)(2,1)S(1)} %collective-permute-done.3.refs_1_, bf16[20,24,256]{2,1,0:T(8,128)(2,1)S(1)} %collective-permute-done.4.refs_2_, ...), custom_call_target="tpu_custom_call" | custom-call | flops 125829120 | bytes 983040 | tf_op jit(solution)/shard_map/packed_grams/pallas_call | solution.py:176
  34.2 0.0 collective-permute-done.7.refs_1_
  34.2 4.6 %collective-permute-start.11 = (bf16[768,128]{1,0:T(8,128)(2,1)S(1)}, bf16[768,128]{1,0:T(8,128)(2,1)S(1)}, u32[]{:S(2)}, u32[]{:S(2)}) collective-permute-start(bf16[768,128]{1,0:T(8,128)(2,1)S(1)} %get-tuple-element.43), channel_id=1, source_target_pairs={{0,7},{8,0},{16,8},{24,16},{25,24},{17,25},{9,17},{1,9},{2,1},{10,... | collective-permute-start | bytes 589832 | tf_op jit(solution)/shard_map/ppermute | solution.py:516
  38.8 0.0 collective-permute-done.9.refs_3_
  38.8 1.8 %packed_grams.3 = (f32[768,128]{1,0:T(8,128)S(1)}, bf16[768,128]{1,0:T(8,128)(2,1)S(1)}) custom-call(bf16[20,24,256]{2,1,0:T(8,128)(2,1)S(1)} %constant_dynamic-slice_fusion.9.refs_0_, bf16[20,24,256]{2,1,0:T(8,128)(2,1)S(1)} %collective-permute-done.7.refs_1_, bf16[20,24,256]{2,1,0:T(8,128)(2,1)S(1)} %collective-permute-done.8.refs_2_, ...), custom_call_target="tpu_custom_call" | custom-call | flops 125829120 | bytes 983040 | tf_op jit(solution)/shard_map/packed_grams/pallas_call | solution.py:176
  40.6 0.1 collective-permute-start.10
  40.7 0.1 add_multiply_fusion.row_ref
  40.8 0.0 collective-permute-done.refs_1_
  40.8 0.1 collective-permute-start.17
  40.9 0.1 collective-permute-start.16
  41.0 8.3 %collective-permute-done.10.refs_1_.refs_0_ = bf16[768,128]{1,0:T(8,128)(2,1)S(1)} collective-permute-done((bf16[768,128]{1,0:T(8,128)(2,1)S(1)}, bf16[768,128]{1,0:T(8,128)(2,1)S(1)}, u32[]{:S(2)}, u32[]{:S(2)}) %collective-permute-start.10) | collective-permute-done | bytes 196640 | tf_op jit(solution)/shard_map/ppermute | solution.py:515
  49.3 0.0 collective-permute-start.15
  49.3 0.0 collective-permute-done.6.refs_0_
  49.3 0.1 collective-permute-start.18
  49.4 0.1 add_divide_fusion.taper_ref
  49.5 6.4 %blends.2.refs_4_ = bf16[1920,128]{1,0:T(8,128)(2,1)S(1)} custom-call(s32[48,16]{1,0:T(8,128)S(1)} %add_multiply_fusion.row_ref, f32[48,16]{1,0:T(8,128)S(1)} %add_divide_fusion.taper_ref, bf16[768,128]{1,0:T(8,128)(2,1)S(1)} %collective-permute-done.6.refs_0_, bf16[768,128]{1,0:T(8,128)(2,1)S(1)} %collective-permute-done.10.refs_1_.refs_0_, ...), custom_call_target="tpu_custom_call" | custom-call | flops 471859200 | bytes 1474560 | tf_op jit(solution)/shard_map/blends/pallas_call | solution.py:322
  55.9 2.1 %collective-permute-done.1.refs_2_ = bf16[20,24,256]{2,1,0:T(8,128)(2,1)S(1)} collective-permute-done((bf16[20,24,256]{2,1,0:T(8,128)(2,1)S(1)}, bf16[20,24,256]{2,1,0:T(8,128)(2,1)S(1)}, u32[]{:S(2)}, u32[]{:S(2)}) %collective-permute-start.1) | collective-permute-done | bytes 245792 | tf_op jit(solution)/shard_map/ppermute | solution.py:486
  58.0 1.3 %apply_blend.2 = (bf16[20,24,256]{2,1,0:T(8,128)(2,1)S(1)}, bf16[20,24,256]{2,1,0:T(8,128)(2,1)S(1)}, bf16[20,24,256]{2,1,0:T(8,128)(2,1)S(1)}, bf16[20,24,256]{2,1,0:T(8,128)(2,1)S(1)}) custom-call(bf16[20,24,256]{2,1,0:T(8,128)(2,1)S(1)} %constant_dynamic-slice_fusion.5.refs_0_, bf16[20,24,256]{2,1,0:T(8,128)(2,1)S(1)} %collective-permute-done.refs_1_, ...), custom_call_target="tpu_custom_call" | custom-call | flops 125829120 | bytes 1966080 | tf_op jit(solution)/shard_map/apply_blend/pallas_call | solution.py:411
  59.3 0.9 collective-permute-start.12
  60.2 1.0 %constant_dynamic-slice_fusion.refs_0_ = bf16[20,24,256]{2,1,0:T(8,128)(2,1)S(1)} fusion(bf16[20,192,256]{2,1,0:T(8,128)(2,1)} %param.6, s32[]{:T(128)S(6)} %select_n.78), kind=kLoop, calls=%fused_computation.12 | loop fusion | bytes 491524 | tf_op jit(solution)/shard_map/dynamic_slice | solution.py:479
  61.2 2.3 %collective-permute-start.13 = (bf16[20,24,256]{2,1,0:T(8,128)(2,1)S(1)}, bf16[20,24,256]{2,1,0:T(8,128)(2,1)S(1)}, u32[]{:S(2)}, u32[]{:S(2)}) collective-permute-start(bf16[20,24,256]{2,1,0:T(8,128)(2,1)S(1)} %get-tuple-element.49), channel_id=1, source_target_pairs={{0,16},{8,24},{16,0},{24,8},{1,17},{9,25},{17,1},{25,9},{2,18},{10... | collective-permute-start | bytes 737288 | tf_op jit(solution)/shard_map/ppermute | solution.py:525
  63.4 6.4 %blends.3.refs_4_ = bf16[1920,128]{1,0:T(8,128)(2,1)S(1)} custom-call(s32[48,16]{1,0:T(8,128)S(1)} %add_multiply_fusion.row_ref, f32[48,16]{1,0:T(8,128)S(1)} %add_divide_fusion.taper_ref, bf16[768,128]{1,0:T(8,128)(2,1)S(1)} %collective-permute-done.10.refs_1_.refs_0_, f32[768,128]{1,0:T(8,128)S(1)} %get-tuple-element.45.refs_2_.refs_1_, ...), custom_call_target="tpu_custom_call" | custom-call | flops 471859200 | bytes 1474560 | tf_op jit(solution)/shard_map/blends/pallas_call | solution.py:322
  69.9 0.0 collective-permute-done.15.refs_1_
  69.9 0.0 collective-permute-done.17.refs_3_
  69.9 1.3 %apply_blend.3 = (bf16[20,24,256]{2,1,0:T(8,128)(2,1)S(1)}, bf16[20,24,256]{2,1,0:T(8,128)(2,1)S(1)}, bf16[20,24,256]{2,1,0:T(8,128)(2,1)S(1)}, bf16[20,24,256]{2,1,0:T(8,128)(2,1)S(1)}) custom-call(bf16[20,24,256]{2,1,0:T(8,128)(2,1)S(1)} %constant_dynamic-slice_fusion.refs_0_, bf16[20,24,256]{2,1,0:T(8,128)(2,1)S(1)} %collective-permute-done.15.refs_1_, ...), custom_call_target="tpu_custom_call" | custom-call | flops 125829120 | bytes 1966080 | tf_op jit(solution)/shard_map/apply_blend/pallas_call | solution.py:411
  71.3 0.1 collective-permute-start.19
  71.3 0.1 collective-permute-start.20
  71.4 1.8 %collective-permute-start.14 = (bf16[20,24,256]{2,1,0:T(8,128)(2,1)S(1)}, bf16[20,24,256]{2,1,0:T(8,128)(2,1)S(1)}, u32[]{:S(2)}, u32[]{:S(2)}) collective-permute-start(bf16[20,24,256]{2,1,0:T(8,128)(2,1)S(1)} %get-tuple-element.50), channel_id=1, source_target_pairs={{0,24},{8,16},{16,8},{24,0},{1,25},{9,17},{17,9},{25,1},{2,26},{10... | collective-permute-start | bytes 737288 | tf_op jit(solution)/shard_map/ppermute | solution.py:525
  73.2 0.2 broadcast_in_dim.2
  73.4 0.1 collective-permute-start.21
  73.6 10.8 %collective-permute-done.14 = bf16[20,24,256]{2,1,0:T(8,128)(2,1)S(1)} collective-permute-done((bf16[20,24,256]{2,1,0:T(8,128)(2,1)S(1)}, bf16[20,24,256]{2,1,0:T(8,128)(2,1)S(1)}, u32[]{:S(2)}, u32[]{:S(2)}) %collective-permute-start.14) | collective-permute-done | bytes 245792 | tf_op jit(solution)/shard_map/ppermute | solution.py:525
  84.6 0.0 copy-start.1
  84.6 5.1 %collective-permute-done.21 = bf16[20,24,256]{2,1,0:T(8,128)(2,1)S(1)} collective-permute-done((bf16[20,24,256]{2,1,0:T(8,128)(2,1)S(1)}, bf16[20,24,256]{2,1,0:T(8,128)(2,1)S(1)}, u32[]{:S(2)}, u32[]{:S(2)}) %collective-permute-start.21) | collective-permute-done | bytes 245792 | tf_op jit(solution)/shard_map/ppermute | solution.py:525
  89.7 0.7 constant_dynamic-update-slice_fusion
  (24 shorter events, 0.2 us)
Async XLA Ops:
  0.0 23.1 %copy-start = (s32[192,16]{0,1:T(8,128)S(1)}, s32[192,16]{0,1:T(8,128)}, u32[]{:S(2)}) copy-start(s32[192,16]{0,1:T(8,128)} %param.11) | copy-start | bytes 36868
  2.7 22.7 %collective-permute-start.5 = (bf16[20,24,256]{2,1,0:T(8,128)(2,1)S(1)}, bf16[20,24,256]{2,1,0:T(8,128)(2,1)S(1)}, u32[]{:S(2)}, u32[]{:S(2)}) collective-permute-start(bf16[20,24,256]{2,1,0:T(8,128)(2,1)S(1)} %constant_dynamic-slice_fusion.15), channel_id=1, source_target_pairs={{0,24},{8,16},{16,8},{24,0},{1,25},{9,17},{17,9},{25,1},{2,26},{10... | collective-permute-start | bytes 737288 | tf_op jit(solution)/shard_map/ppermute | solution.py:486
  6.1 18.1 %collective-permute-start.3 = (bf16[20,24,256]{2,1,0:T(8,128)(2,1)S(1)}, bf16[20,24,256]{2,1,0:T(8,128)(2,1)S(1)}, u32[]{:S(2)}, u32[]{:S(2)}) collective-permute-start(bf16[20,24,256]{2,1,0:T(8,128)(2,1)S(1)} %constant_dynamic-slice_fusion.14), channel_id=1, source_target_pairs={{0,8},{8,0},{16,24},{24,16},{1,9},{9,1},{17,25},{25,17},{2,10},{10... | collective-permute-start | bytes 737288 | tf_op jit(solution)/shard_map/ppermute | solution.py:486
  9.5 29.3 %collective-permute-start.8 = (bf16[20,24,256]{2,1,0:T(8,128)(2,1)}, bf16[20,24,256]{2,1,0:T(8,128)(2,1)S(1)}, u32[]{:S(2)}, u32[]{:S(2)}) collective-permute-start(bf16[20,24,256]{2,1,0:T(8,128)(2,1)} %constant_dynamic-slice_fusion.12), channel_id=1, source_target_pairs={{0,16},{8,24},{16,0},{24,8},{1,17},{9,25},{17,1},{25,9},{2,18},{10... | collective-permute-start | bytes 737288 | tf_op jit(solution)/shard_map/ppermute | solution.py:486
  11.1 27.7 %collective-permute-start.9 = (bf16[20,24,256]{2,1,0:T(8,128)(2,1)}, bf16[20,24,256]{2,1,0:T(8,128)(2,1)S(1)}, u32[]{:S(2)}, u32[]{:S(2)}) collective-permute-start(bf16[20,24,256]{2,1,0:T(8,128)(2,1)} %constant_dynamic-slice_fusion.11), channel_id=1, source_target_pairs={{0,24},{8,16},{16,8},{24,0},{1,25},{9,17},{17,9},{25,1},{2,26},{10... | collective-permute-start | bytes 737288 | tf_op jit(solution)/shard_map/ppermute | solution.py:486
  14.2 20.0 %collective-permute-start.7 = (bf16[20,24,256]{2,1,0:T(8,128)(2,1)}, bf16[20,24,256]{2,1,0:T(8,128)(2,1)S(1)}, u32[]{:S(2)}, u32[]{:S(2)}) collective-permute-start(bf16[20,24,256]{2,1,0:T(8,128)(2,1)} %constant_dynamic-slice_fusion.10), channel_id=1, source_target_pairs={{0,8},{8,0},{16,24},{24,16},{1,9},{9,1},{17,25},{25,17},{2,10},{10... | collective-permute-start | bytes 737288 | tf_op jit(solution)/shard_map/ppermute | solution.py:486
  14.9 9.4 %copy-start.2 = (s32[192]{0:T(256)S(1)}, s32[192]{0:T(256)}, u32[]{:S(2)}) copy-start(s32[192]{0:T(256)} %param.10) | copy-start | bytes 2308
  24.2 8.1 %collective-permute-start.4 = (bf16[20,24,256]{2,1,0:T(8,128)(2,1)}, bf16[20,24,256]{2,1,0:T(8,128)(2,1)S(1)}, u32[]{:S(2)}, u32[]{:S(2)}) collective-permute-start(bf16[20,24,256]{2,1,0:T(8,128)(2,1)} %picked.1), channel_id=1, source_target_pairs={{0,16},{8,24},{16,0},{24,8},{1,17},{9,25},{17,1},{25,9},{2,18},{10... | collective-permute-start | bytes 737288 | tf_op jit(solution)/shard_map/ppermute | solution.py:486
  25.4 15.4 %collective-permute-start = (bf16[20,24,256]{2,1,0:T(8,128)(2,1)}, bf16[20,24,256]{2,1,0:T(8,128)(2,1)S(1)}, u32[]{:S(2)}, u32[]{:S(2)}) collective-permute-start(bf16[20,24,256]{2,1,0:T(8,128)(2,1)} %constant_dynamic-slice_fusion.6), channel_id=1, source_target_pairs={{0,8},{8,0},{16,24},{24,16},{1,9},{9,1},{17,25},{25,17},{2,10},{10... | collective-permute-start | bytes 737288 | tf_op jit(solution)/shard_map/ppermute | solution.py:486
  32.3 8.6 %collective-permute-start.2 = (bf16[20,24,256]{2,1,0:T(8,128)(2,1)}, bf16[20,24,256]{2,1,0:T(8,128)(2,1)S(1)}, u32[]{:S(2)}, u32[]{:S(2)}) collective-permute-start(bf16[20,24,256]{2,1,0:T(8,128)(2,1)} %constant_dynamic-slice_fusion.7), channel_id=1, source_target_pairs={{0,24},{8,16},{16,8},{24,0},{1,25},{9,17},{17,9},{25,1},{2,26},{10... | collective-permute-start | bytes 737288 | tf_op jit(solution)/shard_map/ppermute | solution.py:486
  34.2 15.1 %collective-permute-start.11 = (bf16[768,128]{1,0:T(8,128)(2,1)S(1)}, bf16[768,128]{1,0:T(8,128)(2,1)S(1)}, u32[]{:S(2)}, u32[]{:S(2)}) collective-permute-start(bf16[768,128]{1,0:T(8,128)(2,1)S(1)} %get-tuple-element.43), channel_id=1, source_target_pairs={{0,7},{8,0},{16,8},{24,16},{25,24},{17,25},{9,17},{1,9},{2,1},{10,... | collective-permute-start | bytes 589832 | tf_op jit(solution)/shard_map/ppermute | solution.py:516
  38.8 10.5 %collective-permute-start.6 = (bf16[768,128]{1,0:T(8,128)(2,1)S(1)}, bf16[768,128]{1,0:T(8,128)(2,1)S(1)}, u32[]{:S(2)}, u32[]{:S(2)}) collective-permute-start(bf16[768,128]{1,0:T(8,128)(2,1)S(1)} %get-tuple-element.43), channel_id=1, source_target_pairs={{0,8},{8,16},{16,24},{24,25},{25,17},{17,9},{9,1},{1,2},{2,10},{10... | collective-permute-start | bytes 589832 | tf_op jit(solution)/shard_map/ppermute | solution.py:515
  40.6 8.6 %collective-permute-start.10 = (bf16[768,128]{1,0:T(8,128)(2,1)S(1)}, bf16[768,128]{1,0:T(8,128)(2,1)S(1)}, u32[]{:S(2)}, u32[]{:S(2)}) collective-permute-start(bf16[768,128]{1,0:T(8,128)(2,1)S(1)} %get-tuple-element.44), channel_id=1, source_target_pairs={{0,8},{8,16},{16,24},{24,25},{25,17},{17,9},{9,1},{1,2},{2,10},{10... | collective-permute-start | bytes 589832 | tf_op jit(solution)/shard_map/ppermute | solution.py:515
  40.8 29.1 %collective-permute-start.17 = (bf16[20,24,256]{2,1,0:T(8,128)(2,1)S(1)}, bf16[20,24,256]{2,1,0:T(8,128)(2,1)S(1)}, u32[]{:S(2)}, u32[]{:S(2)}) collective-permute-start(bf16[20,24,256]{2,1,0:T(8,128)(2,1)S(1)} %constant_dynamic-slice_fusion.2), channel_id=1, source_target_pairs={{0,24},{8,16},{16,8},{24,0},{1,25},{9,17},{17,9},{25,1},{2,26},{10... | collective-permute-start | bytes 737288 | tf_op jit(solution)/shard_map/ppermute | solution.py:486
  40.9 29.0 %collective-permute-start.16 = (bf16[20,24,256]{2,1,0:T(8,128)(2,1)S(1)}, bf16[20,24,256]{2,1,0:T(8,128)(2,1)S(1)}, u32[]{:S(2)}, u32[]{:S(2)}) collective-permute-start(bf16[20,24,256]{2,1,0:T(8,128)(2,1)S(1)} %constant_dynamic-slice_fusion.3), channel_id=1, source_target_pairs={{0,16},{8,24},{16,0},{24,8},{1,17},{9,25},{17,1},{25,9},{2,18},{10... | collective-permute-start | bytes 737288 | tf_op jit(solution)/shard_map/ppermute | solution.py:486
  49.3 8.8 %collective-permute-start.1 = (bf16[20,24,256]{2,1,0:T(8,128)(2,1)S(1)}, bf16[20,24,256]{2,1,0:T(8,128)(2,1)S(1)}, u32[]{:S(2)}, u32[]{:S(2)}) collective-permute-start(bf16[20,24,256]{2,1,0:T(8,128)(2,1)S(1)} %constant_dynamic-slice_fusion.8), channel_id=1, source_target_pairs={{0,16},{8,24},{16,0},{24,8},{1,17},{9,25},{17,1},{25,9},{2,18},{10... | collective-permute-start | bytes 737288 | tf_op jit(solution)/shard_map/ppermute | solution.py:486
  49.3 20.6 %collective-permute-start.15 = (bf16[20,24,256]{2,1,0:T(8,128)(2,1)S(1)}, bf16[20,24,256]{2,1,0:T(8,128)(2,1)S(1)}, u32[]{:S(2)}, u32[]{:S(2)}) collective-permute-start(bf16[20,24,256]{2,1,0:T(8,128)(2,1)S(1)} %constant_dynamic-slice_fusion.1), channel_id=1, source_target_pairs={{0,8},{8,0},{16,24},{24,16},{1,9},{9,1},{17,25},{25,17},{2,10},{10... | collective-permute-start | bytes 737288 | tf_op jit(solution)/shard_map/ppermute | solution.py:486
  49.3 11.9 %collective-permute-start.18 = (bf16[768,128]{1,0:T(8,128)(2,1)S(1)}, bf16[768,128]{1,0:T(8,128)(2,1)S(1)}, u32[]{:S(2)}, u32[]{:S(2)}) collective-permute-start(bf16[768,128]{1,0:T(8,128)(2,1)S(1)} %get-tuple-element.44), channel_id=1, source_target_pairs={{0,7},{8,0},{16,8},{24,16},{25,24},{17,25},{9,17},{1,9},{2,1},{10,... | collective-permute-start | bytes 589832 | tf_op jit(solution)/shard_map/ppermute | solution.py:516
  59.3 14.1 %collective-permute-start.12 = (bf16[20,24,256]{2,1,0:T(8,128)(2,1)S(1)}, bf16[20,24,256]{2,1,0:T(8,128)(2,1)S(1)}, u32[]{:S(2)}, u32[]{:S(2)}) collective-permute-start(bf16[20,24,256]{2,1,0:T(8,128)(2,1)S(1)} %get-tuple-element.48), channel_id=1, source_target_pairs={{0,8},{8,0},{16,24},{24,16},{1,9},{9,1},{17,25},{25,17},{2,10},{10... | collective-permute-start | bytes 737288 | tf_op jit(solution)/shard_map/ppermute | solution.py:525
  61.2 12.4 %collective-permute-start.13 = (bf16[20,24,256]{2,1,0:T(8,128)(2,1)S(1)}, bf16[20,24,256]{2,1,0:T(8,128)(2,1)S(1)}, u32[]{:S(2)}, u32[]{:S(2)}) collective-permute-start(bf16[20,24,256]{2,1,0:T(8,128)(2,1)S(1)} %get-tuple-element.49), channel_id=1, source_target_pairs={{0,16},{8,24},{16,0},{24,8},{1,17},{9,25},{17,1},{25,9},{2,18},{10... | collective-permute-start | bytes 737288 | tf_op jit(solution)/shard_map/ppermute | solution.py:525
  71.3 13.2 %collective-permute-start.19 = (bf16[20,24,256]{2,1,0:T(8,128)(2,1)S(1)}, bf16[20,24,256]{2,1,0:T(8,128)(2,1)S(1)}, u32[]{:S(2)}, u32[]{:S(2)}) collective-permute-start(bf16[20,24,256]{2,1,0:T(8,128)(2,1)S(1)} %get-tuple-element.56), channel_id=1, source_target_pairs={{0,8},{8,0},{16,24},{24,16},{1,9},{9,1},{17,25},{25,17},{2,10},{10... | collective-permute-start | bytes 737288 | tf_op jit(solution)/shard_map/ppermute | solution.py:525
  71.3 13.2 %collective-permute-start.20 = (bf16[20,24,256]{2,1,0:T(8,128)(2,1)S(1)}, bf16[20,24,256]{2,1,0:T(8,128)(2,1)S(1)}, u32[]{:S(2)}, u32[]{:S(2)}) collective-permute-start(bf16[20,24,256]{2,1,0:T(8,128)(2,1)S(1)} %get-tuple-element.57), channel_id=1, source_target_pairs={{0,16},{8,24},{16,0},{24,8},{1,17},{9,25},{17,1},{25,9},{2,18},{10... | collective-permute-start | bytes 737288 | tf_op jit(solution)/shard_map/ppermute | solution.py:525
  71.4 13.0 %collective-permute-start.14 = (bf16[20,24,256]{2,1,0:T(8,128)(2,1)S(1)}, bf16[20,24,256]{2,1,0:T(8,128)(2,1)S(1)}, u32[]{:S(2)}, u32[]{:S(2)}) collective-permute-start(bf16[20,24,256]{2,1,0:T(8,128)(2,1)S(1)} %get-tuple-element.50), channel_id=1, source_target_pairs={{0,24},{8,16},{16,8},{24,0},{1,25},{9,17},{17,9},{25,1},{2,26},{10... | collective-permute-start | bytes 737288 | tf_op jit(solution)/shard_map/ppermute | solution.py:525
  73.4 16.3 %collective-permute-start.21 = (bf16[20,24,256]{2,1,0:T(8,128)(2,1)S(1)}, bf16[20,24,256]{2,1,0:T(8,128)(2,1)S(1)}, u32[]{:S(2)}, u32[]{:S(2)}) collective-permute-start(bf16[20,24,256]{2,1,0:T(8,128)(2,1)S(1)} %get-tuple-element.58), channel_id=1, source_target_pairs={{0,24},{8,16},{16,8},{24,0},{1,25},{9,17},{17,9},{25,1},{2,26},{10... | collective-permute-start | bytes 737288 | tf_op jit(solution)/shard_map/ppermute | solution.py:525
  84.6 5.1 %copy-start.1 = (bf16[20,192,256]{2,1,0:T(8,128)(2,1)}, bf16[20,192,256]{2,1,0:T(8,128)(2,1)S(1)}, u32[]{:S(2)}) copy-start(bf16[20,192,256]{2,1,0:T(8,128)(2,1)S(1)} %constant_dynamic-update-slice_fusion.1) | copy-start | bytes 5898244

commit v6 on v5

--- a/solution.py
+++ b/solution.py
@@ -489,8 +489,10 @@
 
     order = far_first + [0]
     everything = [(d, c) for c in chunks for d in order]
-    (last,) = picked(scaled_sensor_spread, everything[:1], groups, size)
-    spread_taken = {everything[0]: last} | pieces(scaled_sensor_spread, everything[1:])
+    spread_taken = pieces(scaled_sensor_spread, everything[:1])
+    gated, _ = lax.optimization_barrier((scaled_sensor_spread, last))
+    (last,) = picked(gated, everything[1:2], groups, size)
+    spread_taken |= {everything[1]: last} | pieces(scaled_sensor_spread, everything[2:])
     field_taken = pieces(prior_fields, everything)
     spread_parts = [exchanged(spread_taken, c) for c in chunks]
     field_parts = [exchanged(field_taken, c) for c in chunks]

time: 91 us -> 90.8 us (level)
  no operation moved by 1% of the time
where the time goes in v6:
time: 90.8 us; the launch traced here: 90.2 us
  waiting for transfers between devices  32.9 us (36%)
  Pallas kernels  20.8 us (23%)
  local copies, waits for them, and re-layouts  19.3 us (21%)
  starting transfers between devices  15.7 us (17%)
  other arithmetic  1.11 us (1%)
    dynamic_slice x15, local copies, waits for them, and re-layouts, pieces(): last = taken[d, c] = lax.dynamic_slice_in_dim(x, start, size, 1)  18 us
    ppermute x6, waiting for transfers between devices, on_device(): came.append((d, c, lax.ppermute(out_parts[d], 'mem', peers[d])))  15.9 us
    pallas_call x2, Pallas kernels, blends(): pl.pallas_call(functools.partial(blend_kernel, members=members, neighbour...  12.9 us
    ppermute x12, waiting for transfers between devices, exchanged(): parts = {d: lax.ppermute(taken[d, c], 'mem', peers[d]) for d in far_first}  8.72 us
    ppermute x2, waiting for transfers between devices, on_device(): left.append(lax.ppermute(packed, ('mem', 'lon'), forward))  8.26 us
    ppermute x12, starting transfers between devices, exchanged(): parts = {d: lax.ppermute(taken[d, c], 'mem', peers[d]) for d in far_first}  5.77 us
    ppermute x6, starting transfers between devices, on_device(): came.append((d, c, lax.ppermute(out_parts[d], 'mem', peers[d])))  5.14 us
    ppermute x2, starting transfers between devices, on_device(): right.append(lax.ppermute(packed, ('mem', 'lon'), backward))  4.69 us
  transfers between devices with their start and end apart: 22, of which 5 were waited for; matrix products, arithmetic and copies ran while one was open for 21% of the time, Pallas kernels for 21%

profile of v6, /device:TPU:0, one launch (start us, length us, event | category | flops | bytes accessed | tf_op | source)
XLA Modules:
  0.0 90.2 jit_solution(909782744192644924)
XLA Ops:
  0.0 1.0 %constant_dynamic-slice_fusion.15 = bf16[20,24,256]{2,1,0:T(8,128)(2,1)S(1)} fusion(bf16[20,192,256]{2,1,0:T(8,128)(2,1)} %whole_ref, s32[]{:T(128)S(6)} %select_n.72), kind=kLoop, calls=%fused_computation.31 | loop fusion | bytes 491524 | tf_op jit(solution)/shard_map/dynamic_slice | solution.py:479
  1.0 1.7 %picked.1 = bf16[20,24,256]{2,1,0:T(8,128)(2,1)} custom-call(bf16[20,192,256]{2,1,0:T(8,128)(2,1)} %whole_ref), custom_call_target="tpu_custom_call" | custom-call | bytes 491520 | tf_op jit(solution)/shard_map/picked/pallas_call | solution.py:59
  2.7 2.5 %collective-permute-start.5 = (bf16[20,24,256]{2,1,0:T(8,128)(2,1)}, bf16[20,24,256]{2,1,0:T(8,128)(2,1)S(1)}, u32[]{:S(2)}, u32[]{:S(2)}) collective-permute-start(bf16[20,24,256]{2,1,0:T(8,128)(2,1)} %picked.1), channel_id=1, source_target_pairs={{0,24},{8,16},{16,8},{24,0},{1,25},{9,17},{17,9},{25,1},{2,26},{10... | collective-permute-start | bytes 737288 | tf_op jit(solution)/shard_map/ppermute | solution.py:486
  5.1 1.0 %constant_dynamic-slice_fusion.14 = bf16[20,24,256]{2,1,0:T(8,128)(2,1)S(1)} fusion(bf16[20,192,256]{2,1,0:T(8,128)(2,1)} %whole_ref, s32[]{:T(128)S(6)} %select_n.73), kind=kLoop, calls=%fused_computation.30 | loop fusion | bytes 491524 | tf_op jit(solution)/shard_map/dynamic_slice | solution.py:479
  6.1 0.7 collective-permute-start.3
  6.8 1.0 %constant_dynamic-slice_fusion.13.refs_0_ = bf16[20,24,256]{2,1,0:T(8,128)(2,1)S(1)} fusion(bf16[20,192,256]{2,1,0:T(8,128)(2,1)} %whole_ref, s32[]{:T(128)S(6)} %select_n.74), kind=kLoop, calls=%fused_computation.29 | loop fusion | bytes 491524 | tf_op jit(solution)/shard_map/dynamic_slice | solution.py:479
  7.8 1.7 %constant_dynamic-slice_fusion.12 = bf16[20,24,256]{2,1,0:T(8,128)(2,1)} fusion(bf16[20,192,256]{2,1,0:T(8,128)(2,1)} %whole_ref, s32[]{:T(128)S(6)} %select_n.75), kind=kLoop, calls=%fused_computation.28 | loop fusion | bytes 491524 | tf_op jit(solution)/shard_map/dynamic_slice | solution.py:479
  9.5 0.0 collective-permute-start.8
  9.5 1.7 %constant_dynamic-slice_fusion.11 = bf16[20,24,256]{2,1,0:T(8,128)(2,1)} fusion(bf16[20,192,256]{2,1,0:T(8,128)(2,1)} %whole_ref, s32[]{:T(128)S(6)} %select_n.76), kind=kLoop, calls=%fused_computation.27 | loop fusion | bytes 491524 | tf_op jit(solution)/shard_map/dynamic_slice | solution.py:479
  11.1 1.4 %collective-permute-start.9 = (bf16[20,24,256]{2,1,0:T(8,128)(2,1)}, bf16[20,24,256]{2,1,0:T(8,128)(2,1)S(1)}, u32[]{:S(2)}, u32[]{:S(2)}) collective-permute-start(bf16[20,24,256]{2,1,0:T(8,128)(2,1)} %constant_dynamic-slice_fusion.11), channel_id=1, source_target_pairs={{0,24},{8,16},{16,8},{24,0},{1,25},{9,17},{17,9},{25,1},{2,26},{10... | collective-permute-start | bytes 737288 | tf_op jit(solution)/shard_map/ppermute | solution.py:486
  12.5 1.7 %constant_dynamic-slice_fusion.10 = bf16[20,24,256]{2,1,0:T(8,128)(2,1)} fusion(bf16[20,192,256]{2,1,0:T(8,128)(2,1)} %whole_ref, s32[]{:T(128)S(6)} %select_n.77), kind=kLoop, calls=%fused_computation.26 | loop fusion | bytes 491524 | tf_op jit(solution)/shard_map/dynamic_slice | solution.py:479
  14.2 0.8 collective-permute-start.7
  14.9 1.0 %constant_dynamic-slice_fusion.9.refs_0_ = bf16[20,24,256]{2,1,0:T(8,128)(2,1)S(1)} fusion(bf16[20,192,256]{2,1,0:T(8,128)(2,1)} %whole_ref, s32[]{:T(128)S(6)} %select_n.78), kind=kLoop, calls=%fused_computation.25 | loop fusion | bytes 491524 | tf_op jit(solution)/shard_map/dynamic_slice | solution.py:479
  15.9 1.0 %constant_dynamic-slice_fusion.8 = bf16[20,24,256]{2,1,0:T(8,128)(2,1)S(1)} fusion(bf16[20,192,256]{2,1,0:T(8,128)(2,1)} %param.6, s32[]{:T(128)S(6)} %select_n.72), kind=kLoop, calls=%fused_computation.24 | loop fusion | bytes 491524 | tf_op jit(solution)/shard_map/dynamic_slice | solution.py:479
  16.9 1.7 %constant_dynamic-slice_fusion.7 = bf16[20,24,256]{2,1,0:T(8,128)(2,1)} fusion(bf16[20,192,256]{2,1,0:T(8,128)(2,1)} %param.6, s32[]{:T(128)S(6)} %select_n.79), kind=kLoop, calls=%fused_computation.23 | loop fusion | bytes 491524 | tf_op jit(solution)/shard_map/dynamic_slice | solution.py:479
  18.5 1.7 %constant_dynamic-slice_fusion.6 = bf16[20,24,256]{2,1,0:T(8,128)(2,1)} fusion(bf16[20,192,256]{2,1,0:T(8,128)(2,1)} %param.6, s32[]{:T(128)S(6)} %select_n.73), kind=kLoop, calls=%fused_computation.22 | loop fusion | bytes 491524 | tf_op jit(solution)/shard_map/dynamic_slice | solution.py:479
  20.2 1.0 %constant_dynamic-slice_fusion.5.refs_0_ = bf16[20,24,256]{2,1,0:T(8,128)(2,1)S(1)} fusion(bf16[20,192,256]{2,1,0:T(8,128)(2,1)} %param.6, s32[]{:T(128)S(6)} %select_n.74), kind=kLoop, calls=%fused_computation.21 | loop fusion | bytes 491524 | tf_op jit(solution)/shard_map/dynamic_slice | solution.py:479
  21.2 1.0 %constant_dynamic-slice_fusion.3 = bf16[20,24,256]{2,1,0:T(8,128)(2,1)S(1)} fusion(bf16[20,192,256]{2,1,0:T(8,128)(2,1)} %param.6, s32[]{:T(128)S(6)} %select_n.75), kind=kLoop, calls=%fused_computation.15 | loop fusion | bytes 491524 | tf_op jit(solution)/shard_map/dynamic_slice | solution.py:479
  22.1 1.0 %constant_dynamic-slice_fusion.2 = bf16[20,24,256]{2,1,0:T(8,128)(2,1)S(1)} fusion(bf16[20,192,256]{2,1,0:T(8,128)(2,1)} %param.6, s32[]{:T(128)S(6)} %select_n.76), kind=kLoop, calls=%fused_computation.14 | loop fusion | bytes 491524 | tf_op jit(solution)/shard_map/dynamic_slice | solution.py:479
  23.1 0.1 constant_dynamic-slice_fusion.4
  23.2 1.0 %constant_dynamic-slice_fusion.1 = bf16[20,24,256]{2,1,0:T(8,128)(2,1)S(1)} fusion(bf16[20,192,256]{2,1,0:T(8,128)(2,1)} %param.6, s32[]{:T(128)S(6)} %select_n.77), kind=kLoop, calls=%fused_computation.13 | loop fusion | bytes 491524 | tf_op jit(solution)/shard_map/dynamic_slice | solution.py:479
  24.2 0.0 collective-permute-done.3.refs_1_
  24.2 0.1 collective-permute-start.4
  24.3 0.1 dynamic_slice.69
  24.4 0.1 copy.8
  24.5 0.9 %dynamic-slice_multiply_fusion = (f32[48,256]{1,0:T(8,128)S(1)}, f32[48,256]{1,0:T(8,128)S(1)}) fusion(f32[192,256]{1,0:T(8,128)} %param.8, s32[]{:T(128)S(6)} %select_n.74, f32[192,256]{1,0:T(8,128)} %param.9, s32[48]{0:T(128)S(1)} %dynamic_slice.69), kind=kLoop, calls=%fused_computation.1 | loop fusion | flops 36864 | bytes 196804 | tf_op jit(solution)/shard_map/mul | solution.py:503
  25.4 0.0 collective-permute-done.5.refs_3_
  25.4 0.2 collective-permute-start
  25.5 6.6 %collective-permute-done.4.refs_2_ = bf16[20,24,256]{2,1,0:T(8,128)(2,1)S(1)} collective-permute-done((bf16[20,24,256]{2,1,0:T(8,128)(2,1)S(1)}, bf16[20,24,256]{2,1,0:T(8,128)(2,1)S(1)}, u32[]{:S(2)}, u32[]{:S(2)}) %collective-permute-start.4) | collective-permute-done | bytes 245792 | tf_op jit(solution)/shard_map/ppermute | solution.py:486
  32.1 1.8 %packed_grams.2 = (f32[768,128]{1,0:T(8,128)S(1)}, bf16[768,128]{1,0:T(8,128)(2,1)S(1)}) custom-call(bf16[20,24,256]{2,1,0:T(8,128)(2,1)S(1)} %constant_dynamic-slice_fusion.13.refs_0_, bf16[20,24,256]{2,1,0:T(8,128)(2,1)S(1)} %collective-permute-done.3.refs_1_, bf16[20,24,256]{2,1,0:T(8,128)(2,1)S(1)} %collective-permute-done.4.refs_2_, ...), custom_call_target="tpu_custom_call" | custom-call | flops 125829120 | bytes 983040 | tf_op jit(solution)/shard_map/packed_grams/pallas_call | solution.py:176
  33.9 0.0 collective-permute-done.7.refs_1_
  34.0 4.6 %collective-permute-start.11 = (bf16[768,128]{1,0:T(8,128)(2,1)S(1)}, bf16[768,128]{1,0:T(8,128)(2,1)S(1)}, u32[]{:S(2)}, u32[]{:S(2)}) collective-permute-start(bf16[768,128]{1,0:T(8,128)(2,1)S(1)} %get-tuple-element.43), channel_id=1, source_target_pairs={{0,7},{8,0},{16,8},{24,16},{25,24},{17,25},{9,17},{1,9},{2,1},{10,... | collective-permute-start | bytes 589832 | tf_op jit(solution)/shard_map/ppermute | solution.py:518
  38.6 0.0 collective-permute-done.9.refs_3_
  38.6 0.0 collective-permute-start.6
  38.6 0.0 collective-permute-done.8.refs_2_
  38.6 1.8 %packed_grams.3 = (f32[768,128]{1,0:T(8,128)S(1)}, bf16[768,128]{1,0:T(8,128)(2,1)S(1)}) custom-call(bf16[20,24,256]{2,1,0:T(8,128)(2,1)S(1)} %constant_dynamic-slice_fusion.9.refs_0_, bf16[20,24,256]{2,1,0:T(8,128)(2,1)S(1)} %collective-permute-done.7.refs_1_, bf16[20,24,256]{2,1,0:T(8,128)(2,1)S(1)} %collective-permute-done.8.refs_2_, ...), custom_call_target="tpu_custom_call" | custom-call | flops 125829120 | bytes 983040 | tf_op jit(solution)/shard_map/packed_grams/pallas_call | solution.py:176
  40.4 0.1 collective-permute-start.10
  40.5 0.1 add_multiply_fusion.row_ref
  40.6 0.0 collective-permute-done.refs_1_
  40.6 0.1 collective-permute-start.17
  40.7 0.0 collective-permute-done.2.refs_3_
  40.7 0.1 collective-permute-start.16
  40.8 8.3 %collective-permute-done.10.refs_1_.refs_0_ = bf16[768,128]{1,0:T(8,128)(2,1)S(1)} collective-permute-done((bf16[768,128]{1,0:T(8,128)(2,1)S(1)}, bf16[768,128]{1,0:T(8,128)(2,1)S(1)}, u32[]{:S(2)}, u32[]{:S(2)}) %collective-permute-start.10) | collective-permute-done | bytes 196640 | tf_op jit(solution)/shard_map/ppermute | solution.py:517
  49.1 0.0 collective-permute-start.1
  49.1 0.0 collective-permute-done.6.refs_0_
  49.1 0.1 collective-permute-start.18
  49.2 0.1 add_divide_fusion.taper_ref
  49.3 6.4 %blends.2.refs_4_ = bf16[1920,128]{1,0:T(8,128)(2,1)S(1)} custom-call(s32[48,16]{1,0:T(8,128)S(1)} %add_multiply_fusion.row_ref, f32[48,16]{1,0:T(8,128)S(1)} %add_divide_fusion.taper_ref, bf16[768,128]{1,0:T(8,128)(2,1)S(1)} %collective-permute-done.6.refs_0_, bf16[768,128]{1,0:T(8,128)(2,1)S(1)} %collective-permute-done.10.refs_1_.refs_0_, ...), custom_call_target="tpu_custom_call" | custom-call | flops 471859200 | bytes 1474560 | tf_op jit(solution)/shard_map/blends/pallas_call | solution.py:322
  55.7 2.1 %collective-permute-done.1.refs_2_ = bf16[20,24,256]{2,1,0:T(8,128)(2,1)S(1)} collective-permute-done((bf16[20,24,256]{2,1,0:T(8,128)(2,1)S(1)}, bf16[20,24,256]{2,1,0:T(8,128)(2,1)S(1)}, u32[]{:S(2)}, u32[]{:S(2)}) %collective-permute-start.1) | collective-permute-done | bytes 245792 | tf_op jit(solution)/shard_map/ppermute | solution.py:486
  57.8 1.3 %apply_blend.2 = (bf16[20,24,256]{2,1,0:T(8,128)(2,1)S(1)}, bf16[20,24,256]{2,1,0:T(8,128)(2,1)S(1)}, bf16[20,24,256]{2,1,0:T(8,128)(2,1)S(1)}, bf16[20,24,256]{2,1,0:T(8,128)(2,1)S(1)}) custom-call(bf16[20,24,256]{2,1,0:T(8,128)(2,1)S(1)} %constant_dynamic-slice_fusion.5.refs_0_, bf16[20,24,256]{2,1,0:T(8,128)(2,1)S(1)} %collective-permute-done.refs_1_, ...), custom_call_target="tpu_custom_call" | custom-call | flops 125829120 | bytes 1966080 | tf_op jit(solution)/shard_map/apply_blend/pallas_call | solution.py:411
  59.1 0.9 collective-permute-start.12
  60.0 1.0 %constant_dynamic-slice_fusion.refs_0_ = bf16[20,24,256]{2,1,0:T(8,128)(2,1)S(1)} fusion(bf16[20,192,256]{2,1,0:T(8,128)(2,1)} %param.6, s32[]{:T(128)S(6)} %select_n.78), kind=kLoop, calls=%fused_computation.12 | loop fusion | bytes 491524 | tf_op jit(solution)/shard_map/dynamic_slice | solution.py:479
  61.0 2.2 %collective-permute-start.13 = (bf16[20,24,256]{2,1,0:T(8,128)(2,1)S(1)}, bf16[20,24,256]{2,1,0:T(8,128)(2,1)S(1)}, u32[]{:S(2)}, u32[]{:S(2)}) collective-permute-start(bf16[20,24,256]{2,1,0:T(8,128)(2,1)S(1)} %get-tuple-element.49), channel_id=1, source_target_pairs={{0,16},{8,24},{16,0},{24,8},{1,17},{9,25},{17,1},{25,9},{2,18},{10... | collective-permute-start | bytes 737288 | tf_op jit(solution)/shard_map/ppermute | solution.py:527
  63.2 6.5 %blends.3.refs_4_ = bf16[1920,128]{1,0:T(8,128)(2,1)S(1)} custom-call(s32[48,16]{1,0:T(8,128)S(1)} %add_multiply_fusion.row_ref, f32[48,16]{1,0:T(8,128)S(1)} %add_divide_fusion.taper_ref, bf16[768,128]{1,0:T(8,128)(2,1)S(1)} %collective-permute-done.10.refs_1_.refs_0_, f32[768,128]{1,0:T(8,128)S(1)} %get-tuple-element.45.refs_2_.refs_1_, ...), custom_call_target="tpu_custom_call" | custom-call | flops 471859200 | bytes 1474560 | tf_op jit(solution)/shard_map/blends/pallas_call | solution.py:322
  69.7 1.3 %apply_blend.3 = (bf16[20,24,256]{2,1,0:T(8,128)(2,1)S(1)}, bf16[20,24,256]{2,1,0:T(8,128)(2,1)S(1)}, bf16[20,24,256]{2,1,0:T(8,128)(2,1)S(1)}, bf16[20,24,256]{2,1,0:T(8,128)(2,1)S(1)}) custom-call(bf16[20,24,256]{2,1,0:T(8,128)(2,1)S(1)} %constant_dynamic-slice_fusion.refs_0_, bf16[20,24,256]{2,1,0:T(8,128)(2,1)S(1)} %collective-permute-done.15.refs_1_, ...), custom_call_target="tpu_custom_call" | custom-call | flops 125829120 | bytes 1966080 | tf_op jit(solution)/shard_map/apply_blend/pallas_call | solution.py:411
  71.1 0.1 collective-permute-start.19
  71.1 0.1 collective-permute-start.20
  71.2 1.8 %collective-permute-start.14 = (bf16[20,24,256]{2,1,0:T(8,128)(2,1)S(1)}, bf16[20,24,256]{2,1,0:T(8,128)(2,1)S(1)}, u32[]{:S(2)}, u32[]{:S(2)}) collective-permute-start(bf16[20,24,256]{2,1,0:T(8,128)(2,1)S(1)} %get-tuple-element.50), channel_id=1, source_target_pairs={{0,24},{8,16},{16,8},{24,0},{1,25},{9,17},{17,9},{25,1},{2,26},{10... | collective-permute-start | bytes 737288 | tf_op jit(solution)/shard_map/ppermute | solution.py:527
  73.0 0.2 broadcast_in_dim.2
  73.2 0.1 collective-permute-start.21
  73.4 10.8 %collective-permute-done.14 = bf16[20,24,256]{2,1,0:T(8,128)(2,1)S(1)} collective-permute-done((bf16[20,24,256]{2,1,0:T(8,128)(2,1)S(1)}, bf16[20,24,256]{2,1,0:T(8,128)(2,1)S(1)}, u32[]{:S(2)}, u32[]{:S(2)}) %collective-permute-start.14) | collective-permute-done | bytes 245792 | tf_op jit(solution)/shard_map/ppermute | solution.py:527
  84.4 0.0 copy-start.1
  84.4 5.1 %collective-permute-done.21 = bf16[20,24,256]{2,1,0:T(8,128)(2,1)S(1)} collective-permute-done((bf16[20,24,256]{2,1,0:T(8,128)(2,1)S(1)}, bf16[20,24,256]{2,1,0:T(8,128)(2,1)S(1)}, u32[]{:S(2)}, u32[]{:S(2)}) %collective-permute-start.21) | collective-permute-done | bytes 245792 | tf_op jit(solution)/shard_map/ppermute | solution.py:527
  89.5 0.7 constant_dynamic-update-slice_fusion
  (24 shorter events, 0.2 us)
Async XLA Ops:
  0.0 23.1 %copy-start = (s32[192,16]{0,1:T(8,128)S(1)}, s32[192,16]{0,1:T(8,128)}, u32[]{:S(2)}) copy-start(s32[192,16]{0,1:T(8,128)} %param.11) | copy-start | bytes 36868
  2.7 22.7 %collective-permute-start.5 = (bf16[20,24,256]{2,1,0:T(8,128)(2,1)}, bf16[20,24,256]{2,1,0:T(8,128)(2,1)S(1)}, u32[]{:S(2)}, u32[]{:S(2)}) collective-permute-start(bf16[20,24,256]{2,1,0:T(8,128)(2,1)} %picked.1), channel_id=1, source_target_pairs={{0,24},{8,16},{16,8},{24,0},{1,25},{9,17},{17,9},{25,1},{2,26},{10... | collective-permute-start | bytes 737288 | tf_op jit(solution)/shard_map/ppermute | solution.py:486
  6.1 18.1 %collective-permute-start.3 = (bf16[20,24,256]{2,1,0:T(8,128)(2,1)S(1)}, bf16[20,24,256]{2,1,0:T(8,128)(2,1)S(1)}, u32[]{:S(2)}, u32[]{:S(2)}) collective-permute-start(bf16[20,24,256]{2,1,0:T(8,128)(2,1)S(1)} %constant_dynamic-slice_fusion.14), channel_id=1, source_target_pairs={{0,8},{8,0},{16,24},{24,16},{1,9},{9,1},{17,25},{25,17},{2,10},{10... | collective-permute-start | bytes 737288 | tf_op jit(solution)/shard_map/ppermute | solution.py:486
  9.5 29.1 %collective-permute-start.8 = (bf16[20,24,256]{2,1,0:T(8,128)(2,1)}, bf16[20,24,256]{2,1,0:T(8,128)(2,1)S(1)}, u32[]{:S(2)}, u32[]{:S(2)}) collective-permute-start(bf16[20,24,256]{2,1,0:T(8,128)(2,1)} %constant_dynamic-slice_fusion.12), channel_id=1, source_target_pairs={{0,16},{8,24},{16,0},{24,8},{1,17},{9,25},{17,1},{25,9},{2,18},{10... | collective-permute-start | bytes 737288 | tf_op jit(solution)/shard_map/ppermute | solution.py:486
  11.1 27.4 %collective-permute-start.9 = (bf16[20,24,256]{2,1,0:T(8,128)(2,1)}, bf16[20,24,256]{2,1,0:T(8,128)(2,1)S(1)}, u32[]{:S(2)}, u32[]{:S(2)}) collective-permute-start(bf16[20,24,256]{2,1,0:T(8,128)(2,1)} %constant_dynamic-slice_fusion.11), channel_id=1, source_target_pairs={{0,24},{8,16},{16,8},{24,0},{1,25},{9,17},{17,9},{25,1},{2,26},{10... | collective-permute-start | bytes 737288 | tf_op jit(solution)/shard_map/ppermute | solution.py:486
  14.2 19.8 %collective-permute-start.7 = (bf16[20,24,256]{2,1,0:T(8,128)(2,1)}, bf16[20,24,256]{2,1,0:T(8,128)(2,1)S(1)}, u32[]{:S(2)}, u32[]{:S(2)}) collective-permute-start(bf16[20,24,256]{2,1,0:T(8,128)(2,1)} %constant_dynamic-slice_fusion.10), channel_id=1, source_target_pairs={{0,8},{8,0},{16,24},{24,16},{1,9},{9,1},{17,25},{25,17},{2,10},{10... | collective-permute-start | bytes 737288 | tf_op jit(solution)/shard_map/ppermute | solution.py:486
  14.9 9.4 %copy-start.2 = (s32[192]{0:T(256)S(1)}, s32[192]{0:T(256)}, u32[]{:S(2)}) copy-start(s32[192]{0:T(256)} %param.10) | copy-start | bytes 2308
  24.2 7.9 %collective-permute-start.4 = (bf16[20,24,256]{2,1,0:T(8,128)(2,1)S(1)}, bf16[20,24,256]{2,1,0:T(8,128)(2,1)S(1)}, u32[]{:S(2)}, u32[]{:S(2)}) collective-permute-start(bf16[20,24,256]{2,1,0:T(8,128)(2,1)S(1)} %constant_dynamic-slice_fusion.15), channel_id=1, source_target_pairs={{0,16},{8,24},{16,0},{24,8},{1,17},{9,25},{17,1},{25,9},{2,18},{10... | collective-permute-start | bytes 737288 | tf_op jit(solution)/shard_map/ppermute | solution.py:486
  25.4 15.2 %collective-permute-start = (bf16[20,24,256]{2,1,0:T(8,128)(2,1)}, bf16[20,24,256]{2,1,0:T(8,128)(2,1)S(1)}, u32[]{:S(2)}, u32[]{:S(2)}) collective-permute-start(bf16[20,24,256]{2,1,0:T(8,128)(2,1)} %constant_dynamic-slice_fusion.6), channel_id=1, source_target_pairs={{0,8},{8,0},{16,24},{24,16},{1,9},{9,1},{17,25},{25,17},{2,10},{10... | collective-permute-start | bytes 737288 | tf_op jit(solution)/shard_map/ppermute | solution.py:486
  32.1 8.6 %collective-permute-start.2 = (bf16[20,24,256]{2,1,0:T(8,128)(2,1)}, bf16[20,24,256]{2,1,0:T(8,128)(2,1)S(1)}, u32[]{:S(2)}, u32[]{:S(2)}) collective-permute-start(bf16[20,24,256]{2,1,0:T(8,128)(2,1)} %constant_dynamic-slice_fusion.7), channel_id=1, source_target_pairs={{0,24},{8,16},{16,8},{24,0},{1,25},{9,17},{17,9},{25,1},{2,26},{10... | collective-permute-start | bytes 737288 | tf_op jit(solution)/shard_map/ppermute | solution.py:486
  34.0 15.1 %collective-permute-start.11 = (bf16[768,128]{1,0:T(8,128)(2,1)S(1)}, bf16[768,128]{1,0:T(8,128)(2,1)S(1)}, u32[]{:S(2)}, u32[]{:S(2)}) collective-permute-start(bf16[768,128]{1,0:T(8,128)(2,1)S(1)} %get-tuple-element.43), channel_id=1, source_target_pairs={{0,7},{8,0},{16,8},{24,16},{25,24},{17,25},{9,17},{1,9},{2,1},{10,... | collective-permute-start | bytes 589832 | tf_op jit(solution)/shard_map/ppermute | solution.py:518
  38.6 10.5 %collective-permute-start.6 = (bf16[768,128]{1,0:T(8,128)(2,1)S(1)}, bf16[768,128]{1,0:T(8,128)(2,1)S(1)}, u32[]{:S(2)}, u32[]{:S(2)}) collective-permute-start(bf16[768,128]{1,0:T(8,128)(2,1)S(1)} %get-tuple-element.43), channel_id=1, source_target_pairs={{0,8},{8,16},{16,24},{24,25},{25,17},{17,9},{9,1},{1,2},{2,10},{10... | collective-permute-start | bytes 589832 | tf_op jit(solution)/shard_map/ppermute | solution.py:517
  40.4 8.6 %collective-permute-start.10 = (bf16[768,128]{1,0:T(8,128)(2,1)S(1)}, bf16[768,128]{1,0:T(8,128)(2,1)S(1)}, u32[]{:S(2)}, u32[]{:S(2)}) collective-permute-start(bf16[768,128]{1,0:T(8,128)(2,1)S(1)} %get-tuple-element.44), channel_id=1, source_target_pairs={{0,8},{8,16},{16,24},{24,25},{25,17},{17,9},{9,1},{1,2},{2,10},{10... | collective-permute-start | bytes 589832 | tf_op jit(solution)/shard_map/ppermute | solution.py:517
  40.6 29.1 %collective-permute-start.17 = (bf16[20,24,256]{2,1,0:T(8,128)(2,1)S(1)}, bf16[20,24,256]{2,1,0:T(8,128)(2,1)S(1)}, u32[]{:S(2)}, u32[]{:S(2)}) collective-permute-start(bf16[20,24,256]{2,1,0:T(8,128)(2,1)S(1)} %constant_dynamic-slice_fusion.2), channel_id=1, source_target_pairs={{0,24},{8,16},{16,8},{24,0},{1,25},{9,17},{17,9},{25,1},{2,26},{10... | collective-permute-start | bytes 737288 | tf_op jit(solution)/shard_map/ppermute | solution.py:486
  40.7 29.0 %collective-permute-start.16 = (bf16[20,24,256]{2,1,0:T(8,128)(2,1)S(1)}, bf16[20,24,256]{2,1,0:T(8,128)(2,1)S(1)}, u32[]{:S(2)}, u32[]{:S(2)}) collective-permute-start(bf16[20,24,256]{2,1,0:T(8,128)(2,1)S(1)} %constant_dynamic-slice_fusion.3), channel_id=1, source_target_pairs={{0,16},{8,24},{16,0},{24,8},{1,17},{9,25},{17,1},{25,9},{2,18},{10... | collective-permute-start | bytes 737288 | tf_op jit(solution)/shard_map/ppermute | solution.py:486
  49.1 8.8 %collective-permute-start.1 = (bf16[20,24,256]{2,1,0:T(8,128)(2,1)S(1)}, bf16[20,24,256]{2,1,0:T(8,128)(2,1)S(1)}, u32[]{:S(2)}, u32[]{:S(2)}) collective-permute-start(bf16[20,24,256]{2,1,0:T(8,128)(2,1)S(1)} %constant_dynamic-slice_fusion.8), channel_id=1, source_target_pairs={{0,16},{8,24},{16,0},{24,8},{1,17},{9,25},{17,1},{25,9},{2,18},{10... | collective-permute-start | bytes 737288 | tf_op jit(solution)/shard_map/ppermute | solution.py:486
  49.1 20.6 %collective-permute-start.15 = (bf16[20,24,256]{2,1,0:T(8,128)(2,1)S(1)}, bf16[20,24,256]{2,1,0:T(8,128)(2,1)S(1)}, u32[]{:S(2)}, u32[]{:S(2)}) collective-permute-start(bf16[20,24,256]{2,1,0:T(8,128)(2,1)S(1)} %constant_dynamic-slice_fusion.1), channel_id=1, source_target_pairs={{0,8},{8,0},{16,24},{24,16},{1,9},{9,1},{17,25},{25,17},{2,10},{10... | collective-permute-start | bytes 737288 | tf_op jit(solution)/shard_map/ppermute | solution.py:486
  49.1 11.9 %collective-permute-start.18 = (bf16[768,128]{1,0:T(8,128)(2,1)S(1)}, bf16[768,128]{1,0:T(8,128)(2,1)S(1)}, u32[]{:S(2)}, u32[]{:S(2)}) collective-permute-start(bf16[768,128]{1,0:T(8,128)(2,1)S(1)} %get-tuple-element.44), channel_id=1, source_target_pairs={{0,7},{8,0},{16,8},{24,16},{25,24},{17,25},{9,17},{1,9},{2,1},{10,... | collective-permute-start | bytes 589832 | tf_op jit(solution)/shard_map/ppermute | solution.py:518
  59.1 14.1 %collective-permute-start.12 = (bf16[20,24,256]{2,1,0:T(8,128)(2,1)S(1)}, bf16[20,24,256]{2,1,0:T(8,128)(2,1)S(1)}, u32[]{:S(2)}, u32[]{:S(2)}) collective-permute-start(bf16[20,24,256]{2,1,0:T(8,128)(2,1)S(1)} %get-tuple-element.48), channel_id=1, source_target_pairs={{0,8},{8,0},{16,24},{24,16},{1,9},{9,1},{17,25},{25,17},{2,10},{10... | collective-permute-start | bytes 737288 | tf_op jit(solution)/shard_map/ppermute | solution.py:527
  61.0 12.4 %collective-permute-start.13 = (bf16[20,24,256]{2,1,0:T(8,128)(2,1)S(1)}, bf16[20,24,256]{2,1,0:T(8,128)(2,1)S(1)}, u32[]{:S(2)}, u32[]{:S(2)}) collective-permute-start(bf16[20,24,256]{2,1,0:T(8,128)(2,1)S(1)} %get-tuple-element.49), channel_id=1, source_target_pairs={{0,16},{8,24},{16,0},{24,8},{1,17},{9,25},{17,1},{25,9},{2,18},{10... | collective-permute-start | bytes 737288 | tf_op jit(solution)/shard_map/ppermute | solution.py:527
  71.1 13.2 %collective-permute-start.19 = (bf16[20,24,256]{2,1,0:T(8,128)(2,1)S(1)}, bf16[20,24,256]{2,1,0:T(8,128)(2,1)S(1)}, u32[]{:S(2)}, u32[]{:S(2)}) collective-permute-start(bf16[20,24,256]{2,1,0:T(8,128)(2,1)S(1)} %get-tuple-element.56), channel_id=1, source_target_pairs={{0,8},{8,0},{16,24},{24,16},{1,9},{9,1},{17,25},{25,17},{2,10},{10... | collective-permute-start | bytes 737288 | tf_op jit(solution)/shard_map/ppermute | solution.py:527
  71.1 13.2 %collective-permute-start.20 = (bf16[20,24,256]{2,1,0:T(8,128)(2,1)S(1)}, bf16[20,24,256]{2,1,0:T(8,128)(2,1)S(1)}, u32[]{:S(2)}, u32[]{:S(2)}) collective-permute-start(bf16[20,24,256]{2,1,0:T(8,128)(2,1)S(1)} %get-tuple-element.57), channel_id=1, source_target_pairs={{0,16},{8,24},{16,0},{24,8},{1,17},{9,25},{17,1},{25,9},{2,18},{10... | collective-permute-start | bytes 737288 | tf_op jit(solution)/shard_map/ppermute | solution.py:527
  71.2 13.0 %collective-permute-start.14 = (bf16[20,24,256]{2,1,0:T(8,128)(2,1)S(1)}, bf16[20,24,256]{2,1,0:T(8,128)(2,1)S(1)}, u32[]{:S(2)}, u32[]{:S(2)}) collective-permute-start(bf16[20,24,256]{2,1,0:T(8,128)(2,1)S(1)} %get-tuple-element.50), channel_id=1, source_target_pairs={{0,24},{8,16},{16,8},{24,0},{1,25},{9,17},{17,9},{25,1},{2,26},{10... | collective-permute-start | bytes 737288 | tf_op jit(solution)/shard_map/ppermute | solution.py:527
  73.2 16.3 %collective-permute-start.21 = (bf16[20,24,256]{2,1,0:T(8,128)(2,1)S(1)}, bf16[20,24,256]{2,1,0:T(8,128)(2,1)S(1)}, u32[]{:S(2)}, u32[]{:S(2)}) collective-permute-start(bf16[20,24,256]{2,1,0:T(8,128)(2,1)S(1)} %get-tuple-element.58), channel_id=1, source_target_pairs={{0,24},{8,16},{16,8},{24,0},{1,25},{9,17},{17,9},{25,1},{2,26},{10... | collective-permute-start | bytes 737288 | tf_op jit(solution)/shard_map/ppermute | solution.py:527
  84.4 5.1 %copy-start.1 = (bf16[20,192,256]{2,1,0:T(8,128)(2,1)}, bf16[20,192,256]{2,1,0:T(8,128)(2,1)S(1)}, u32[]{:S(2)}) copy-start(bf16[20,192,256]{2,1,0:T(8,128)(2,1)S(1)} %constant_dynamic-update-slice_fusion.1) | copy-start | bytes 5898244

commit v7 on v5

--- a/solution.py
+++ b/solution.py
@@ -16,7 +16,7 @@
 VMEM_BYTES = 16 * 1024 * 1024
 CROWDED_BYTES = 66_000_000
 CHUNKS = 2
-GROUP = 12
+GROUP = 8
 PAD = 1
 
 
@@ -469,12 +469,15 @@
     chunks = range(CHUNKS)
     last = None
 
-    def pieces(x, wanted):
+    def after(x, earlier):
+        return lax.optimization_barrier((x, earlier))[0]
+
+    def sliced(x, wanted):
         nonlocal last
         taken = {}
         for d, c in wanted:
             if last is not None:
-                x, _ = lax.optimization_barrier((x, last))
+                x = after(x, last)
             start = ((mem ^ d) ^ flip) * blocks + c * size
             last = taken[d, c] = lax.dynamic_slice_in_dim(x, start, size, 1)
         return taken
@@ -489,11 +492,11 @@
 
     order = far_first + [0]
     everything = [(d, c) for c in chunks for d in order]
-    (last,) = picked(scaled_sensor_spread, everything[:1], groups, size)
-    spread_taken = {everything[0]: last} | pieces(scaled_sensor_spread, everything[1:])
-    field_taken = pieces(prior_fields, everything)
+    spread_taken = sliced(scaled_sensor_spread, everything[:1])
+    (last,) = picked(after(scaled_sensor_spread, last), everything[1:2], groups, size)
+    spread_taken |= {everything[1]: last} | sliced(scaled_sensor_spread, everything[2:])
+    field_taken = sliced(prior_fields, everything[:2])
     spread_parts = [exchanged(spread_taken, c) for c in chunks]
-    field_parts = [exchanged(field_taken, c) for c in chunks]
 
     slot_ids = jnp.arange(width, dtype=jnp.int32)
     live = (slot_ids[None, :] < own_rows(active_sensor_number)[:, None]).astype(F32)
@@ -514,6 +517,9 @@
         own.append(here)
         left.append(lax.ppermute(packed, ("mem", "lon"), forward))
         right.append(lax.ppermute(packed, ("mem", "lon"), backward))
+    last = own[-1]
+    field_taken |= sliced(prior_fields, everything[2:])
+    field_parts = [exchanged(field_taken, c) for c in chunks]
     window = left + own + right
 
     came = []

time: 91 us -> 90.9 us (level)
  local copies, waits for them, and re-layouts: 19.3 us -> 10.3 us
  starting transfers between devices: 15.7 us -> 23.7 us
  Pallas kernels: 20.8 us -> 25.1 us
  waiting for transfers between devices: 33.1 us -> 29.9 us
    dynamic_slice x15, local copies, waits for them, and re-layouts: 18 us -> 9 us  [sliced(): last = taken[d, c] = lax.dynamic_slice_in_dim(x, start, size, 1)]
    ppermute x2, waiting for transfers between devices: 8.26 us -> 3.23 us  [on_device(): left.append(lax.ppermute(packed, ('mem', 'lon'), forward))]
    ppermute x2, starting transfers between devices: 4.69 us -> 9.58 us  [on_device(): right.append(lax.ppermute(packed, ('mem', 'lon'), backward))]
    ppermute x12, starting transfers between devices: 5.77 us -> 9.51 us  [exchanged(): parts = {d: lax.ppermute(taken[d, c], 'mem', peers[d]) for d in far_first}]
    pallas_call x2, Pallas kernels: 12.9 us -> 16.6 us  [blends(): pl.pallas_call(functools.partial(blend_kernel, members=members, neighbour...]
    ppermute x6, waiting for transfers between devices: 15.9 us -> 17.8 us  [on_device(): came.append((d, c, lax.ppermute(out_parts[d], 'mem', peers[d])))]
  transfers between devices with their start and end apart: 22 -> 22, of which waited for: 5 -> 5; matrix products, arithmetic and copies ran while one was open for 21% -> 11% of each run, Pallas kernels for 21% -> 26%
where the time goes in v7:
time: 90.9 us; the launch traced here: 90.5 us
  waiting for transfers between devices  29.9 us (33%)
  Pallas kernels  25.1 us (28%)
  starting transfers between devices  23.7 us (26%)
  local copies, waits for them, and re-layouts  10.3 us (11%)
  other arithmetic  1.11 us (1%)
    ppermute x6, waiting for transfers between devices, on_device(): came.append((d, c, lax.ppermute(out_parts[d], 'mem', peers[d])))  17.8 us
    pallas_call x2, Pallas kernels, blends(): pl.pallas_call(functools.partial(blend_kernel, members=members, neighbour...  16.6 us
    ppermute x2, starting transfers between devices, on_device(): right.append(lax.ppermute(packed, ('mem', 'lon'), backward))  9.58 us
    ppermute x12, starting transfers between devices, exchanged(): parts = {d: lax.ppermute(taken[d, c], 'mem', peers[d]) for d in far_first}  9.51 us
    dynamic_slice x15, local copies, waits for them, and re-layouts, sliced(): last = taken[d, c] = lax.dynamic_slice_in_dim(x, start, size, 1)  9 us
    ppermute x12, waiting for transfers between devices, exchanged(): parts = {d: lax.ppermute(taken[d, c], 'mem', peers[d]) for d in far_first}  8.82 us
    ppermute x6, starting transfers between devices, on_device(): came.append((d, c, lax.ppermute(out_parts[d], 'mem', peers[d])))  4.57 us
    pallas_call x2, Pallas kernels, packed_grams(): pl.pallas_call(functools.partial(gram_kernel, groups=groups, share=share,...  3.94 us
  transfers between devices with their start and end apart: 22, of which 5 were waited for; matrix products, arithmetic and copies ran while one was open for 11% of the time, Pallas kernels for 26%

profile of v7, /device:TPU:0, one launch (start us, length us, event | category | flops | bytes accessed | tf_op | source)
XLA Modules:
  0.0 90.5 jit_solution(15950494849133068258)
XLA Ops:
  0.0 1.0 %constant_dynamic-slice_fusion.15 = bf16[20,24,256]{2,1,0:T(8,128)(2,1)S(1)} fusion(bf16[20,192,256]{2,1,0:T(8,128)(2,1)} %whole_ref, s32[]{:T(128)S(6)} %select_n.72), kind=kLoop, calls=%fused_computation.31 | loop fusion | bytes 491524 | tf_op jit(solution)/shard_map/dynamic_slice | solution.py:482
  1.0 1.7 %picked.1 = bf16[20,24,256]{2,1,0:T(8,128)(2,1)} custom-call(bf16[20,192,256]{2,1,0:T(8,128)(2,1)} %whole_ref), custom_call_target="tpu_custom_call" | custom-call | bytes 491520 | tf_op jit(solution)/shard_map/picked/pallas_call | solution.py:59
  2.7 2.5 %collective-permute-start.8 = (bf16[20,24,256]{2,1,0:T(8,128)(2,1)}, bf16[20,24,256]{2,1,0:T(8,128)(2,1)S(1)}, u32[]{:S(2)}, u32[]{:S(2)}) collective-permute-start(bf16[20,24,256]{2,1,0:T(8,128)(2,1)} %picked.1), channel_id=1, source_target_pairs={{0,24},{8,16},{16,8},{24,0},{1,25},{9,17},{17,9},{25,1},{2,26},{10... | collective-permute-start | bytes 737288 | tf_op jit(solution)/shard_map/ppermute | solution.py:489
  5.1 1.0 %constant_dynamic-slice_fusion.14 = bf16[20,24,256]{2,1,0:T(8,128)(2,1)S(1)} fusion(bf16[20,192,256]{2,1,0:T(8,128)(2,1)} %whole_ref, s32[]{:T(128)S(6)} %select_n.73), kind=kLoop, calls=%fused_computation.30 | loop fusion | bytes 491524 | tf_op jit(solution)/shard_map/dynamic_slice | solution.py:482
  6.1 0.7 collective-permute-start.6
  6.8 1.0 %constant_dynamic-slice_fusion.13.refs_0_ = bf16[20,24,256]{2,1,0:T(8,128)(2,1)S(1)} fusion(bf16[20,192,256]{2,1,0:T(8,128)(2,1)} %whole_ref, s32[]{:T(128)S(6)} %select_n.74), kind=kLoop, calls=%fused_computation.29 | loop fusion | bytes 491524 | tf_op jit(solution)/shard_map/dynamic_slice | solution.py:482
  7.8 1.0 %constant_dynamic-slice_fusion.12 = bf16[20,24,256]{2,1,0:T(8,128)(2,1)S(1)} fusion(bf16[20,192,256]{2,1,0:T(8,128)(2,1)} %whole_ref, s32[]{:T(128)S(6)} %select_n.75), kind=kLoop, calls=%fused_computation.28 | loop fusion | bytes 491524 | tf_op jit(solution)/shard_map/dynamic_slice | solution.py:482
  8.8 0.1 collective-permute-start.1
  8.9 1.0 %constant_dynamic-slice_fusion.11 = bf16[20,24,256]{2,1,0:T(8,128)(2,1)S(1)} fusion(bf16[20,192,256]{2,1,0:T(8,128)(2,1)} %whole_ref, s32[]{:T(128)S(6)} %select_n.76), kind=kLoop, calls=%fused_computation.27 | loop fusion | bytes 491524 | tf_op jit(solution)/shard_map/dynamic_slice | solution.py:482
  9.9 1.4 %collective-permute-start.2 = (bf16[20,24,256]{2,1,0:T(8,128)(2,1)S(1)}, bf16[20,24,256]{2,1,0:T(8,128)(2,1)S(1)}, u32[]{:S(2)}, u32[]{:S(2)}) collective-permute-start(bf16[20,24,256]{2,1,0:T(8,128)(2,1)S(1)} %constant_dynamic-slice_fusion.11), channel_id=1, source_target_pairs={{0,24},{8,16},{16,8},{24,0},{1,25},{9,17},{17,9},{25,1},{2,26},{10... | collective-permute-start | bytes 737288 | tf_op jit(solution)/shard_map/ppermute | solution.py:489
  11.3 1.0 %constant_dynamic-slice_fusion.10 = bf16[20,24,256]{2,1,0:T(8,128)(2,1)S(1)} fusion(bf16[20,192,256]{2,1,0:T(8,128)(2,1)} %whole_ref, s32[]{:T(128)S(6)} %select_n.77), kind=kLoop, calls=%fused_computation.26 | loop fusion | bytes 491524 | tf_op jit(solution)/shard_map/dynamic_slice | solution.py:482
  12.2 0.8 collective-permute-start
  13.1 0.1 constant_dynamic-slice_fusion.4
  13.1 1.0 %constant_dynamic-slice_fusion.9.refs_0_ = bf16[20,24,256]{2,1,0:T(8,128)(2,1)S(1)} fusion(bf16[20,192,256]{2,1,0:T(8,128)(2,1)} %whole_ref, s32[]{:T(128)S(6)} %select_n.78), kind=kLoop, calls=%fused_computation.25 | loop fusion | bytes 491524 | tf_op jit(solution)/shard_map/dynamic_slice | solution.py:482
  14.1 1.0 %constant_dynamic-slice_fusion.6 = bf16[20,24,256]{2,1,0:T(8,128)(2,1)S(1)} fusion(bf16[20,192,256]{2,1,0:T(8,128)(2,1)} %param.6, s32[]{:T(128)S(6)} %select_n.72), kind=kLoop, calls=%fused_computation.22 | loop fusion | bytes 491524 | tf_op jit(solution)/shard_map/dynamic_slice | solution.py:482
  15.1 0.1 copy.8
  15.2 0.1 add_multiply_fusion.row_ref
  15.3 0.0 collective-permute-done.6.refs_1_
  15.3 0.1 collective-permute-start.7
  15.4 1.1 %constant_dynamic-slice_fusion.5 = bf16[20,24,256]{2,1,0:T(8,128)(2,1)S(1)} fusion(bf16[20,192,256]{2,1,0:T(8,128)(2,1)} %param.6, s32[]{:T(128)S(6)} %select_n.79), kind=kLoop, calls=%fused_computation.21 | loop fusion | bytes 491524 | tf_op jit(solution)/shard_map/dynamic_slice | solution.py:482
  16.5 0.1 dynamic_slice.64
  16.6 0.9 %dynamic-slice_multiply_fusion = (f32[48,256]{1,0:T(8,128)S(1)}, f32[48,256]{1,0:T(8,128)S(1)}) fusion(f32[192,256]{1,0:T(8,128)} %param.8, s32[]{:T(128)S(6)} %select_n.74, f32[192,256]{1,0:T(8,128)} %param.9, s32[48]{0:T(128)S(1)} %dynamic_slice.64), kind=kLoop, calls=%fused_computation.1 | loop fusion | flops 36864 | bytes 196804 | tf_op jit(solution)/shard_map/mul | solution.py:504
  17.5 2.0 %collective-permute-start.4 = (bf16[20,24,256]{2,1,0:T(8,128)(2,1)S(1)}, bf16[20,24,256]{2,1,0:T(8,128)(2,1)S(1)}, u32[]{:S(2)}, u32[]{:S(2)}) collective-permute-start(bf16[20,24,256]{2,1,0:T(8,128)(2,1)S(1)} %constant_dynamic-slice_fusion.6), channel_id=1, source_target_pairs={{0,16},{8,24},{16,0},{24,8},{1,17},{9,25},{17,1},{25,9},{2,18},{10... | collective-permute-start | bytes 737288 | tf_op jit(solution)/shard_map/ppermute | solution.py:489
  19.4 8.8 %collective-permute-done.7.refs_2_ = bf16[20,24,256]{2,1,0:T(8,128)(2,1)S(1)} collective-permute-done((bf16[20,24,256]{2,1,0:T(8,128)(2,1)S(1)}, bf16[20,24,256]{2,1,0:T(8,128)(2,1)S(1)}, u32[]{:S(2)}, u32[]{:S(2)}) %collective-permute-start.7) | collective-permute-done | bytes 245792 | tf_op jit(solution)/shard_map/ppermute | solution.py:489
  28.2 1.4 %collective-permute-start.5 = (bf16[20,24,256]{2,1,0:T(8,128)(2,1)S(1)}, bf16[20,24,256]{2,1,0:T(8,128)(2,1)S(1)}, u32[]{:S(2)}, u32[]{:S(2)}) collective-permute-start(bf16[20,24,256]{2,1,0:T(8,128)(2,1)S(1)} %constant_dynamic-slice_fusion.5), channel_id=1, source_target_pairs={{0,24},{8,16},{16,8},{24,0},{1,25},{9,17},{17,9},{25,1},{2,26},{10... | collective-permute-start | bytes 737288 | tf_op jit(solution)/shard_map/ppermute | solution.py:489
  29.7 2.0 %packed_grams.3 = (f32[768,128]{1,0:T(8,128)S(1)}, bf16[768,128]{1,0:T(8,128)(2,1)S(1)}) custom-call(bf16[20,24,256]{2,1,0:T(8,128)(2,1)S(1)} %constant_dynamic-slice_fusion.13.refs_0_, bf16[20,24,256]{2,1,0:T(8,128)(2,1)S(1)} %collective-permute-done.6.refs_1_, bf16[20,24,256]{2,1,0:T(8,128)(2,1)S(1)} %collective-permute-done.7.refs_2_, ...), custom_call_target="tpu_custom_call" | custom-call | flops 125829120 | bytes 983040 | tf_op jit(solution)/shard_map/packed_grams/pallas_call | solution.py:176
  31.6 0.0 collective-permute-done.refs_1_
  31.6 4.6 %collective-permute-start.11 = (bf16[768,128]{1,0:T(8,128)(2,1)S(1)}, bf16[768,128]{1,0:T(8,128)(2,1)S(1)}, u32[]{:S(2)}, u32[]{:S(2)}) collective-permute-start(bf16[768,128]{1,0:T(8,128)(2,1)S(1)} %get-tuple-element.44), channel_id=1, source_target_pairs={{0,7},{8,0},{16,8},{24,16},{25,24},{17,25},{9,17},{1,9},{2,1},{10,... | collective-permute-start | bytes 589832 | tf_op jit(solution)/shard_map/ppermute | solution.py:519
  36.3 0.0 collective-permute-done.2.refs_3_
  36.3 0.0 collective-permute-start.9
  36.3 0.0 collective-permute-done.1.refs_2_
  36.3 2.0 %packed_grams.2 = (f32[768,128]{1,0:T(8,128)S(1)}, bf16[768,128]{1,0:T(8,128)(2,1)S(1)}) custom-call(bf16[20,24,256]{2,1,0:T(8,128)(2,1)S(1)} %constant_dynamic-slice_fusion.9.refs_0_, bf16[20,24,256]{2,1,0:T(8,128)(2,1)S(1)} %collective-permute-done.refs_1_, bf16[20,24,256]{2,1,0:T(8,128)(2,1)S(1)} %collective-permute-done.1.refs_2_, ...), custom_call_target="tpu_custom_call" | custom-call | flops 125829120 | bytes 983040 | tf_op jit(solution)/shard_map/packed_grams/pallas_call | solution.py:176
  38.3 0.1 collective-permute-start.10
  38.5 0.0 collective-permute-done.5.refs_3_
  38.5 5.0 %collective-permute-start.18 = (bf16[768,128]{1,0:T(8,128)(2,1)S(1)}, bf16[768,128]{1,0:T(8,128)(2,1)S(1)}, u32[]{:S(2)}, u32[]{:S(2)}) collective-permute-start(bf16[768,128]{1,0:T(8,128)(2,1)S(1)} %get-tuple-element.45), channel_id=1, source_target_pairs={{0,7},{8,0},{16,8},{24,16},{25,24},{17,25},{9,17},{1,9},{2,1},{10,... | collective-permute-start | bytes 589832 | tf_op jit(solution)/shard_map/ppermute | solution.py:519
  43.5 0.0 collective-permute-done.4.refs_2_
  43.5 0.0 collective-permute-start.17
  43.5 3.2 %collective-permute-done.10.refs_1_.refs_0_ = bf16[768,128]{1,0:T(8,128)(2,1)S(1)} collective-permute-done((bf16[768,128]{1,0:T(8,128)(2,1)S(1)}, bf16[768,128]{1,0:T(8,128)(2,1)S(1)}, u32[]{:S(2)}, u32[]{:S(2)}) %collective-permute-start.10) | collective-permute-done | bytes 196640 | tf_op jit(solution)/shard_map/ppermute | solution.py:518
  46.7 0.0 collective-permute-start.16
  46.7 0.0 collective-permute-done.11.refs_4_.refs_3_
  46.8 0.5 collective-permute-start.15
  47.3 0.1 add_divide_fusion.taper_ref
  47.4 8.3 %blends.2.refs_4_ = bf16[1920,128]{1,0:T(8,128)(2,1)S(1)} custom-call(s32[48,16]{1,0:T(8,128)S(1)} %add_multiply_fusion.row_ref, f32[48,16]{1,0:T(8,128)S(1)} %add_divide_fusion.taper_ref, bf16[768,128]{1,0:T(8,128)(2,1)S(1)} %collective-permute-done.9.refs_0_, bf16[768,128]{1,0:T(8,128)(2,1)S(1)} %collective-permute-done.10.refs_1_.refs_0_, ...), custom_call_target="tpu_custom_call" | custom-call | flops 471859200 | bytes 1474560 | tf_op jit(solution)/shard_map/blends/pallas_call | solution.py:322
  55.6 0.0 collective-permute-done.3.refs_1_
  55.6 1.4 %apply_blend.2 = (bf16[20,24,256]{2,1,0:T(8,128)(2,1)S(1)}, bf16[20,24,256]{2,1,0:T(8,128)(2,1)S(1)}, bf16[20,24,256]{2,1,0:T(8,128)(2,1)S(1)}, bf16[20,24,256]{2,1,0:T(8,128)(2,1)S(1)}) custom-call(bf16[20,24,256]{2,1,0:T(8,128)(2,1)S(1)} %constant_dynamic-slice_fusion.7.refs_0_, bf16[20,24,256]{2,1,0:T(8,128)(2,1)S(1)} %collective-permute-done.3.refs_1_, ...), custom_call_target="tpu_custom_call" | custom-call | flops 125829120 | bytes 1966080 | tf_op jit(solution)/shard_map/apply_blend/pallas_call | solution.py:411
  57.1 0.1 collective-permute-start.12
  57.3 0.0 collective-permute-done.18.refs_4_
  57.3 8.3 %blends.3.refs_4_ = bf16[1920,128]{1,0:T(8,128)(2,1)S(1)} custom-call(s32[48,16]{1,0:T(8,128)S(1)} %add_multiply_fusion.row_ref, f32[48,16]{1,0:T(8,128)S(1)} %add_divide_fusion.taper_ref, bf16[768,128]{1,0:T(8,128)(2,1)S(1)} %collective-permute-done.10.refs_1_.refs_0_, f32[768,128]{1,0:T(8,128)S(1)} %get-tuple-element.46.refs_2_.refs_1_, ...), custom_call_target="tpu_custom_call" | custom-call | flops 471859200 | bytes 1474560 | tf_op jit(solution)/shard_map/blends/pallas_call | solution.py:322
  65.6 2.1 %collective-permute-start.13 = (bf16[20,24,256]{2,1,0:T(8,128)(2,1)S(1)}, bf16[20,24,256]{2,1,0:T(8,128)(2,1)S(1)}, u32[]{:S(2)}, u32[]{:S(2)}) collective-permute-start(bf16[20,24,256]{2,1,0:T(8,128)(2,1)S(1)} %get-tuple-element.49), channel_id=1, source_target_pairs={{0,16},{8,24},{16,0},{24,8},{1,17},{9,25},{17,1},{25,9},{2,18},{10... | collective-permute-start | bytes 737288 | tf_op jit(solution)/shard_map/ppermute | solution.py:531
  67.7 0.0 collective-permute-done.15.refs_1_
  67.7 0.0 collective-permute-done.17.refs_3_
  67.7 0.0 collective-permute-done.16.refs_2_
  67.7 1.5 %apply_blend.3 = (bf16[20,24,256]{2,1,0:T(8,128)(2,1)S(1)}, bf16[20,24,256]{2,1,0:T(8,128)(2,1)S(1)}, bf16[20,24,256]{2,1,0:T(8,128)(2,1)S(1)}, bf16[20,24,256]{2,1,0:T(8,128)(2,1)S(1)}) custom-call(bf16[20,24,256]{2,1,0:T(8,128)(2,1)S(1)} %constant_dynamic-slice_fusion.refs_0_, bf16[20,24,256]{2,1,0:T(8,128)(2,1)S(1)} %collective-permute-done.15.refs_1_, ...), custom_call_target="tpu_custom_call" | custom-call | flops 125829120 | bytes 1966080 | tf_op jit(solution)/shard_map/apply_blend/pallas_call | solution.py:411
  69.1 0.2 collective-permute-start.19
  69.4 0.3 collective-permute-start.20
  69.7 1.4 %collective-permute-start.14 = (bf16[20,24,256]{2,1,0:T(8,128)(2,1)S(1)}, bf16[20,24,256]{2,1,0:T(8,128)(2,1)S(1)}, u32[]{:S(2)}, u32[]{:S(2)}) collective-permute-start(bf16[20,24,256]{2,1,0:T(8,128)(2,1)S(1)} %get-tuple-element.50), channel_id=1, source_target_pairs={{0,24},{8,16},{16,8},{24,0},{1,25},{9,17},{17,9},{25,1},{2,26},{10... | collective-permute-start | bytes 737288 | tf_op jit(solution)/shard_map/ppermute | solution.py:531
  71.1 0.2 broadcast_in_dim.2
  71.3 0.0 collective-permute-done.12
  71.3 0.4 collective-permute-start.21
  71.8 2.7 %collective-permute-done.13 = bf16[20,24,256]{2,1,0:T(8,128)(2,1)S(1)} collective-permute-done((bf16[20,24,256]{2,1,0:T(8,128)(2,1)S(1)}, bf16[20,24,256]{2,1,0:T(8,128)(2,1)S(1)}, u32[]{:S(2)}, u32[]{:S(2)}) %collective-permute-start.13) | collective-permute-done | bytes 245792 | tf_op jit(solution)/shard_map/ppermute | solution.py:531
  74.5 10.0 %collective-permute-done.14 = bf16[20,24,256]{2,1,0:T(8,128)(2,1)S(1)} collective-permute-done((bf16[20,24,256]{2,1,0:T(8,128)(2,1)S(1)}, bf16[20,24,256]{2,1,0:T(8,128)(2,1)S(1)}, u32[]{:S(2)}, u32[]{:S(2)}) %collective-permute-start.14) | collective-permute-done | bytes 245792 | tf_op jit(solution)/shard_map/ppermute | solution.py:531
  84.7 0.0 copy-start.2
  84.7 5.1 %collective-permute-done.21 = bf16[20,24,256]{2,1,0:T(8,128)(2,1)S(1)} collective-permute-done((bf16[20,24,256]{2,1,0:T(8,128)(2,1)S(1)}, bf16[20,24,256]{2,1,0:T(8,128)(2,1)S(1)}, u32[]{:S(2)}, u32[]{:S(2)}) %collective-permute-start.21) | collective-permute-done | bytes 245792 | tf_op jit(solution)/shard_map/ppermute | solution.py:531
  89.8 0.7 constant_dynamic-update-slice_fusion
  (26 shorter events, 0.4 us)
Async XLA Ops:
  0.0 13.1 %copy-start = (s32[192,16]{0,1:T(8,128)S(1)}, s32[192,16]{0,1:T(8,128)}, u32[]{:S(2)}) copy-start(s32[192,16]{0,1:T(8,128)} %param.11) | copy-start | bytes 36868
  2.7 14.8 %collective-permute-start.8 = (bf16[20,24,256]{2,1,0:T(8,128)(2,1)}, bf16[20,24,256]{2,1,0:T(8,128)(2,1)S(1)}, u32[]{:S(2)}, u32[]{:S(2)}) collective-permute-start(bf16[20,24,256]{2,1,0:T(8,128)(2,1)} %picked.1), channel_id=1, source_target_pairs={{0,24},{8,16},{16,8},{24,0},{1,25},{9,17},{17,9},{25,1},{2,26},{10... | collective-permute-start | bytes 737288 | tf_op jit(solution)/shard_map/ppermute | solution.py:489
  5.1 11.3 %copy-start.3 = (s32[192]{0:T(256)S(1)}, s32[192]{0:T(256)}, u32[]{:S(2)}) copy-start(s32[192]{0:T(256)} %param.10) | copy-start | bytes 2308
  6.1 9.2 %collective-permute-start.6 = (bf16[20,24,256]{2,1,0:T(8,128)(2,1)S(1)}, bf16[20,24,256]{2,1,0:T(8,128)(2,1)S(1)}, u32[]{:S(2)}, u32[]{:S(2)}) collective-permute-start(bf16[20,24,256]{2,1,0:T(8,128)(2,1)S(1)} %constant_dynamic-slice_fusion.14), channel_id=1, source_target_pairs={{0,8},{8,0},{16,24},{24,16},{1,9},{9,1},{17,25},{25,17},{2,10},{10... | collective-permute-start | bytes 737288 | tf_op jit(solution)/shard_map/ppermute | solution.py:489
  8.8 27.5 %collective-permute-start.1 = (bf16[20,24,256]{2,1,0:T(8,128)(2,1)S(1)}, bf16[20,24,256]{2,1,0:T(8,128)(2,1)S(1)}, u32[]{:S(2)}, u32[]{:S(2)}) collective-permute-start(bf16[20,24,256]{2,1,0:T(8,128)(2,1)S(1)} %constant_dynamic-slice_fusion.12), channel_id=1, source_target_pairs={{0,16},{8,24},{16,0},{24,8},{1,17},{9,25},{17,1},{25,9},{2,18},{10... | collective-permute-start | bytes 737288 | tf_op jit(solution)/shard_map/ppermute | solution.py:489
  9.9 26.4 %collective-permute-start.2 = (bf16[20,24,256]{2,1,0:T(8,128)(2,1)S(1)}, bf16[20,24,256]{2,1,0:T(8,128)(2,1)S(1)}, u32[]{:S(2)}, u32[]{:S(2)}) collective-permute-start(bf16[20,24,256]{2,1,0:T(8,128)(2,1)S(1)} %constant_dynamic-slice_fusion.11), channel_id=1, source_target_pairs={{0,24},{8,16},{16,8},{24,0},{1,25},{9,17},{17,9},{25,1},{2,26},{10... | collective-permute-start | bytes 737288 | tf_op jit(solution)/shard_map/ppermute | solution.py:489
  12.2 19.4 %collective-permute-start = (bf16[20,24,256]{2,1,0:T(8,128)(2,1)S(1)}, bf16[20,24,256]{2,1,0:T(8,128)(2,1)S(1)}, u32[]{:S(2)}, u32[]{:S(2)}) collective-permute-start(bf16[20,24,256]{2,1,0:T(8,128)(2,1)S(1)} %constant_dynamic-slice_fusion.10), channel_id=1, source_target_pairs={{0,8},{8,0},{16,24},{24,16},{1,9},{9,1},{17,25},{25,17},{2,10},{10... | collective-permute-start | bytes 737288 | tf_op jit(solution)/shard_map/ppermute | solution.py:489
  15.2 23.1 %copy-start.1 = (bf16[20,192,256]{2,1,0:T(8,128)(2,1)S(1)}, bf16[20,192,256]{2,1,0:T(8,128)(2,1)}, u32[]{:S(2)}) copy-start(bf16[20,192,256]{2,1,0:T(8,128)(2,1)} %param.6) | copy-start | bytes 5898244
  15.3 12.9 %collective-permute-start.7 = (bf16[20,24,256]{2,1,0:T(8,128)(2,1)S(1)}, bf16[20,24,256]{2,1,0:T(8,128)(2,1)S(1)}, u32[]{:S(2)}, u32[]{:S(2)}) collective-permute-start(bf16[20,24,256]{2,1,0:T(8,128)(2,1)S(1)} %constant_dynamic-slice_fusion.15), channel_id=1, source_target_pairs={{0,16},{8,24},{16,0},{24,8},{1,17},{9,25},{17,1},{25,9},{2,18},{10... | collective-permute-start | bytes 737288 | tf_op jit(solution)/shard_map/ppermute | solution.py:489
  17.5 26.0 %collective-permute-start.4 = (bf16[20,24,256]{2,1,0:T(8,128)(2,1)S(1)}, bf16[20,24,256]{2,1,0:T(8,128)(2,1)S(1)}, u32[]{:S(2)}, u32[]{:S(2)}) collective-permute-start(bf16[20,24,256]{2,1,0:T(8,128)(2,1)S(1)} %constant_dynamic-slice_fusion.6), channel_id=1, source_target_pairs={{0,16},{8,24},{16,0},{24,8},{1,17},{9,25},{17,1},{25,9},{2,18},{10... | collective-permute-start | bytes 737288 | tf_op jit(solution)/shard_map/ppermute | solution.py:489
  28.2 10.3 %collective-permute-start.5 = (bf16[20,24,256]{2,1,0:T(8,128)(2,1)S(1)}, bf16[20,24,256]{2,1,0:T(8,128)(2,1)S(1)}, u32[]{:S(2)}, u32[]{:S(2)}) collective-permute-start(bf16[20,24,256]{2,1,0:T(8,128)(2,1)S(1)} %constant_dynamic-slice_fusion.5), channel_id=1, source_target_pairs={{0,24},{8,16},{16,8},{24,0},{1,25},{9,17},{17,9},{25,1},{2,26},{10... | collective-permute-start | bytes 737288 | tf_op jit(solution)/shard_map/ppermute | solution.py:489
  31.6 15.1 %collective-permute-start.11 = (bf16[768,128]{1,0:T(8,128)(2,1)S(1)}, bf16[768,128]{1,0:T(8,128)(2,1)S(1)}, u32[]{:S(2)}, u32[]{:S(2)}) collective-permute-start(bf16[768,128]{1,0:T(8,128)(2,1)S(1)} %get-tuple-element.44), channel_id=1, source_target_pairs={{0,7},{8,0},{16,8},{24,16},{25,24},{17,25},{9,17},{1,9},{2,1},{10,... | collective-permute-start | bytes 589832 | tf_op jit(solution)/shard_map/ppermute | solution.py:519
  36.3 10.5 %collective-permute-start.9 = (bf16[768,128]{1,0:T(8,128)(2,1)S(1)}, bf16[768,128]{1,0:T(8,128)(2,1)S(1)}, u32[]{:S(2)}, u32[]{:S(2)}) collective-permute-start(bf16[768,128]{1,0:T(8,128)(2,1)S(1)} %get-tuple-element.44), channel_id=1, source_target_pairs={{0,8},{8,16},{16,24},{24,25},{25,17},{17,9},{9,1},{1,2},{2,10},{10... | collective-permute-start | bytes 589832 | tf_op jit(solution)/shard_map/ppermute | solution.py:518
  38.3 8.5 %collective-permute-start.10 = (bf16[768,128]{1,0:T(8,128)(2,1)S(1)}, bf16[768,128]{1,0:T(8,128)(2,1)S(1)}, u32[]{:S(2)}, u32[]{:S(2)}) collective-permute-start(bf16[768,128]{1,0:T(8,128)(2,1)S(1)} %get-tuple-element.45), channel_id=1, source_target_pairs={{0,8},{8,16},{16,24},{24,25},{25,17},{17,9},{9,1},{1,2},{2,10},{10... | collective-permute-start | bytes 589832 | tf_op jit(solution)/shard_map/ppermute | solution.py:518
  38.5 18.7 %collective-permute-start.18 = (bf16[768,128]{1,0:T(8,128)(2,1)S(1)}, bf16[768,128]{1,0:T(8,128)(2,1)S(1)}, u32[]{:S(2)}, u32[]{:S(2)}) collective-permute-start(bf16[768,128]{1,0:T(8,128)(2,1)S(1)} %get-tuple-element.45), channel_id=1, source_target_pairs={{0,7},{8,0},{16,8},{24,16},{25,24},{17,25},{9,17},{1,9},{2,1},{10,... | collective-permute-start | bytes 589832 | tf_op jit(solution)/shard_map/ppermute | solution.py:519
  43.5 24.2 %collective-permute-start.17 = (bf16[20,24,256]{2,1,0:T(8,128)(2,1)S(1)}, bf16[20,24,256]{2,1,0:T(8,128)(2,1)S(1)}, u32[]{:S(2)}, u32[]{:S(2)}) collective-permute-start(bf16[20,24,256]{2,1,0:T(8,128)(2,1)S(1)} %constant_dynamic-slice_fusion.2), channel_id=1, source_target_pairs={{0,24},{8,16},{16,8},{24,0},{1,25},{9,17},{17,9},{25,1},{2,26},{10... | collective-permute-start | bytes 737288 | tf_op jit(solution)/shard_map/ppermute | solution.py:489
  46.7 20.9 %collective-permute-start.16 = (bf16[20,24,256]{2,1,0:T(8,128)(2,1)S(1)}, bf16[20,24,256]{2,1,0:T(8,128)(2,1)S(1)}, u32[]{:S(2)}, u32[]{:S(2)}) collective-permute-start(bf16[20,24,256]{2,1,0:T(8,128)(2,1)S(1)} %constant_dynamic-slice_fusion.3), channel_id=1, source_target_pairs={{0,16},{8,24},{16,0},{24,8},{1,17},{9,25},{17,1},{25,9},{2,18},{10... | collective-permute-start | bytes 737288 | tf_op jit(solution)/shard_map/ppermute | solution.py:489
  46.7 8.9 %collective-permute-start.3 = (bf16[20,24,256]{2,1,0:T(8,128)(2,1)S(1)}, bf16[20,24,256]{2,1,0:T(8,128)(2,1)S(1)}, u32[]{:S(2)}, u32[]{:S(2)}) collective-permute-start(bf16[20,24,256]{2,1,0:T(8,128)(2,1)S(1)} %constant_dynamic-slice_fusion.8), channel_id=1, source_target_pairs={{0,8},{8,0},{16,24},{24,16},{1,9},{9,1},{17,25},{25,17},{2,10},{10... | collective-permute-start | bytes 737288 | tf_op jit(solution)/shard_map/ppermute | solution.py:489
  46.8 20.9 %collective-permute-start.15 = (bf16[20,24,256]{2,1,0:T(8,128)(2,1)S(1)}, bf16[20,24,256]{2,1,0:T(8,128)(2,1)S(1)}, u32[]{:S(2)}, u32[]{:S(2)}) collective-permute-start(bf16[20,24,256]{2,1,0:T(8,128)(2,1)S(1)} %constant_dynamic-slice_fusion.1), channel_id=1, source_target_pairs={{0,8},{8,0},{16,24},{24,16},{1,9},{9,1},{17,25},{25,17},{2,10},{10... | collective-permute-start | bytes 737288 | tf_op jit(solution)/shard_map/ppermute | solution.py:489
  57.1 14.2 %collective-permute-start.12 = (bf16[20,24,256]{2,1,0:T(8,128)(2,1)S(1)}, bf16[20,24,256]{2,1,0:T(8,128)(2,1)S(1)}, u32[]{:S(2)}, u32[]{:S(2)}) collective-permute-start(bf16[20,24,256]{2,1,0:T(8,128)(2,1)S(1)} %get-tuple-element.48), channel_id=1, source_target_pairs={{0,8},{8,0},{16,24},{24,16},{1,9},{9,1},{17,25},{25,17},{2,10},{10... | collective-permute-start | bytes 737288 | tf_op jit(solution)/shard_map/ppermute | solution.py:531
  65.6 8.9 %collective-permute-start.13 = (bf16[20,24,256]{2,1,0:T(8,128)(2,1)S(1)}, bf16[20,24,256]{2,1,0:T(8,128)(2,1)S(1)}, u32[]{:S(2)}, u32[]{:S(2)}) collective-permute-start(bf16[20,24,256]{2,1,0:T(8,128)(2,1)S(1)} %get-tuple-element.49), channel_id=1, source_target_pairs={{0,16},{8,24},{16,0},{24,8},{1,17},{9,25},{17,1},{25,9},{2,18},{10... | collective-permute-start | bytes 737288 | tf_op jit(solution)/shard_map/ppermute | solution.py:531
  69.1 15.5 %collective-permute-start.19 = (bf16[20,24,256]{2,1,0:T(8,128)(2,1)S(1)}, bf16[20,24,256]{2,1,0:T(8,128)(2,1)S(1)}, u32[]{:S(2)}, u32[]{:S(2)}) collective-permute-start(bf16[20,24,256]{2,1,0:T(8,128)(2,1)S(1)} %get-tuple-element.56), channel_id=1, source_target_pairs={{0,8},{8,0},{16,24},{24,16},{1,9},{9,1},{17,25},{25,17},{2,10},{10... | collective-permute-start | bytes 737288 | tf_op jit(solution)/shard_map/ppermute | solution.py:531
  69.4 15.3 %collective-permute-start.20 = (bf16[20,24,256]{2,1,0:T(8,128)(2,1)S(1)}, bf16[20,24,256]{2,1,0:T(8,128)(2,1)S(1)}, u32[]{:S(2)}, u32[]{:S(2)}) collective-permute-start(bf16[20,24,256]{2,1,0:T(8,128)(2,1)S(1)} %get-tuple-element.57), channel_id=1, source_target_pairs={{0,16},{8,24},{16,0},{24,8},{1,17},{9,25},{17,1},{25,9},{2,18},{10... | collective-permute-start | bytes 737288 | tf_op jit(solution)/shard_map/ppermute | solution.py:531
  69.7 14.9 %collective-permute-start.14 = (bf16[20,24,256]{2,1,0:T(8,128)(2,1)S(1)}, bf16[20,24,256]{2,1,0:T(8,128)(2,1)S(1)}, u32[]{:S(2)}, u32[]{:S(2)}) collective-permute-start(bf16[20,24,256]{2,1,0:T(8,128)(2,1)S(1)} %get-tuple-element.50), channel_id=1, source_target_pairs={{0,24},{8,16},{16,8},{24,0},{1,25},{9,17},{17,9},{25,1},{2,26},{10... | collective-permute-start | bytes 737288 | tf_op jit(solution)/shard_map/ppermute | solution.py:531
  71.3 18.4 %collective-permute-start.21 = (bf16[20,24,256]{2,1,0:T(8,128)(2,1)S(1)}, bf16[20,24,256]{2,1,0:T(8,128)(2,1)S(1)}, u32[]{:S(2)}, u32[]{:S(2)}) collective-permute-start(bf16[20,24,256]{2,1,0:T(8,128)(2,1)S(1)} %get-tuple-element.58), channel_id=1, source_target_pairs={{0,24},{8,16},{16,8},{24,0},{1,25},{9,17},{17,9},{25,1},{2,26},{10... | collective-permute-start | bytes 737288 | tf_op jit(solution)/shard_map/ppermute | solution.py:531
  84.7 5.1 %copy-start.2 = (bf16[20,192,256]{2,1,0:T(8,128)(2,1)}, bf16[20,192,256]{2,1,0:T(8,128)(2,1)S(1)}, u32[]{:S(2)}) copy-start(bf16[20,192,256]{2,1,0:T(8,128)(2,1)S(1)} %constant_dynamic-update-slice_fusion.1) | copy-start | bytes 5898244

commit v8 on v7

--- a/solution.py
+++ b/solution.py
@@ -495,7 +495,6 @@
     spread_taken = sliced(scaled_sensor_spread, everything[:1])
     (last,) = picked(after(scaled_sensor_spread, last), everything[1:2], groups, size)
     spread_taken |= {everything[1]: last} | sliced(scaled_sensor_spread, everything[2:])
-    field_taken = sliced(prior_fields, everything[:2])
     spread_parts = [exchanged(spread_taken, c) for c in chunks]
 
     slot_ids = jnp.arange(width, dtype=jnp.int32)
@@ -515,10 +514,13 @@
             spread_parts[c], obs_scale, weighted, c * size
         )
         own.append(here)
+        if c == 0:
+            last = here
+            field_taken = sliced(prior_fields, everything[:1])
         left.append(lax.ppermute(packed, ("mem", "lon"), forward))
         right.append(lax.ppermute(packed, ("mem", "lon"), backward))
     last = own[-1]
-    field_taken |= sliced(prior_fields, everything[2:])
+    field_taken |= sliced(prior_fields, everything[1:])
     field_parts = [exchanged(field_taken, c) for c in chunks]
     window = left + own + right
 

time: 90.9 us -> 99.4 us (1.094)
  waiting for transfers between devices: 29.9 us -> 42.6 us
  starting transfers between devices: 23.7 us -> 19.4 us
    ppermute x2, waiting for transfers between devices: 3.23 us -> 10.3 us  [on_device(): left.append(lax.ppermute(packed, ('mem', 'lon'), forward))]
    ppermute x12, waiting for transfers between devices: 8.82 us -> 14.7 us  [exchanged(): parts = {d: lax.ppermute(taken[d, c], 'mem', peers[d]) for d in far_first}]
    ppermute x2, starting transfers between devices: 9.58 us -> 4.62 us  [on_device(): right.append(lax.ppermute(packed, ('mem', 'lon'), backward))]
    ppermute x12, starting transfers between devices: 9.51 us -> 10.6 us  [exchanged(): parts = {d: lax.ppermute(taken[d, c], 'mem', peers[d]) for d in far_first}]
  transfers between devices with their start and end apart: 22 -> 22, of which waited for: 5 -> 6; matrix products, arithmetic and copies ran while one was open for 11% -> 10% of each run, Pallas kernels for 26% -> 24%
where the time goes in v8:
time: 99.4 us; the launch traced here: 99 us
  waiting for transfers between devices  42.6 us (43%)
  Pallas kernels  25.1 us (25%)
  starting transfers between devices  19.4 us (20%)
  local copies, waits for them, and re-layouts  10.2 us (10%)
  other arithmetic  1.25 us (1%)
    ppermute x6, waiting for transfers between devices, on_device(): came.append((d, c, lax.ppermute(out_parts[d], 'mem', peers[d])))  17.6 us
    pallas_call x2, Pallas kernels, blends(): pl.pallas_call(functools.partial(blend_kernel, members=members, neighbour...  16.6 us
    ppermute x12, waiting for transfers between devices, exchanged(): parts = {d: lax.ppermute(taken[d, c], 'mem', peers[d]) for d in far_first}  14.7 us
    ppermute x12, starting transfers between devices, exchanged(): parts = {d: lax.ppermute(taken[d, c], 'mem', peers[d]) for d in far_first}  10.6 us
    ppermute x2, waiting for transfers between devices, on_device(): left.append(lax.ppermute(packed, ('mem', 'lon'), forward))  10.3 us
    dynamic_slice x15, local copies, waits for them, and re-layouts, sliced(): last = taken[d, c] = lax.dynamic_slice_in_dim(x, start, size, 1)  8.91 us
    ppermute x2, starting transfers between devices, on_device(): right.append(lax.ppermute(packed, ('mem', 'lon'), backward))  4.62 us
    ppermute x6, starting transfers between devices, on_device(): came.append((d, c, lax.ppermute(out_parts[d], 'mem', peers[d])))  4.24 us
  transfers between devices with their start and end apart: 22, of which 6 were waited for; matrix products, arithmetic and copies ran while one was open for 10% of the time, Pallas kernels for 24%

profile of v8, /device:TPU:0, one launch (start us, length us, event | category | flops | bytes accessed | tf_op | source)
XLA Modules:
  0.0 99.0 jit_solution(4309005031143771507)
XLA Ops:
  0.0 1.0 constant_dynamic-slice_fusion.15
  1.0 1.7 %picked.1 = bf16[20,24,256]{2,1,0:T(8,128)(2,1)} custom-call(bf16[20,192,256]{2,1,0:T(8,128)(2,1)} %whole_ref), custom_call_target="tpu_custom_call" | custom-call | bytes 491520 | tf_op jit(solution)/shard_map/picked/pallas_call | solution.py:59
  2.7 0.0 copy-start.3
  2.7 2.5 %collective-permute-start.6 = (bf16[20,24,256]{2,1,0:T(8,128)(2,1)}, bf16[20,24,256]{2,1,0:T(8,128)(2,1)S(1)}, u32[]{:S(2)}, u32[]{:S(2)}) collective-permute-start(bf16[20,24,256]{2,1,0:T(8,128)(2,1)} %picked.1), channel_id=1, source_target_pairs={{0,24},{8,16},{16,8},{24,0},{1,25},{9,17},{17,9},{25,1},{2,26},{10... | collective-permute-start | bytes 737288 | tf_op jit(solution)/shard_map/ppermute | solution.py:489
  5.1 1.0 constant_dynamic-slice_fusion.14
  6.1 0.7 collective-permute-start.4
  6.8 1.0 constant_dynamic-slice_fusion.13.refs_0_
  7.8 1.0 constant_dynamic-slice_fusion.12
  8.8 0.1 collective-permute-start.1
  8.9 1.0 constant_dynamic-slice_fusion.11
  9.9 1.4 %collective-permute-start.2 = (bf16[20,24,256]{2,1,0:T(8,128)(2,1)S(1)}, bf16[20,24,256]{2,1,0:T(8,128)(2,1)S(1)}, u32[]{:S(2)}, u32[]{:S(2)}) collective-permute-start(bf16[20,24,256]{2,1,0:T(8,128)(2,1)S(1)} %constant_dynamic-slice_fusion.11), channel_id=1, source_target_pairs={{0,24},{8,16},{16,8},{24,0},{1,25},{9,17},{17,9},{25,1},{2,26},{10... | collective-permute-start | bytes 737288 | tf_op jit(solution)/shard_map/ppermute | solution.py:489
  11.3 1.0 constant_dynamic-slice_fusion.10
  12.2 0.8 collective-permute-start
  13.1 0.1 constant_dynamic-slice_fusion.4
  13.2 0.1 copy.8
  13.2 0.1 add_multiply_fusion.row_ref
  13.3 1.0 constant_dynamic-slice_fusion.9.refs_0_
  14.3 0.1 dynamic_slice.64
  14.4 1.1 %dynamic-slice_multiply_fusion = (f32[48,256]{1,0:T(8,128)S(1)}, f32[48,256]{1,0:T(8,128)S(1)}) fusion(f32[192,256]{1,0:T(8,128)} %param.8, s32[]{:T(128)S(6)} %select_n.74, f32[192,256]{1,0:T(8,128)} %param.9, s32[48]{0:T(128)S(1)} %dynamic_slice.64), kind=kLoop, calls=%fused_computation.1 | loop fusion | flops 36864 | bytes 196804 | tf_op jit(solution)/shard_map/mul | solution.py:503
  15.5 0.0 collective-permute-done.refs_1_
  15.5 0.1 collective-permute-start.5
  15.6 6.6 %collective-permute-done.2.refs_3_ = bf16[20,24,256]{2,1,0:T(8,128)(2,1)S(1)} collective-permute-done((bf16[20,24,256]{2,1,0:T(8,128)(2,1)S(1)}, bf16[20,24,256]{2,1,0:T(8,128)(2,1)S(1)}, u32[]{:S(2)}, u32[]{:S(2)}) %collective-permute-start.2) | collective-permute-done | bytes 245792 | tf_op jit(solution)/shard_map/ppermute | solution.py:489
  22.2 0.0 collective-permute-done.1.refs_2_
  22.2 2.0 %packed_grams.2 = (f32[768,128]{1,0:T(8,128)S(1)}, bf16[768,128]{1,0:T(8,128)(2,1)S(1)}) custom-call(bf16[20,24,256]{2,1,0:T(8,128)(2,1)S(1)} %constant_dynamic-slice_fusion.9.refs_0_, bf16[20,24,256]{2,1,0:T(8,128)(2,1)S(1)} %collective-permute-done.refs_1_, bf16[20,24,256]{2,1,0:T(8,128)(2,1)S(1)} %collective-permute-done.1.refs_2_, ...), custom_call_target="tpu_custom_call" | custom-call | flops 125829120 | bytes 983040 | tf_op jit(solution)/shard_map/packed_grams/pallas_call | solution.py:176
  24.2 1.0 constant_dynamic-slice_fusion.8
  25.2 1.0 constant_dynamic-slice_fusion.7
  26.2 0.6 collective-permute-start.3
  26.8 2.0 %collective-permute-start.8 = (bf16[20,24,256]{2,1,0:T(8,128)(2,1)S(1)}, bf16[20,24,256]{2,1,0:T(8,128)(2,1)S(1)}, u32[]{:S(2)}, u32[]{:S(2)}) collective-permute-start(bf16[20,24,256]{2,1,0:T(8,128)(2,1)S(1)} %constant_dynamic-slice_fusion.8), channel_id=1, source_target_pairs={{0,24},{8,16},{16,8},{24,0},{1,25},{9,17},{17,9},{25,1},{2,26},{10... | collective-permute-start | bytes 737288 | tf_op jit(solution)/shard_map/ppermute | solution.py:489
  28.8 0.0 collective-permute-done.4.refs_1_
  28.8 0.0 collective-permute-done.6.refs_3_
  28.8 0.0 collective-permute-done.5.refs_2_
  28.8 2.0 %packed_grams.3 = (f32[768,128]{1,0:T(8,128)S(1)}, bf16[768,128]{1,0:T(8,128)(2,1)S(1)}) custom-call(bf16[20,24,256]{2,1,0:T(8,128)(2,1)S(1)} %constant_dynamic-slice_fusion.13.refs_0_, bf16[20,24,256]{2,1,0:T(8,128)(2,1)S(1)} %collective-permute-done.4.refs_1_, bf16[20,24,256]{2,1,0:T(8,128)(2,1)S(1)} %collective-permute-done.5.refs_2_, ...), custom_call_target="tpu_custom_call" | custom-call | flops 125829120 | bytes 983040 | tf_op jit(solution)/shard_map/packed_grams/pallas_call | solution.py:176
  30.8 4.6 %collective-permute-start.11 = (bf16[768,128]{1,0:T(8,128)(2,1)S(1)}, bf16[768,128]{1,0:T(8,128)(2,1)S(1)}, u32[]{:S(2)}, u32[]{:S(2)}) collective-permute-start(bf16[768,128]{1,0:T(8,128)(2,1)S(1)} %get-tuple-element.45), channel_id=1, source_target_pairs={{0,7},{8,0},{16,8},{24,16},{25,24},{17,25},{9,17},{1,9},{2,1},{10,... | collective-permute-start | bytes 589832 | tf_op jit(solution)/shard_map/ppermute | solution.py:521
  35.4 0.0 collective-permute-start.9
  35.4 0.0 collective-permute-start.10
  35.6 10.3 %collective-permute-done.10.refs_1_.refs_0_ = bf16[768,128]{1,0:T(8,128)(2,1)S(1)} collective-permute-done((bf16[768,128]{1,0:T(8,128)(2,1)S(1)}, bf16[768,128]{1,0:T(8,128)(2,1)S(1)}, u32[]{:S(2)}, u32[]{:S(2)}) %collective-permute-start.10) | collective-permute-done | bytes 196640 | tf_op jit(solution)/shard_map/ppermute | solution.py:520
  45.9 0.0 collective-permute-start.18
  45.9 0.0 collective-permute-done.11.refs_4_.refs_3_
  45.9 2.1 %collective-permute-start.16 = (bf16[20,24,256]{2,1,0:T(8,128)(2,1)S(1)}, bf16[20,24,256]{2,1,0:T(8,128)(2,1)S(1)}, u32[]{:S(2)}, u32[]{:S(2)}) collective-permute-start(bf16[20,24,256]{2,1,0:T(8,128)(2,1)S(1)} %constant_dynamic-slice_fusion.3), channel_id=1, source_target_pairs={{0,16},{8,24},{16,0},{24,8},{1,17},{9,25},{17,1},{25,9},{2,18},{10... | collective-permute-start | bytes 737288 | tf_op jit(solution)/shard_map/ppermute | solution.py:489
  48.0 0.2 collective-permute-start.7
  48.2 0.1 add_divide_fusion.taper_ref
  48.3 8.3 %blends.2.refs_4_ = bf16[1920,128]{1,0:T(8,128)(2,1)S(1)} custom-call(s32[48,16]{1,0:T(8,128)S(1)} %add_multiply_fusion.row_ref, f32[48,16]{1,0:T(8,128)S(1)} %add_divide_fusion.taper_ref, bf16[768,128]{1,0:T(8,128)(2,1)S(1)} %collective-permute-done.9.refs_0_, bf16[768,128]{1,0:T(8,128)(2,1)S(1)} %collective-permute-done.10.refs_1_.refs_0_, ...), custom_call_target="tpu_custom_call" | custom-call | flops 471859200 | bytes 1474560 | tf_op jit(solution)/shard_map/blends/pallas_call | solution.py:322
  56.6 8.1 %collective-permute-done.7.refs_2_ = bf16[20,24,256]{2,1,0:T(8,128)(2,1)S(1)} collective-permute-done((bf16[20,24,256]{2,1,0:T(8,128)(2,1)S(1)}, bf16[20,24,256]{2,1,0:T(8,128)(2,1)S(1)}, u32[]{:S(2)}, u32[]{:S(2)}) %collective-permute-start.7) | collective-permute-done | bytes 245792 | tf_op jit(solution)/shard_map/ppermute | solution.py:489
  64.7 1.4 %apply_blend.2 = (bf16[20,24,256]{2,1,0:T(8,128)(2,1)S(1)}, bf16[20,24,256]{2,1,0:T(8,128)(2,1)S(1)}, bf16[20,24,256]{2,1,0:T(8,128)(2,1)S(1)}, bf16[20,24,256]{2,1,0:T(8,128)(2,1)S(1)}) custom-call(bf16[20,24,256]{2,1,0:T(8,128)(2,1)S(1)} %constant_dynamic-slice_fusion.6.refs_0_, bf16[20,24,256]{2,1,0:T(8,128)(2,1)S(1)} %collective-permute-done.3.refs_1_, ...), custom_call_target="tpu_custom_call" | custom-call | flops 125829120 | bytes 1966080 | tf_op jit(solution)/shard_map/apply_blend/pallas_call | solution.py:411
  66.1 0.1 collective-permute-start.12
  66.2 0.0 collective-permute-done.18.refs_4_
  66.3 8.3 %blends.3.refs_4_ = bf16[1920,128]{1,0:T(8,128)(2,1)S(1)} custom-call(s32[48,16]{1,0:T(8,128)S(1)} %add_multiply_fusion.row_ref, f32[48,16]{1,0:T(8,128)S(1)} %add_divide_fusion.taper_ref, bf16[768,128]{1,0:T(8,128)(2,1)S(1)} %collective-permute-done.10.refs_1_.refs_0_, f32[768,128]{1,0:T(8,128)S(1)} %get-tuple-element.43.refs_2_.refs_1_, ...), custom_call_target="tpu_custom_call" | custom-call | flops 471859200 | bytes 1474560 | tf_op jit(solution)/shard_map/blends/pallas_call | solution.py:322
  74.6 0.5 collective-permute-start.13
  75.0 0.0 collective-permute-done.15.refs_1_
  75.0 0.0 collective-permute-done.17.refs_3_
  75.0 0.0 collective-permute-done.16.refs_2_
  75.0 1.5 %apply_blend.3 = (bf16[20,24,256]{2,1,0:T(8,128)(2,1)S(1)}, bf16[20,24,256]{2,1,0:T(8,128)(2,1)S(1)}, bf16[20,24,256]{2,1,0:T(8,128)(2,1)S(1)}, bf16[20,24,256]{2,1,0:T(8,128)(2,1)S(1)}) custom-call(bf16[20,24,256]{2,1,0:T(8,128)(2,1)S(1)} %constant_dynamic-slice_fusion.refs_0_, bf16[20,24,256]{2,1,0:T(8,128)(2,1)S(1)} %collective-permute-done.15.refs_1_, ...), custom_call_target="tpu_custom_call" | custom-call | flops 125829120 | bytes 1966080 | tf_op jit(solution)/shard_map/apply_blend/pallas_call | solution.py:411
  76.5 0.3 collective-permute-start.19
  76.8 1.6 %collective-permute-start.20 = (bf16[20,24,256]{2,1,0:T(8,128)(2,1)S(1)}, bf16[20,24,256]{2,1,0:T(8,128)(2,1)S(1)}, u32[]{:S(2)}, u32[]{:S(2)}) collective-permute-start(bf16[20,24,256]{2,1,0:T(8,128)(2,1)S(1)} %get-tuple-element.57), channel_id=1, source_target_pairs={{0,16},{8,24},{16,0},{24,8},{1,17},{9,25},{17,1},{25,9},{2,18},{10... | collective-permute-start | bytes 737288 | tf_op jit(solution)/shard_map/ppermute | solution.py:533
  78.4 0.0 collective-permute-start.14
  78.4 0.2 broadcast_in_dim.2
  78.7 0.0 collective-permute-done.12
  78.7 1.8 %collective-permute-start.21 = (bf16[20,24,256]{2,1,0:T(8,128)(2,1)S(1)}, bf16[20,24,256]{2,1,0:T(8,128)(2,1)S(1)}, u32[]{:S(2)}, u32[]{:S(2)}) collective-permute-start(bf16[20,24,256]{2,1,0:T(8,128)(2,1)S(1)} %get-tuple-element.58), channel_id=1, source_target_pairs={{0,24},{8,16},{16,8},{24,0},{1,25},{9,17},{17,9},{25,1},{2,26},{10... | collective-permute-start | bytes 737288 | tf_op jit(solution)/shard_map/ppermute | solution.py:533
  80.5 3.0 %collective-permute-done.13 = bf16[20,24,256]{2,1,0:T(8,128)(2,1)S(1)} collective-permute-done((bf16[20,24,256]{2,1,0:T(8,128)(2,1)S(1)}, bf16[20,24,256]{2,1,0:T(8,128)(2,1)S(1)}, u32[]{:S(2)}, u32[]{:S(2)}) %collective-permute-start.13) | collective-permute-done | bytes 245792 | tf_op jit(solution)/shard_map/ppermute | solution.py:533
  83.5 9.5 %collective-permute-done.14 = bf16[20,24,256]{2,1,0:T(8,128)(2,1)S(1)} collective-permute-done((bf16[20,24,256]{2,1,0:T(8,128)(2,1)S(1)}, bf16[20,24,256]{2,1,0:T(8,128)(2,1)S(1)}, u32[]{:S(2)}, u32[]{:S(2)}) %collective-permute-start.14) | collective-permute-done | bytes 245792 | tf_op jit(solution)/shard_map/ppermute | solution.py:533
  93.1 0.0 collective-permute-done.20
  93.2 0.0 copy-start.2
  93.2 5.1 %collective-permute-done.21 = bf16[20,24,256]{2,1,0:T(8,128)(2,1)S(1)} collective-permute-done((bf16[20,24,256]{2,1,0:T(8,128)(2,1)S(1)}, bf16[20,24,256]{2,1,0:T(8,128)(2,1)S(1)}, u32[]{:S(2)}, u32[]{:S(2)}) %collective-permute-start.21) | collective-permute-done | bytes 245792 | tf_op jit(solution)/shard_map/ppermute | solution.py:533
  98.3 0.7 constant_dynamic-update-slice_fusion
  (26 shorter events, 0.4 us)
Async XLA Ops:
  0.0 13.1 %copy-start = (s32[192,16]{0,1:T(8,128)S(1)}, s32[192,16]{0,1:T(8,128)}, u32[]{:S(2)}) copy-start(s32[192,16]{0,1:T(8,128)} %param.11) | copy-start | bytes 36868
  2.7 11.7 %copy-start.3 = (s32[192]{0:T(256)S(1)}, s32[192]{0:T(256)}, u32[]{:S(2)}) copy-start(s32[192]{0:T(256)} %param.10) | copy-start | bytes 2308
  2.7 26.1 %collective-permute-start.6 = (bf16[20,24,256]{2,1,0:T(8,128)(2,1)}, bf16[20,24,256]{2,1,0:T(8,128)(2,1)S(1)}, u32[]{:S(2)}, u32[]{:S(2)}) collective-permute-start(bf16[20,24,256]{2,1,0:T(8,128)(2,1)} %picked.1), channel_id=1, source_target_pairs={{0,24},{8,16},{16,8},{24,0},{1,25},{9,17},{17,9},{25,1},{2,26},{10... | collective-permute-start | bytes 737288 | tf_op jit(solution)/shard_map/ppermute | solution.py:489
  6.1 22.7 %collective-permute-start.4 = (bf16[20,24,256]{2,1,0:T(8,128)(2,1)S(1)}, bf16[20,24,256]{2,1,0:T(8,128)(2,1)S(1)}, u32[]{:S(2)}, u32[]{:S(2)}) collective-permute-start(bf16[20,24,256]{2,1,0:T(8,128)(2,1)S(1)} %constant_dynamic-slice_fusion.14), channel_id=1, source_target_pairs={{0,8},{8,0},{16,24},{24,16},{1,9},{9,1},{17,25},{25,17},{2,10},{10... | collective-permute-start | bytes 737288 | tf_op jit(solution)/shard_map/ppermute | solution.py:489
  8.8 13.4 %collective-permute-start.1 = (bf16[20,24,256]{2,1,0:T(8,128)(2,1)S(1)}, bf16[20,24,256]{2,1,0:T(8,128)(2,1)S(1)}, u32[]{:S(2)}, u32[]{:S(2)}) collective-permute-start(bf16[20,24,256]{2,1,0:T(8,128)(2,1)S(1)} %constant_dynamic-slice_fusion.12), channel_id=1, source_target_pairs={{0,16},{8,24},{16,0},{24,8},{1,17},{9,25},{17,1},{25,9},{2,18},{10... | collective-permute-start | bytes 737288 | tf_op jit(solution)/shard_map/ppermute | solution.py:489
  9.9 12.4 %collective-permute-start.2 = (bf16[20,24,256]{2,1,0:T(8,128)(2,1)S(1)}, bf16[20,24,256]{2,1,0:T(8,128)(2,1)S(1)}, u32[]{:S(2)}, u32[]{:S(2)}) collective-permute-start(bf16[20,24,256]{2,1,0:T(8,128)(2,1)S(1)} %constant_dynamic-slice_fusion.11), channel_id=1, source_target_pairs={{0,24},{8,16},{16,8},{24,0},{1,25},{9,17},{17,9},{25,1},{2,26},{10... | collective-permute-start | bytes 737288 | tf_op jit(solution)/shard_map/ppermute | solution.py:489
  12.2 3.2 %collective-permute-start = (bf16[20,24,256]{2,1,0:T(8,128)(2,1)S(1)}, bf16[20,24,256]{2,1,0:T(8,128)(2,1)S(1)}, u32[]{:S(2)}, u32[]{:S(2)}) collective-permute-start(bf16[20,24,256]{2,1,0:T(8,128)(2,1)S(1)} %constant_dynamic-slice_fusion.10), channel_id=1, source_target_pairs={{0,8},{8,0},{16,24},{24,16},{1,9},{9,1},{17,25},{25,17},{2,10},{10... | collective-permute-start | bytes 737288 | tf_op jit(solution)/shard_map/ppermute | solution.py:489
  14.4 21.0 %copy-start.1 = (bf16[20,192,256]{2,1,0:T(8,128)(2,1)S(1)}, bf16[20,192,256]{2,1,0:T(8,128)(2,1)}, u32[]{:S(2)}) copy-start(bf16[20,192,256]{2,1,0:T(8,128)(2,1)} %param.6) | copy-start | bytes 5898244
  15.5 13.3 %collective-permute-start.5 = (bf16[20,24,256]{2,1,0:T(8,128)(2,1)S(1)}, bf16[20,24,256]{2,1,0:T(8,128)(2,1)S(1)}, u32[]{:S(2)}, u32[]{:S(2)}) collective-permute-start(bf16[20,24,256]{2,1,0:T(8,128)(2,1)S(1)} %constant_dynamic-slice_fusion.15), channel_id=1, source_target_pairs={{0,16},{8,24},{16,0},{24,8},{1,17},{9,25},{17,1},{25,9},{2,18},{10... | collective-permute-start | bytes 737288 | tf_op jit(solution)/shard_map/ppermute | solution.py:489
  26.2 21.9 %collective-permute-start.3 = (bf16[20,24,256]{2,1,0:T(8,128)(2,1)S(1)}, bf16[20,24,256]{2,1,0:T(8,128)(2,1)S(1)}, u32[]{:S(2)}, u32[]{:S(2)}) collective-permute-start(bf16[20,24,256]{2,1,0:T(8,128)(2,1)S(1)} %constant_dynamic-slice_fusion.7), channel_id=1, source_target_pairs={{0,8},{8,0},{16,24},{24,16},{1,9},{9,1},{17,25},{25,17},{2,10},{10... | collective-permute-start | bytes 737288 | tf_op jit(solution)/shard_map/ppermute | solution.py:489
  26.8 21.3 %collective-permute-start.8 = (bf16[20,24,256]{2,1,0:T(8,128)(2,1)S(1)}, bf16[20,24,256]{2,1,0:T(8,128)(2,1)S(1)}, u32[]{:S(2)}, u32[]{:S(2)}) collective-permute-start(bf16[20,24,256]{2,1,0:T(8,128)(2,1)S(1)} %constant_dynamic-slice_fusion.8), channel_id=1, source_target_pairs={{0,24},{8,16},{16,8},{24,0},{1,25},{9,17},{17,9},{25,1},{2,26},{10... | collective-permute-start | bytes 737288 | tf_op jit(solution)/shard_map/ppermute | solution.py:489
  30.8 15.1 %collective-permute-start.11 = (bf16[768,128]{1,0:T(8,128)(2,1)S(1)}, bf16[768,128]{1,0:T(8,128)(2,1)S(1)}, u32[]{:S(2)}, u32[]{:S(2)}) collective-permute-start(bf16[768,128]{1,0:T(8,128)(2,1)S(1)} %get-tuple-element.45), channel_id=1, source_target_pairs={{0,7},{8,0},{16,8},{24,16},{25,24},{17,25},{9,17},{1,9},{2,1},{10,... | collective-permute-start | bytes 589832 | tf_op jit(solution)/shard_map/ppermute | solution.py:521
  35.4 10.5 %collective-permute-start.9 = (bf16[768,128]{1,0:T(8,128)(2,1)S(1)}, bf16[768,128]{1,0:T(8,128)(2,1)S(1)}, u32[]{:S(2)}, u32[]{:S(2)}) collective-permute-start(bf16[768,128]{1,0:T(8,128)(2,1)S(1)} %get-tuple-element.45), channel_id=1, source_target_pairs={{0,8},{8,16},{16,24},{24,25},{25,17},{17,9},{9,1},{1,2},{2,10},{10... | collective-permute-start | bytes 589832 | tf_op jit(solution)/shard_map/ppermute | solution.py:520
  35.4 10.5 %collective-permute-start.10 = (bf16[768,128]{1,0:T(8,128)(2,1)S(1)}, bf16[768,128]{1,0:T(8,128)(2,1)S(1)}, u32[]{:S(2)}, u32[]{:S(2)}) collective-permute-start(bf16[768,128]{1,0:T(8,128)(2,1)S(1)} %get-tuple-element.46), channel_id=1, source_target_pairs={{0,8},{8,16},{16,24},{24,25},{25,17},{17,9},{9,1},{1,2},{2,10},{10... | collective-permute-start | bytes 589832 | tf_op jit(solution)/shard_map/ppermute | solution.py:520
  45.9 20.4 %collective-permute-start.18 = (bf16[768,128]{1,0:T(8,128)(2,1)S(1)}, bf16[768,128]{1,0:T(8,128)(2,1)S(1)}, u32[]{:S(2)}, u32[]{:S(2)}) collective-permute-start(bf16[768,128]{1,0:T(8,128)(2,1)S(1)} %get-tuple-element.46), channel_id=1, source_target_pairs={{0,7},{8,0},{16,8},{24,16},{25,24},{17,25},{9,17},{1,9},{2,1},{10,... | collective-permute-start | bytes 589832 | tf_op jit(solution)/shard_map/ppermute | solution.py:521
  45.9 29.1 %collective-permute-start.17 = (bf16[20,24,256]{2,1,0:T(8,128)(2,1)S(1)}, bf16[20,24,256]{2,1,0:T(8,128)(2,1)S(1)}, u32[]{:S(2)}, u32[]{:S(2)}) collective-permute-start(bf16[20,24,256]{2,1,0:T(8,128)(2,1)S(1)} %constant_dynamic-slice_fusion.2), channel_id=1, source_target_pairs={{0,24},{8,16},{16,8},{24,0},{1,25},{9,17},{17,9},{25,1},{2,26},{10... | collective-permute-start | bytes 737288 | tf_op jit(solution)/shard_map/ppermute | solution.py:489
  45.9 29.1 %collective-permute-start.16 = (bf16[20,24,256]{2,1,0:T(8,128)(2,1)S(1)}, bf16[20,24,256]{2,1,0:T(8,128)(2,1)S(1)}, u32[]{:S(2)}, u32[]{:S(2)}) collective-permute-start(bf16[20,24,256]{2,1,0:T(8,128)(2,1)S(1)} %constant_dynamic-slice_fusion.3), channel_id=1, source_target_pairs={{0,16},{8,24},{16,0},{24,8},{1,17},{9,25},{17,1},{25,9},{2,18},{10... | collective-permute-start | bytes 737288 | tf_op jit(solution)/shard_map/ppermute | solution.py:489
  48.0 27.0 %collective-permute-start.15 = (bf16[20,24,256]{2,1,0:T(8,128)(2,1)S(1)}, bf16[20,24,256]{2,1,0:T(8,128)(2,1)S(1)}, u32[]{:S(2)}, u32[]{:S(2)}) collective-permute-start(bf16[20,24,256]{2,1,0:T(8,128)(2,1)S(1)} %constant_dynamic-slice_fusion.1), channel_id=1, source_target_pairs={{0,8},{8,0},{16,24},{24,16},{1,9},{9,1},{17,25},{25,17},{2,10},{10... | collective-permute-start | bytes 737288 | tf_op jit(solution)/shard_map/ppermute | solution.py:489
  48.0 16.6 %collective-permute-start.7 = (bf16[20,24,256]{2,1,0:T(8,128)(2,1)S(1)}, bf16[20,24,256]{2,1,0:T(8,128)(2,1)S(1)}, u32[]{:S(2)}, u32[]{:S(2)}) collective-permute-start(bf16[20,24,256]{2,1,0:T(8,128)(2,1)S(1)} %constant_dynamic-slice_fusion.5), channel_id=1, source_target_pairs={{0,16},{8,24},{16,0},{24,8},{1,17},{9,25},{17,1},{25,9},{2,18},{10... | collective-permute-start | bytes 737288 | tf_op jit(solution)/shard_map/ppermute | solution.py:489
  66.1 12.5 %collective-permute-start.12 = (bf16[20,24,256]{2,1,0:T(8,128)(2,1)S(1)}, bf16[20,24,256]{2,1,0:T(8,128)(2,1)S(1)}, u32[]{:S(2)}, u32[]{:S(2)}) collective-permute-start(bf16[20,24,256]{2,1,0:T(8,128)(2,1)S(1)} %get-tuple-element.48), channel_id=1, source_target_pairs={{0,8},{8,0},{16,24},{24,16},{1,9},{9,1},{17,25},{25,17},{2,10},{10... | collective-permute-start | bytes 737288 | tf_op jit(solution)/shard_map/ppermute | solution.py:533
  74.6 8.9 %collective-permute-start.13 = (bf16[20,24,256]{2,1,0:T(8,128)(2,1)S(1)}, bf16[20,24,256]{2,1,0:T(8,128)(2,1)S(1)}, u32[]{:S(2)}, u32[]{:S(2)}) collective-permute-start(bf16[20,24,256]{2,1,0:T(8,128)(2,1)S(1)} %get-tuple-element.49), channel_id=1, source_target_pairs={{0,16},{8,24},{16,0},{24,8},{1,17},{9,25},{17,1},{25,9},{2,18},{10... | collective-permute-start | bytes 737288 | tf_op jit(solution)/shard_map/ppermute | solution.py:533
  76.5 16.6 %collective-permute-start.19 = (bf16[20,24,256]{2,1,0:T(8,128)(2,1)S(1)}, bf16[20,24,256]{2,1,0:T(8,128)(2,1)S(1)}, u32[]{:S(2)}, u32[]{:S(2)}) collective-permute-start(bf16[20,24,256]{2,1,0:T(8,128)(2,1)S(1)} %get-tuple-element.56), channel_id=1, source_target_pairs={{0,8},{8,0},{16,24},{24,16},{1,9},{9,1},{17,25},{25,17},{2,10},{10... | collective-permute-start | bytes 737288 | tf_op jit(solution)/shard_map/ppermute | solution.py:533
  76.8 16.4 %collective-permute-start.20 = (bf16[20,24,256]{2,1,0:T(8,128)(2,1)S(1)}, bf16[20,24,256]{2,1,0:T(8,128)(2,1)S(1)}, u32[]{:S(2)}, u32[]{:S(2)}) collective-permute-start(bf16[20,24,256]{2,1,0:T(8,128)(2,1)S(1)} %get-tuple-element.57), channel_id=1, source_target_pairs={{0,16},{8,24},{16,0},{24,8},{1,17},{9,25},{17,1},{25,9},{2,18},{10... | collective-permute-start | bytes 737288 | tf_op jit(solution)/shard_map/ppermute | solution.py:533
  78.4 14.6 %collective-permute-start.14 = (bf16[20,24,256]{2,1,0:T(8,128)(2,1)S(1)}, bf16[20,24,256]{2,1,0:T(8,128)(2,1)S(1)}, u32[]{:S(2)}, u32[]{:S(2)}) collective-permute-start(bf16[20,24,256]{2,1,0:T(8,128)(2,1)S(1)} %get-tuple-element.50), channel_id=1, source_target_pairs={{0,24},{8,16},{16,8},{24,0},{1,25},{9,17},{17,9},{25,1},{2,26},{10... | collective-permute-start | bytes 737288 | tf_op jit(solution)/shard_map/ppermute | solution.py:533
  78.7 19.6 %collective-permute-start.21 = (bf16[20,24,256]{2,1,0:T(8,128)(2,1)S(1)}, bf16[20,24,256]{2,1,0:T(8,128)(2,1)S(1)}, u32[]{:S(2)}, u32[]{:S(2)}) collective-permute-start(bf16[20,24,256]{2,1,0:T(8,128)(2,1)S(1)} %get-tuple-element.58), channel_id=1, source_target_pairs={{0,24},{8,16},{16,8},{24,0},{1,25},{9,17},{17,9},{25,1},{2,26},{10... | collective-permute-start | bytes 737288 | tf_op jit(solution)/shard_map/ppermute | solution.py:533
  93.2 5.1 %copy-start.2 = (bf16[20,192,256]{2,1,0:T(8,128)(2,1)}, bf16[20,192,256]{2,1,0:T(8,128)(2,1)S(1)}, u32[]{:S(2)}) copy-start(bf16[20,192,256]{2,1,0:T(8,128)(2,1)S(1)} %constant_dynamic-update-slice_fusion.1) | copy-start | bytes 5898244
